TPU v7x, 32 devices: a whole 2x2x4 slice. The times are simulated.
32 devices in a mesh: dp: 2 (over x), row: 4 (over y, core), col: 4 (over z).
Axes of the slice: x: 2, y: 2, z: 4, core: 2. Of those that a mesh axis runs over, the one named last changes fastest.
Arguments:
- block_input: bfloat16 [2048, 1024], P(('dp', 'col'), 'row'), may hold values from -6 to 6
- query_weight: bfloat16 [1024, 2048], P('row', 'col'), may hold values from -0.1875 to 0.1875
- key_weight: bfloat16 [1024, 1024], P('row', 'col'), may hold values from -0.1875 to 0.1875
- value_weight: bfloat16 [1024, 1024], P('row', 'col'), may hold values from -0.1875 to 0.1875
- projection_weight: bfloat16 [2048, 1024], P('col', 'row'), may hold values from -1 to 1
- w_gate: bfloat16 [1024, 3072], P('row', 'col'), may hold values from -0.1875 to 0.1875
- w_up: bfloat16 [1024, 3072], P('row', 'col'), may hold values from -0.1875 to 0.1875
- w_down: bfloat16 [3072, 1024], P('col', 'row'), may hold values from -0.15625 to 0.15625
- attn_gain: float32 [1024], P('row'), may hold values from 0.1 to 1.9
- ffn_gain: float32 [1024], P('row'), may hold values from 0.1 to 1.9
- query_gain: float32 [128], replicated, may hold values from 0.7 to 1.6, as said below
- key_gain: float32 [128], replicated, may hold values from 0.7 to 1.6, as said below
- cotangent: float32 [2048, 1024], P(('dp', 'col'), 'row'), may hold values from -6 to 6
Outputs:
- block_output: float32 [2048, 1024], P(('dp', 'col'), 'row')
- input_grad: float32 [2048, 1024], P(('dp', 'col'), 'row')
- grad_query: float32 [1024, 2048], P('row', 'col')
- grad_key: float32 [1024, 1024], P('row', 'col')
- grad_value: float32 [1024, 1024], P('row', 'col')
- grad_proj: float32 [2048, 1024], P('col', 'row')
- grad_gate: float32 [1024, 3072], P('row', 'col')
- grad_up: float32 [1024, 3072], P('row', 'col')
- grad_down: float32 [3072, 1024], P('col', 'row')
- attn_dgain: float32 [1024], P('row')
- ffn_dgain: float32 [1024], P('row')
- query_dgain: float32 [128], replicated
- key_dgain: float32 [128], replicated
Inputs may be any that keep to these rules, and one draw needn't show every extreme that they name: `query_gain`: 128 positive entries. `key_gain`: 128 positive entries.
All inputs are finite; a program needn't handle non-finite values.
Results may differ from a plain program's by a relative error of at most 0.018.
Values may be sent and summed in bfloat16 or wider, within the bound.
No kernel may reach another device: no remote copies, remote signals or barrier semaphores. Data moves between devices by JAX's collectives and lax.ppermute only.
A program may use at most 128 MiB of HBM per device.

v0:
```python
import jax
import jax.numpy as jnp
from jax import lax
from jax.sharding import PartitionSpec as P

MODEL_WIDTH = 1024
QUERY_HEADS = 16
KEY_VALUE_HEADS = 8
HEAD_DIMENSION = 128
SEQUENCE_LENGTH = 256


epsilon = 1e-06
rope_base = 1000000.0
masked_value = -1e30


def matrix_product(left, right):
    return jnp.dot(left, right, preferred_element_type=jnp.float32)


def rope_tables(length, head_size):
    places = jnp.arange(length).astype(jnp.float32)
    freqs = rope_base ** (-(jnp.arange(head_size // 2).astype(jnp.float32) * 2.0) / head_size)
    angles = places[:, None] * freqs[None, :]
    angles = jnp.concatenate([angles, angles], 1)
    return (jnp.cos(angles), jnp.sin(angles))


def rotate(values, cos_tab, sin_tab):
    half_dim = values.shape[-1] // 2
    turned = jnp.concatenate([-values[..., half_dim:], values[..., :half_dim]], -1)
    return values * cos_tab + turned * sin_tab


def rotate_back(grads, cos_tab, sin_tab):
    half_dim = grads.shape[-1] // 2
    by_sin = grads * sin_tab
    turned = jnp.concatenate([by_sin[..., half_dim:], -by_sin[..., :half_dim]], -1)
    return grads * cos_tab + turned


def head_norm(values):
    scales = lax.rsqrt(jnp.mean(values * values, -1, keepdims=True) + epsilon)
    return (values * scales, scales)


def head_norm_back(grads, normed, scales, gain):
    reduce_axes = tuple(range(grads.ndim - 1))
    dgain = jnp.sum(grads * normed, axis=reduce_axes)
    scaled = grads * gain
    return (scales * (scaled - normed * jnp.mean(scaled * normed, -1, keepdims=True)), dgain)


def causal_keep(length):
    row_ids = lax.broadcasted_iota(jnp.int32, (length, length), 0)
    col_ids = lax.broadcasted_iota(jnp.int32, (length, length), 1)
    return row_ids >= col_ids


def masked_scores(query_rot, key_rot):
    factor = query_rot.shape[-1] ** (-0.5)
    scores = (
        jnp.einsum("qgrd,kgd->grqk", query_rot, key_rot, preferred_element_type=jnp.float32)
        * factor
    )
    return jnp.where(causal_keep(query_rot.shape[0]), scores, masked_value)


def attend(query_rot, key_rot, values):
    scores = masked_scores(query_rot, key_rot)
    row_max = jnp.max(scores, -1, keepdims=True)
    exp_scores = jnp.exp(scores - row_max)
    totals = jnp.sum(exp_scores, -1, keepdims=True)
    probs_b = (exp_scores / totals).astype(jnp.bfloat16)
    log_sum = row_max + jnp.log(totals)
    outputs = jnp.einsum("grqk,kgd->qgrd", probs_b, values, preferred_element_type=jnp.float32)
    return (outputs.astype(jnp.bfloat16), log_sum[..., 0])


def attend_back(query_rot, key_rot, values, outputs, grad_out, log_sum):
    factor = query_rot.shape[-1] ** (-0.5)
    scores = masked_scores(query_rot, key_rot)
    probs = jnp.exp(scores - log_sum[..., None])
    probs_b = probs.astype(jnp.bfloat16)
    value_rows_gradient = jnp.einsum(
        "grqk,qgrd->kgd", probs_b, grad_out, preferred_element_type=jnp.float32
    )
    d_probs = jnp.einsum("qgrd,kgd->grqk", grad_out, values, preferred_element_type=jnp.float32)
    delta_rows = jnp.transpose(
        jnp.sum(grad_out.astype(jnp.float32) * outputs.astype(jnp.float32), -1), (1, 2, 0)
    )
    ds_b = (probs * (d_probs - delta_rows[..., None])).astype(jnp.bfloat16)
    d_query = (
        jnp.einsum("grqk,kgd->qgrd", ds_b, key_rot, preferred_element_type=jnp.float32) * factor
    )
    d_key = (
        jnp.einsum("grqk,qgrd->kgd", ds_b, query_rot, preferred_element_type=jnp.float32) * factor
    )
    return (d_query, d_key, value_rows_gradient)


def width_total(values):
    return lax.psum(values, "row")


def width_inner(values):
    return lax.psum(values, "row")


def from_col(values):
    return lax.all_gather(values, "col", axis=0, tiled=True)


def onto_col(values):
    return lax.psum_scatter(values, "col", scatter_dimension=0, tiled=True)


def back_from_col(values):
    return lax.all_gather(values, "col", axis=0, tiled=True)


def back_onto_col(values):
    return lax.psum_scatter(values, "col", scatter_dimension=0, tiled=True)


def to_sequence(values):
    return lax.all_to_all(values, "row", split_axis=0, concat_axis=1, tiled=True)


def to_tokens(values):
    return lax.all_to_all(values, "row", split_axis=1, concat_axis=0, tiled=True)


def per_device(
    block_input,
    query_weight,
    key_weight,
    value_weight,
    projection_weight,
    w_gate,
    w_up,
    w_down,
    attn_gain,
    ffn_gain,
    query_gain,
    key_gain,
    cotangent,
):
    width_row = block_input.shape[1]
    width_q = query_weight.shape[1]
    width_kv = key_weight.shape[1]
    width_ff = w_gate.shape[1]
    heads_kv = width_kv // HEAD_DIMENSION
    query_groups = QUERY_HEADS // KEY_VALUE_HEADS
    w_qkv = jnp.concatenate([query_weight, key_weight, value_weight], 1)
    w_gu = jnp.concatenate([w_gate, w_up], 1)
    cos_tab, sin_tab = rope_tables(SEQUENCE_LENGTH, HEAD_DIMENSION)
    q_cos, q_sin = (cos_tab[:, None, None, :], sin_tab[:, None, None, :])
    k_cos, k_sin = (cos_tab[:, None, :], sin_tab[:, None, :])
    inputs = block_input.astype(jnp.float32)
    r_one = lax.rsqrt(width_total(jnp.sum(inputs * inputs, -1)) / MODEL_WIDTH + epsilon)[:, None]
    n_one = inputs * r_one
    a_all = from_col((n_one * attn_gain).astype(jnp.bfloat16))
    qkv_full, gu_full, proj_full, down_full = (
        lax.all_gather(w_qkv, "row", axis=0, tiled=True),
        lax.all_gather(w_gu, "row", axis=0, tiled=True),
        lax.all_gather(projection_weight, "row", axis=1, tiled=True),
        lax.all_gather(w_down, "row", axis=1, tiled=True),
    )
    a_seq = to_sequence(a_all)
    qkv = matrix_product(a_seq, qkv_full)
    tok_local = qkv.shape[0]
    sequence_count = tok_local // SEQUENCE_LENGTH
    query_unrotated = qkv[:, :width_q].reshape(
        sequence_count, SEQUENCE_LENGTH, heads_kv, query_groups, HEAD_DIMENSION
    )
    key_unrotated = qkv[:, width_q : width_q + width_kv].reshape(
        sequence_count, SEQUENCE_LENGTH, heads_kv, HEAD_DIMENSION
    )
    value_input = (
        qkv[:, width_q + width_kv :]
        .astype(jnp.bfloat16)
        .reshape(sequence_count, SEQUENCE_LENGTH, heads_kv, HEAD_DIMENSION)
    )
    q_norm, q_scale = head_norm(query_unrotated)
    k_norm, k_scale = head_norm(key_unrotated)
    q_rot = rotate(q_norm * query_gain, q_cos, q_sin).astype(jnp.bfloat16)
    k_rot = rotate(k_norm * key_gain, k_cos, k_sin).astype(jnp.bfloat16)
    attn_out, log_sum = lax.map(
        lambda triple: attend(triple[0], triple[1], triple[2]), (q_rot, k_rot, value_input)
    )
    o_seq = attn_out.reshape(tok_local, width_q)
    hidden_one = inputs + onto_col(to_tokens(matrix_product(o_seq, proj_full)))
    r_two = lax.rsqrt(width_total(jnp.sum(hidden_one * hidden_one, -1)) / MODEL_WIDTH + epsilon)[
        :, None
    ]
    n_two = hidden_one * r_two
    b_all = from_col((n_two * ffn_gain).astype(jnp.bfloat16))
    b_seq = to_sequence(b_all)
    gate_up = matrix_product(b_seq, gu_full)
    gate_val = gate_up[:, :width_ff]
    up_val = gate_up[:, width_ff:]
    sigmoid_gate = jax.nn.sigmoid(gate_val)
    act_val = gate_val * sigmoid_gate
    m_seq = (act_val * up_val).astype(jnp.bfloat16)
    block_output = hidden_one + onto_col(to_tokens(matrix_product(m_seq, down_full)))
    dy_all = back_from_col(cotangent.astype(jnp.bfloat16))
    dy_seq = to_sequence(dy_all)
    g_down = matrix_product(m_seq.T, dy_seq)
    d_act = matrix_product(dy_seq, down_full.T)
    d_gate = d_act * up_val * sigmoid_gate * (1.0 + gate_val * (1.0 - sigmoid_gate))
    d_up = d_act * act_val
    d_gu = jnp.concatenate([d_gate.astype(jnp.bfloat16), d_up.astype(jnp.bfloat16)], 1)
    g_gu = matrix_product(b_seq.T, d_gu)
    g_gu, g_down = (
        lax.psum_scatter(g_gu.astype(jnp.bfloat16), "row", scatter_dimension=0, tiled=True).astype(
            jnp.float32
        ),
        lax.psum_scatter(
            g_down.astype(jnp.bfloat16), "row", scatter_dimension=1, tiled=True
        ).astype(jnp.float32),
    )
    d_bin = back_onto_col(to_tokens(matrix_product(d_gu, gu_full.T)))
    g_gate = g_gu[:, :width_ff]
    g_up = g_gu[:, width_ff:]
    ffn_part = jnp.sum(d_bin * n_two, 0)
    s_two = d_bin * ffn_gain
    inner_two = width_inner(jnp.sum(s_two * n_two, -1)) / MODEL_WIDTH
    d_hidden = cotangent + r_two * (s_two - n_two * inner_two[:, None])
    dh_all = back_from_col(d_hidden.astype(jnp.bfloat16))
    dh_seq = to_sequence(dh_all)
    g_proj = matrix_product(o_seq.T, dh_seq)
    d_out_flat = matrix_product(dh_seq, proj_full.T).astype(jnp.bfloat16)
    output_gradient = d_out_flat.reshape(
        sequence_count, SEQUENCE_LENGTH, heads_kv, query_groups, HEAD_DIMENSION
    )
    d_qrot, d_krot, value_rows_gradient = lax.map(
        lambda items: attend_back(items[0], items[1], items[2], items[3], items[4], items[5]),
        (q_rot, k_rot, value_input, attn_out, output_gradient, log_sum),
    )
    d_qn, qg_part = head_norm_back(rotate_back(d_qrot, q_cos, q_sin), q_norm, q_scale, query_gain)
    normed_key_gradient, kg_part = head_norm_back(
        rotate_back(d_krot, k_cos, k_sin), k_norm, k_scale, key_gain
    )
    d_qkv = jnp.concatenate(
        [
            d_qn.reshape(tok_local, width_q).astype(jnp.bfloat16),
            normed_key_gradient.reshape(tok_local, width_kv).astype(jnp.bfloat16),
            value_rows_gradient.reshape(tok_local, width_kv).astype(jnp.bfloat16),
        ],
        1,
    )
    g_qkv = matrix_product(a_seq.T, d_qkv)
    g_qkv, g_proj = (
        lax.psum_scatter(g_qkv.astype(jnp.bfloat16), "row", scatter_dimension=0, tiled=True).astype(
            jnp.float32
        ),
        lax.psum_scatter(
            g_proj.astype(jnp.bfloat16), "row", scatter_dimension=1, tiled=True
        ).astype(jnp.float32),
    )
    d_ain = back_onto_col(to_tokens(matrix_product(d_qkv, qkv_full.T)))
    g_query = g_qkv[:, :width_q]
    g_key = g_qkv[:, width_q : width_q + width_kv]
    g_value = g_qkv[:, width_q + width_kv :]
    attn_part = jnp.sum(d_ain * n_one, 0)
    s_one = d_ain * attn_gain
    inner_one = width_inner(jnp.sum(s_one * n_one, -1)) / MODEL_WIDTH
    input_grad = d_hidden + r_one * (s_one - n_one * inner_one[:, None])
    g_query, g_key, g_value, g_proj, g_gate, g_up, g_down = (
        lax.psum(g_query.astype(jnp.bfloat16), "dp").astype(jnp.float32),
        lax.psum(g_key.astype(jnp.bfloat16), "dp").astype(jnp.float32),
        lax.psum(g_value.astype(jnp.bfloat16), "dp").astype(jnp.float32),
        lax.psum(g_proj.astype(jnp.bfloat16), "dp").astype(jnp.float32),
        lax.psum(g_gate.astype(jnp.bfloat16), "dp").astype(jnp.float32),
        lax.psum(g_up.astype(jnp.bfloat16), "dp").astype(jnp.float32),
        lax.psum(g_down.astype(jnp.bfloat16), "dp").astype(jnp.float32),
    )
    row_start = lax.axis_index("row") * width_row
    attn_full = lax.dynamic_update_slice_in_dim(
        jnp.zeros((MODEL_WIDTH,), jnp.float32), attn_part, row_start, 0
    )
    ffn_full = lax.dynamic_update_slice_in_dim(
        jnp.zeros((MODEL_WIDTH,), jnp.float32), ffn_part, row_start, 0
    )
    attn_total, ffn_total, query_dgain, key_dgain = lax.psum(
        (attn_full, ffn_full, qg_part, kg_part), ("dp", "row", "col")
    )
    attn_dgain = lax.dynamic_slice_in_dim(attn_total, row_start, width_row, 0)
    ffn_dgain = lax.dynamic_slice_in_dim(ffn_total, row_start, width_row, 0)
    return (
        block_output,
        input_grad,
        g_query,
        g_key,
        g_value,
        g_proj,
        g_gate,
        g_up,
        g_down,
        attn_dgain,
        ffn_dgain,
        query_dgain,
        key_dgain,
    )


def solution(mesh):
    placed = (
        P(("dp", "col"), "row"),
        P("row", "col"),
        P("row", "col"),
        P("row", "col"),
        P("col", "row"),
        P("row", "col"),
        P("row", "col"),
        P("col", "row"),
        P("row"),
        P("row"),
        P(),
        P(),
        P(("dp", "col"), "row"),
    )
    return jax.shard_map(
        per_device,
        mesh=mesh,
        in_specs=placed,
        out_specs=(
            P(("dp", "col"), "row"),
            P(("dp", "col"), "row"),
            P("row", "col"),
            P("row", "col"),
            P("row", "col"),
            P("col", "row"),
            P("row", "col"),
            P("row", "col"),
            P("col", "row"),
            P("row"),
            P("row"),
            P(),
            P(),
        ),
        check_vma=False,
    )
```

profile of v0, /device:TPU:1, one launch (start us, length us, event | category | flops | bytes accessed | tf_op | source)
XLA Modules:
  0.0 505.7 jit_solution(6369405613071935193)
XLA Ops:
  11.0 6.4 %psum.105 = f32[256]{0:T(256)S(1)} all-reduce(f32[256]{0:T(256)S(1)} %fusion.24), channel_id=1, replica_groups=mesh['dp'=2,'row'=4,'col'=4] {'row'}, use_global_device_ids=true, to_apply=%region_1.0 | all-reduce | flops 256 | bytes 2048 | tf_op jit(solution)/shard_map/psum | solution.py:104
  18.4 14.2 %all_gather.24 = bf16[1024,256]{1,0:T(8,128)(2,1)} all-gather(bf16[256,256]{1,0:T(8,128)(2,1)S(1)} %fusion.18), channel_id=1, replica_groups=mesh['dp'=2,'row'=4,'col'=4] {'col'}, dimensions={0}, use_global_device_ids=true | all-gather | bytes 655360 | tf_op jit(solution)/shard_map/all_gather | solution.py:112
  32.6 7.0 %all-to-all-start = ((bf16[4,256,256]{2,1,0:T(8,128)(2,1)}), bf16[4,256,256]{2,1,0:T(8,128)(2,1)S(1)}, u32[]{:S(2)}, u32[]{:S(2)}) async-start(bf16[4,256,256]{2,1,0:T(8,128)(2,1)} %bitcast), calls=%async_computation | async-start | bytes 1048576 | tf_op jit(solution)/shard_map/all_to_all | solution.py:128
  41.6 11.9 %all-to-all-done = bf16[4,256,256]{2,1,0:T(8,128)(2,1)S(1)} async-done(((bf16[4,256,256]{2,1,0:T(8,128)(2,1)}), bf16[4,256,256]{2,1,0:T(8,128)(2,1)S(1)}, u32[]{:S(2)}, u32[]{:S(2)}) %all-to-all-start) | async-done | bytes 524320 | tf_op jit(solution)/shard_map/all_to_all | solution.py:128
  76.8 17.0 %all_to_all.149 = f32[256,4,256]{2,0,1:T(8,128)} all-to-all(f32[256,4,256]{2,0,1:T(8,128)S(1)} %fusion.46), channel_id=1, replica_groups=mesh['dp'=2,'row'=4,'col'=4] {'row'}, dimensions={1} | all-to-all | bytes 2097152 | tf_op jit(solution)/shard_map/all_to_all | solution.py:132
  95.5 19.6 %all_gather.30 = bf16[1024,256]{1,0:T(8,128)(2,1)} all-gather(bf16[256,256]{1,0:T(8,128)(2,1)S(1)} %convert_element_type.161), channel_id=1, replica_groups=mesh['dp'=2,'row'=4,'col'=4] {'col'}, dimensions={0}, use_global_device_ids=true | all-gather | bytes 655360 | tf_op jit(solution)/shard_map/all_gather | solution.py:120
  115.1 7.6 %all-to-all-start.4 = ((bf16[4,256,256]{2,1,0:T(8,128)(2,1)}), bf16[4,256,256]{2,1,0:T(8,128)(2,1)S(1)}, u32[]{:S(2)}, u32[]{:S(2)}) async-start(bf16[4,256,256]{2,1,0:T(8,128)(2,1)} %bitcast.24), calls=%async_computation.6 | async-start | bytes 1048576 | tf_op jit(solution)/shard_map/all_to_all | solution.py:128
  135.9 14.3 %all_gather.27 = bf16[1024,256]{1,0:T(8,128)(2,1)} all-gather(bf16[256,256]{1,0:T(8,128)(2,1)S(1)} %multiply_convert_fusion.5), channel_id=1, replica_groups=mesh['dp'=2,'row'=4,'col'=4] {'col'}, dimensions={0}, use_global_device_ids=true | all-gather | bytes 655360 | tf_op jit(solution)/shard_map/all_gather | solution.py:112
  150.1 7.3 %all-to-all-start.2 = ((bf16[4,256,256]{2,1,0:T(8,128)(2,1)}), bf16[4,256,256]{2,1,0:T(8,128)(2,1)}, u32[]{:S(2)}, u32[]{:S(2)}) async-start(bf16[4,256,256]{2,1,0:T(8,128)(2,1)} %bitcast.19), calls=%async_computation.3 | async-start | bytes 1048576 | tf_op jit(solution)/shard_map/all_to_all | solution.py:128
  158.5 7.1 %all-to-all-done.2 = bf16[4,256,256]{2,1,0:T(8,128)(2,1)} async-done(((bf16[4,256,256]{2,1,0:T(8,128)(2,1)}), bf16[4,256,256]{2,1,0:T(8,128)(2,1)}, u32[]{:S(2)}, u32[]{:S(2)}) %all-to-all-start.2) | async-done | bytes 524320 | tf_op jit(solution)/shard_map/all_to_all | solution.py:128
  171.0 8.1 %all-gather.11.cloned.1.call-done = bf16[768,1024]{1,0:T(8,128)(2,1)} async-done(((bf16[768,256]{1,0:T(8,128)(2,1)}), bf16[768,1024]{1,0:T(8,128)(2,1)}) %all-gather.11.cloned.1.call-update) | async-done | bytes 1572880 | tf_op jit(solution)/shard_map/all_gather | solution.py:169
  184.1 16.8 %all_to_all.150 = f32[256,4,256]{2,0,1:T(8,128)} all-to-all(f32[256,4,256]{2,0,1:T(8,128)S(1)} %bitcast.156), channel_id=1, replica_groups=mesh['dp'=2,'row'=4,'col'=4] {'row'}, dimensions={1} | all-to-all | bytes 2097152 | tf_op jit(solution)/shard_map/all_to_all | solution.py:132
  203.2 17.9 %all_to_all.151 = f32[256,4,256]{2,0,1:T(8,128)} all-to-all(f32[256,4,256]{2,0,1:T(8,128)S(1)} %bitcast.157), channel_id=1, replica_groups=mesh['dp'=2,'row'=4,'col'=4] {'row'}, dimensions={1} | all-to-all | bytes 2097152 | tf_op jit(solution)/shard_map/all_to_all | solution.py:132
  235.9 20.6 %reduce-scatter.11.cloned.1.call-done = f32[256,256]{1,0:T(8,128)} async-done(((f32[1024,256]{1,0:T(8,128)}), f32[256,256]{1,0:T(8,128)}) %reduce-scatter.11.cloned.1.call-update) | async-done | bytes 262160 | tf_op jit(solution)/shard_map/reduce_scatter | solution.py:116
  258.4 12.8 %all_gather.31 = bf16[1024,256]{1,0:T(8,128)(2,1)} all-gather(bf16[256,256]{1,0:T(8,128)(2,1)S(1)} %get-tuple-element.82), channel_id=1, replica_groups=mesh['dp'=2,'row'=4,'col'=4] {'col'}, dimensions={0}, use_global_device_ids=true | all-gather | bytes 655360 | tf_op jit(solution)/shard_map/all_gather | solution.py:120
  271.2 8.0 %all-to-all-start.6 = ((bf16[4,256,256]{2,1,0:T(8,128)(2,1)}), bf16[4,256,256]{2,1,0:T(8,128)(2,1)S(1)}, u32[]{:S(2)}, u32[]{:S(2)}) async-start(bf16[4,256,256]{2,1,0:T(8,128)(2,1)} %bitcast.32), calls=%async_computation.9 | async-start | bytes 1048576 | tf_op jit(solution)/shard_map/all_to_all | solution.py:128
  280.0 13.3 %all-to-all-done.6 = bf16[4,256,256]{2,1,0:T(8,128)(2,1)S(1)} async-done(((bf16[4,256,256]{2,1,0:T(8,128)(2,1)}), bf16[4,256,256]{2,1,0:T(8,128)(2,1)S(1)}, u32[]{:S(2)}, u32[]{:S(2)}) %all-to-all-start.6) | async-done | bytes 524320 | tf_op jit(solution)/shard_map/all_to_all | solution.py:128
  311.9 23.2 %all_to_all.152 = f32[256,4,256]{2,0,1:T(8,128)} all-to-all(f32[256,4,256]{2,0,1:T(8,128)S(1)} %bitcast.158), channel_id=1, replica_groups=mesh['dp'=2,'row'=4,'col'=4] {'row'}, dimensions={1} | all-to-all | bytes 2097152 | tf_op jit(solution)/shard_map/all_to_all | solution.py:132
  345.4 25.0 %reduce-scatter.23.cloned.1.call-done = bf16[768,256]{1,0:T(8,128)(2,1)} async-done(((bf16[768,1024]{1,0:T(8,128)(2,1)}), bf16[768,256]{1,0:T(8,128)(2,1)}) %reduce-scatter.23.cloned.1.call-update) | async-done | bytes 393232 | tf_op jit(solution)/shard_map/reduce_scatter | solution.py:220
  370.3 27.5 %reduce-scatter.19.cloned.1.call-done = bf16[512,256]{1,0:T(8,128)(2,1)} async-done(((bf16[512,1024]{1,0:T(8,128)(2,1)}), bf16[512,256]{1,0:T(8,128)(2,1)}) %reduce-scatter.19.cloned.1.call-update) | async-done | bytes 262160 | tf_op jit(solution)/shard_map/reduce_scatter | solution.py:259
  398.1 29.0 %reduce-scatter.15.cloned.1.call-done = f32[256,256]{1,0:T(8,128)} async-done(((f32[1024,256]{1,0:T(8,128)}), f32[256,256]{1,0:T(8,128)}) %reduce-scatter.15.cloned.1.call-update) | async-done | bytes 262160 | tf_op jit(solution)/shard_map/reduce_scatter | solution.py:124
  428.5 38.9 %all-reduce = (f32[1024]{0:T(1024)S(1)}, f32[1024]{0:T(1024)S(1)}, f32[128]{0:T(128)}, f32[128]{0:T(128)}) all-reduce(f32[1024]{0:T(1024)S(1)} %dynamic_update_slice.20, f32[1024]{0:T(1024)S(1)} %dynamic_update_slice.21, f32[128]{0:T(128)S(1)} %copy-done.44, ...), channel_id=1, replica_groups=mesh['dp'=2,'row'=4,'col'=4] {'dp','row','col'}, use_global_device_ids=true, to_apply=%region_31.32 | all-reduce | flops 2304 | bytes 18432 | tf_op jit(solution)/shard_map/psum | solution.py:287
  468.7 7.1 %psum.108 = f32[256]{0:T(256)S(1)} all-reduce(f32[256]{0:T(256)S(1)} %get-tuple-element.66), channel_id=1, replica_groups=mesh['dp'=2,'row'=4,'col'=4] {'row'}, use_global_device_ids=true, to_apply=%region_18.19 | all-reduce | flops 256 | bytes 2048 | tf_op jit(solution)/shard_map/psum | solution.py:108
  477.6 13.5 %all-reduce.4.cloned.1.call-done = (bf16[256,512]{1,0:T(8,128)(2,1)}, bf16[256,256]{1,0:T(8,128)(2,1)}, bf16[256,256]{1,0:T(8,128)(2,1)}, bf16[512,256]{1,0:T(8,...) async-done(((bf16[256,512]{1,0:T(8,128)(2,1)}, bf16[256,256]{1,0:T(8,128)(2,1)}, bf16[256,256]{1,0:T(8,128)(2,1)}, ...) | async-done | bytes 1966096 | tf_op jit(solution)/shard_map/psum | solution.py:272
  (224 shorter events, 116.9 us)
Async XLA Ops:
  7.2 46.5 %all-gather.7.cloned.1.call-start = ((), (), s32[]{:S(2)}) async-start(), calls=%async_computation.17 | async-start | bytes 1310720 | tf_op jit(solution)/shard_map/all_gather | solution.py:168
  7.9 51.4 %all-gather.5.cloned.1.call-start = ((), (), s32[]{:S(2)}) async-start(), calls=%async_computation.16 | async-start | bytes 2621440 | tf_op jit(solution)/shard_map/all_gather | solution.py:166
  17.4 36.1 %copy-start.34 = (f32[256]{0:T(256)}, f32[256]{0:T(256)S(1)}, u32[]{:S(2)}) copy-start(f32[256]{0:T(256)S(1)} %add_rsqrt_fusion.3) | copy-start | bytes 3076
  32.6 20.9 %all-to-all-start = ((bf16[4,256,256]{2,1,0:T(8,128)(2,1)}), bf16[4,256,256]{2,1,0:T(8,128)(2,1)S(1)}, u32[]{:S(2)}, u32[]{:S(2)}) async-start(bf16[4,256,256]{2,1,0:T(8,128)(2,1)} %bitcast), calls=%async_computation | async-start | bytes 1048576 | tf_op jit(solution)/shard_map/all_to_all | solution.py:128
  39.6 87.3 %reduce-scatter.9.cloned.1.call-start = ((), (), s32[]{:S(2)}) async-start(), calls=%async_computation.18 | async-start | bytes 1310720 | tf_op jit(solution)/shard_map/reduce_scatter | solution.py:116
  93.8 73.0 %all-gather.9.cloned.1.call-start = ((), (), s32[]{:S(2)}) async-start(), calls=%async_computation.19 | async-start | bytes 3932160 | tf_op jit(solution)/shard_map/all_gather | solution.py:167
  94.8 84.3 %all-gather.11.cloned.1.call-start = ((), (), s32[]{:S(2)}) async-start(), calls=%async_computation.20 | async-start | bytes 1966080 | tf_op jit(solution)/shard_map/all_gather | solution.py:169
  115.1 35.0 %all-to-all-start.4 = ((bf16[4,256,256]{2,1,0:T(8,128)(2,1)}), bf16[4,256,256]{2,1,0:T(8,128)(2,1)S(1)}, u32[]{:S(2)}, u32[]{:S(2)}) async-start(bf16[4,256,256]{2,1,0:T(8,128)(2,1)} %bitcast.24), calls=%async_computation.6 | async-start | bytes 1048576 | tf_op jit(solution)/shard_map/all_to_all | solution.py:128
  150.1 15.4 %all-to-all-start.2 = ((bf16[4,256,256]{2,1,0:T(8,128)(2,1)}), bf16[4,256,256]{2,1,0:T(8,128)(2,1)}, u32[]{:S(2)}, u32[]{:S(2)}) async-start(bf16[4,256,256]{2,1,0:T(8,128)(2,1)} %bitcast.19), calls=%async_computation.3 | async-start | bytes 1048576 | tf_op jit(solution)/shard_map/all_to_all | solution.py:128
  157.5 70.9 %reduce-scatter.13.cloned.1.call-start = ((), (), s32[]{:S(2)}) async-start(), calls=%async_computation.22 | async-start | bytes 1310720 | tf_op jit(solution)/shard_map/reduce_scatter | solution.py:124
  200.9 55.6 %reduce-scatter.11.cloned.1.call-start = ((), (), s32[]{:S(2)}) async-start(), calls=%async_computation.21 | async-start | bytes 1310720 | tf_op jit(solution)/shard_map/reduce_scatter | solution.py:116
  221.1 114.2 %reduce-scatter.21.cloned.1.call-start = ((), (), s32[]{:S(2)}) async-start(), calls=%async_computation.26 | async-start | bytes 3932160 | tf_op jit(solution)/shard_map/reduce_scatter | solution.py:217
  271.2 22.0 %all-to-all-start.6 = ((bf16[4,256,256]{2,1,0:T(8,128)(2,1)}), bf16[4,256,256]{2,1,0:T(8,128)(2,1)S(1)}, u32[]{:S(2)}, u32[]{:S(2)}) async-start(bf16[4,256,256]{2,1,0:T(8,128)(2,1)} %bitcast.32), calls=%async_computation.9 | async-start | bytes 1048576 | tf_op jit(solution)/shard_map/all_to_all | solution.py:128
  279.3 62.8 %reduce-scatter.17.cloned.1.call-start = ((), (), s32[]{:S(2)}) async-start(), calls=%async_computation.24 | async-start | bytes 2621440 | tf_op jit(solution)/shard_map/reduce_scatter | solution.py:256
  305.8 64.5 %reduce-scatter.23.cloned.1.call-start = ((), (), s32[]{:S(2)}) async-start(), calls=%async_computation.27 | async-start | bytes 1966080 | tf_op jit(solution)/shard_map/reduce_scatter | solution.py:220
  307.8 90.0 %reduce-scatter.19.cloned.1.call-start = ((), (), s32[]{:S(2)}) async-start(), calls=%async_computation.25 | async-start | bytes 1310720 | tf_op jit(solution)/shard_map/reduce_scatter | solution.py:259
  309.3 117.8 %reduce-scatter.15.cloned.1.call-start = ((), (), s32[]{:S(2)}) async-start(), calls=%async_computation.23 | async-start | bytes 1310720 | tf_op jit(solution)/shard_map/reduce_scatter | solution.py:124
  335.2 62.6 %copy-start.42 = (f32[256]{0:T(256)S(1)}, f32[256]{0:T(256)}, u32[]{:S(2)}) copy-start(f32[256]{0:T(256)} %get-tuple-element.53) | copy-start | bytes 3076
  335.2 91.9 %copy-start.35 = (f32[256]{0:T(256)S(1)}, f32[256]{0:T(256)}, u32[]{:S(2)}) copy-start(f32[256]{0:T(256)} %copy-done.34) | copy-start | bytes 3076
  335.2 91.9 %copy-start.37 = (f32[256]{0:T(256)S(1)}, f32[256]{0:T(256)}, u32[]{:S(2)}) copy-start(f32[256]{0:T(256)} %param.21) | copy-start | bytes 3076
  335.2 155.9 %all-reduce.4.cloned.1.call-start = ((), (), s32[]{:S(2)}) async-start(), calls=%async_computation.28 | async-start | bytes 3932160 | tf_op jit(solution)/shard_map/psum | solution.py:272
  337.4 91.1 %copy-start.43 = (f32[128]{0:T(128)S(1)}, f32[128]{0:T(128)}, u32[]{:S(2)}) copy-start(f32[128]{0:T(128)} %get-tuple-element.67) | copy-start | bytes 1540
  337.4 91.1 %copy-start.44 = (f32[128]{0:T(128)S(1)}, f32[128]{0:T(128)}, u32[]{:S(2)}) copy-start(f32[128]{0:T(128)} %get-tuple-element.51) | copy-start | bytes 1540
  337.4 138.5 %copy-start.18 = (f32[256,256]{1,0:T(8,128)S(1)}, f32[256,256]{1,0:T(8,128)}, u32[]{:S(2)}) copy-start(f32[256,256]{1,0:T(8,128)} %get-tuple-element.83) | copy-start | bytes 786436
  (38 other events, 189.6 us)
Sparse Core Ops, SparseCore 0:
  9.6 19.3 all-gather.6
  31.1 28.1 all-gather.4
  93.9 32.9 reduce-scatter.8
  129.0 28.7 all-gather.8
  159.3 19.8 all-gather.10
  201.0 27.3 reduce-scatter.12
  230.7 25.7 reduce-scatter.10
  259.2 42.4 reduce-scatter.20
  305.9 36.0 reduce-scatter.16
  344.6 25.7 reduce-scatter.22
  372.9 24.8 reduce-scatter.18
  400.0 26.9 reduce-scatter.14
  430.9 60.1 all-reduce.3
where the time goes:
time: 508 us; the launch traced here: 506 us
  blocking collectives  201 us (40%)
  waiting for transfers between devices  174 us (34%)
  matrix products  31.6 us (6%)
  other arithmetic  30.8 us (6%)
  starting transfers between devices  30.6 us (6%)
  local copies, waits for them, and re-layouts  23.9 us (5%)
  between operations  14.7 us (3%)
    all_to_all x4, blocking collectives, to_tokens(): lax.all_to_all(values, 'row', split_axis=1, concat_axis=0, tiled=True)  74.9 us
    psum x1, blocking collectives, per_device(): lax.psum((attn_full, ffn_full, qg_part, kg_part), ('dp', 'row', 'col'))  38.9 us
    all_gather x2, blocking collectives, back_from_col(): return lax.all_gather(values, 'col', axis=0, tiled=True)  32.5 us
    reduce_scatter x2, waiting for transfers between devices, back_onto_col(): return lax.psum_scatter(values, 'col', scatter_dimension=0, tiled=True)  32.3 us
    all_to_all x4, waiting for transfers between devices, to_sequence(): lax.all_to_all(values, 'row', split_axis=0, concat_axis=1, tiled=True)  32.2 us
    all_to_all x4, starting transfers between devices, to_sequence(): lax.all_to_all(values, 'row', split_axis=0, concat_axis=1, tiled=True)  30 us
    all_gather x2, blocking collectives, from_col(): return lax.all_gather(values, 'col', axis=0, tiled=True)  28.5 us
    dot_general x12, matrix products, matrix_product(): return jnp.dot(left, right, preferred_element_type=jnp.float32)  27.9 us
  transfers between devices with their start and end apart: 17, of which 13 were waited for; matrix products, arithmetic and copies ran while one was open for 11% of the time, Pallas kernels for 0%

commit v1 on v0

v1 whole, which is shorter than its diff:
```python
import functools

import jax
import jax.numpy as jnp
import numpy as np
from jax import lax
from jax.experimental import pallas as pl
from jax.experimental.pallas import tpu as pltpu
from jax.sharding import PartitionSpec as P

MODEL_WIDTH = 1024
HEAD_DIMENSION = 128
SEQUENCE_LENGTH = 256
GROUPS = 2

epsilon = 1e-06
rope_base = 1000000.0
masked_value = -1e30

F32 = jnp.float32
BF16 = jnp.bfloat16
BLK = 256
ROWS = 4
SWAP = (0, 2, 1, 3)


def rope_tables():
    places = np.arange(SEQUENCE_LENGTH, dtype=np.float32)
    half = HEAD_DIMENSION // 2
    freqs = np.float32(rope_base) ** (
        -(np.arange(half, dtype=np.float32) * np.float32(2.0)) / np.float32(HEAD_DIMENSION)
    )
    angles = places[:, None] * freqs[None, :].astype(np.float32)
    cos, sin = np.cos(angles), np.sin(angles)
    return (
        np.concatenate([cos, cos], 1).astype(np.float32),
        np.concatenate([-sin, sin], 1).astype(np.float32),
    )


def dot(left, right):
    return jnp.dot(left, right, preferred_element_type=F32)


def dot_nt(left, right):
    return lax.dot_general(left, right, (((1,), (1,)), ((), ())), preferred_element_type=F32)


def dot_tn(left, right):
    return lax.dot_general(left, right, (((0,), (0,)), ((), ())), preferred_element_type=F32)


def call(body, outs, args, scratch=(), flops=0, smem=None):
    vm = pl.BlockSpec(memory_space=pltpu.VMEM)
    in_specs = [vm] * len(args)
    if smem is not None:
        in_specs = [pl.BlockSpec(memory_space=pltpu.SMEM)] + in_specs
        args = (smem,) + tuple(args)
    moved = sum(int(np.prod(a.shape)) * a.dtype.itemsize for a in list(args) + list(outs))
    return pl.pallas_call(
        body,
        out_shape=[jax.ShapeDtypeStruct(o.shape, o.dtype) for o in outs],
        in_specs=in_specs,
        out_specs=[vm] * len(outs),
        scratch_shapes=list(scratch),
        compiler_params=pltpu.CompilerParams(vmem_limit_bytes=40 << 20),
        cost_estimate=pl.CostEstimate(flops=flops, bytes_accessed=moved, transcendentals=0),
    )(*args)


def sds(shape, dtype):
    return jax.ShapeDtypeStruct(shape, dtype)


def split3(values):
    high = values.astype(BF16).astype(F32)
    rest = values - high
    mid = rest.astype(BF16).astype(F32)
    return high, mid, rest - mid


def pack_qkv(wq, wk, wv, ga, gf, out):
    nq, nk = wq.shape[1], wk.shape[1]
    out[0:BLK, 0:nq] = wq[...]
    out[0:BLK, nq : nq + nk] = wk[...]
    out[0:BLK, nq + nk :] = wv[...]
    rows = split3(ga[...]) + split3(gf[...])
    ids = lax.broadcasted_iota(jnp.int32, (16, BLK), 0)
    extra = jnp.zeros((16, BLK), F32)
    for n, row in enumerate(rows):
        extra = jnp.where(ids == n, jnp.broadcast_to(row, (16, BLK)), extra)
    out[BLK : BLK + 16, :] = jnp.zeros((16, out.shape[1]), BF16)
    out[BLK : BLK + 16, 0:BLK] = extra.astype(BF16)


def pack_ffn(wg, wu, wd, out):
    nf = wg.shape[1]
    out[:, 0:nf] = wg[...]
    out[:, nf : 2 * nf] = wu[...]
    for i in range(nf // BLK):
        out[:, 2 * nf + i * BLK : 2 * nf + (i + 1) * BLK] = wd[i * BLK : (i + 1) * BLK, :]


def rope(values, cos, sin):
    return values * cos + pltpu.roll(values, HEAD_DIMENSION // 2, 1) * sin


def rope_back(values, cos, sin):
    return values * cos + pltpu.roll(values * sin, HEAD_DIMENSION // 2, 1)


def head(ref, n):
    return ref[:, n * HEAD_DIMENSION : (n + 1) * HEAD_DIMENSION]


def attn_forward(
    ids, x0, x1, x2, x3, q0, q1, q2, q3, cos_r, sin_r, qg_r, kg_r,
    x_out, a_out, gains, o_out, qn_out, kn_out, sc_out, qr_out, kr_out, v_out, pr_out, qkv,
):
    s1 = ids[2]
    qs = (q0, q1, q2, q3)
    for k, ref in enumerate((x0, x1, x2, x3)):
        x_out[s1 ^ SWAP[k]] = ref[...]
    total = jnp.zeros((BLK, 1), F32)
    for p in range(ROWS):
        x = x_out[p].astype(F32)
        total = total + jnp.sum(x * x, -1, keepdims=True)
        extra = qs[p][BLK : BLK + 16, 0:BLK].astype(F32)
        gains[p : p + 1, :] = extra[0:1] + extra[1:2] + extra[2:3]
        gains[ROWS + p : ROWS + p + 1, :] = extra[3:4] + extra[4:5] + extra[5:6]
    r_one = lax.rsqrt(total / MODEL_WIDTH + epsilon)
    for p in range(ROWS):
        a_out[p] = ((x_out[p].astype(F32) * r_one) * gains[p : p + 1, :]).astype(BF16)
    for p in range(ROWS):
        part = dot(a_out[p], qs[p][0:BLK, :])
        if p == 0:
            qkv[...] = part
        else:
            qkv[...] += part
    cos, sin = cos_r[...], sin_r[...]
    nkv = kn_out.shape[1] // HEAD_DIMENSION
    nq = qn_out.shape[1] // HEAD_DIMENSION
    lanes = lax.broadcasted_iota(jnp.int32, (BLK, HEAD_DIMENSION), 1)
    packed = jnp.zeros((BLK, HEAD_DIMENSION), F32)
    for n in range(nq + nkv):
        raw = head(qkv, n)
        scale = lax.rsqrt(jnp.mean(raw * raw, -1, keepdims=True) + epsilon)
        packed = jnp.where(lanes == n, scale, packed)
        normed = raw * scale
        cols = slice(n * HEAD_DIMENSION, (n + 1) * HEAD_DIMENSION)
        if n < nq:
            qn_out[:, cols] = normed
            qr_out[:, cols] = rope(normed * qg_r[...], cos, sin).astype(BF16)
        else:
            cols = slice((n - nq) * HEAD_DIMENSION, (n - nq + 1) * HEAD_DIMENSION)
            kn_out[:, cols] = normed
            kr_out[:, cols] = rope(normed * kg_r[...], cos, sin).astype(BF16)
    sc_out[...] = packed
    for n in range(nkv):
        v_out[:, n * HEAD_DIMENSION : (n + 1) * HEAD_DIMENSION] = head(qkv, nq + nkv + n).astype(BF16)
    keep = lax.broadcasted_iota(jnp.int32, (BLK, BLK), 0) >= lax.broadcasted_iota(
        jnp.int32, (BLK, BLK), 1
    )
    factor = HEAD_DIMENSION ** (-0.5)
    for n in range(nq):
        g = n // GROUPS
        scores = jnp.where(keep, dot_nt(head(qr_out, n), head(kr_out, g)) * factor, masked_value)
        top = jnp.max(scores, -1, keepdims=True)
        weights = jnp.exp(scores - top)
        probs = weights / jnp.sum(weights, -1, keepdims=True)
        pr_out[n] = probs
        o_out[:, n * HEAD_DIMENSION : (n + 1) * HEAD_DIMENSION] = dot(
            probs.astype(BF16), head(v_out, g)
        ).astype(BF16)


def project(ids, o, w0, w1, w2, w3, s0, s1, s2, s3, place):
    for p, w in enumerate((w0, w1, w2, w3)):
        place[p] = dot(o[...], w[...]).astype(BF16)
    for k, slot in enumerate((s0, s1, s2, s3)):
        slot[...] = place[ids[1] ^ k]


def ffn(
    ids, t0, t1, t2, t3, x, y0, y1, y2, y3, f0, f1, f2, f3, gains,
    s0, s1, s2, s3, b_out, dy_out, m_out, d_out, h_out, gu, da, place,
):
    c, swapped = ids[1], ids[2]
    fs = (f0, f1, f2, f3)
    nf = m_out.shape[1]
    for k, ref in enumerate((t0, t1, t2, t3)):
        h_out[c ^ k] = ref[...].astype(F32)
    for k, ref in enumerate((y0, y1, y2, y3)):
        dy_out[swapped ^ SWAP[k]] = ref[...]
    total = jnp.zeros((BLK, 1), F32)
    for p in range(ROWS):
        h = h_out[p] + x[p].astype(F32)
        h_out[p] = h
        total = total + jnp.sum(h * h, -1, keepdims=True)
    r_two = lax.rsqrt(total / MODEL_WIDTH + epsilon)
    for p in range(ROWS):
        b_out[p] = ((h_out[p] * r_two) * gains[ROWS + p : ROWS + p + 1, :]).astype(BF16)
    for p in range(ROWS):
        part = dot(b_out[p], fs[p][:, 0 : 2 * nf])
        if p == 0:
            gu[...] = part
        else:
            gu[...] += part
    for i in range(nf // BLK):
        at = slice(2 * nf + i * BLK, 2 * nf + (i + 1) * BLK)
        cols = slice(i * BLK, (i + 1) * BLK)
        acc = dot_nt(dy_out[0], fs[0][:, at])
        for p in range(1, ROWS):
            acc = acc + dot_nt(dy_out[p], fs[p][:, at])
        da[:, cols] = acc
    for i in range(nf // BLK):
        cols = slice(i * BLK, (i + 1) * BLK)
        ups = slice(nf + i * BLK, nf + (i + 1) * BLK)
        gate, up, d_act = gu[:, cols], gu[:, ups], da[:, cols]
        sig = 1.0 / (1.0 + jnp.exp(-gate))
        act = gate * sig
        m_out[:, cols] = (act * up).astype(BF16)
        d_out[:, cols] = (d_act * up * sig * (1.0 + gate * (1.0 - sig))).astype(BF16)
        d_out[:, ups] = (d_act * act).astype(BF16)
    for p in range(ROWS):
        place[p] = dot_nt(d_out[...], fs[p][:, 0 : 2 * nf]).astype(BF16)
    for k, slot in enumerate((s0, s1, s2, s3)):
        slot[...] = place[c ^ k]


def down(ids, m, f0, f1, f2, f3, h, s0, s1, s2, s3, h_own, place):
    nf = m.shape[1]
    for p, f in enumerate((f0, f1, f2, f3)):
        acc = jnp.zeros((BLK, BLK), F32)
        for i in range(nf // BLK):
            at = slice(2 * nf + i * BLK, 2 * nf + (i + 1) * BLK)
            acc = acc + dot(m[:, i * BLK : (i + 1) * BLK], f[:, at])
        place[p] = acc.astype(BF16)
    for k, slot in enumerate((s0, s1, s2, s3)):
        slot[...] = place[ids[1] ^ k]
    h_own[...] = h[ids[1]]


def ffn_grads(b, d, m, dy, send, keep):
    nf = m.shape[1]
    for p in range(ROWS):
        out = keep if p < 2 else send
        rows = slice((p % 2) * BLK, (p % 2 + 1) * BLK)
        out[rows, 0 : 2 * nf] = dot_tn(b[p], d[...]).astype(BF16)
        for i in range(nf // BLK):
            at = slice(2 * nf + i * BLK, 2 * nf + (i + 1) * BLK)
            out[rows, at] = dot_tn(m[:, i * BLK : (i + 1) * BLK], dy[p]).astype(BF16)


def attn_grads(a, d, o, dh, send, keep):
    nd = d.shape[1]
    for p in range(ROWS):
        out = keep if p < 2 else send
        rows = slice((p % 2) * BLK, (p % 2 + 1) * BLK)
        out[rows, 0:nd] = dot_tn(a[p], d[...]).astype(BF16)
        for i in range(o.shape[1] // BLK):
            at = slice(nd + i * BLK, nd + (i + 1) * BLK)
            out[rows, at] = dot_tn(o[:, i * BLK : (i + 1) * BLK], dh[p]).astype(BF16)


def attn_backward(
    ids, t0, t1, t2, t3, h, dy, gains, w0, w1, w2, w3, x, q0, q1, q2, q3,
    o, qn, kn, sc, qr, kr, v, pr, cos_r, sin_r, qg_r, kg_r,
    s0, s1, s2, s3, dhb, d_qkv, dh_own, sums, dh, part,
):
    r, c = ids[0], ids[1]
    for k, ref in enumerate((t0, t1, t2, t3)):
        dh[c ^ k] = ref[...].astype(F32)
    total = jnp.zeros((BLK, 1), F32)
    for p in range(ROWS):
        total = total + jnp.sum(h[p] * h[p], -1, keepdims=True)
    r_two = lax.rsqrt(total / MODEL_WIDTH + epsilon)
    sums[...] = jnp.zeros(sums.shape, F32)
    first = (c == 0).astype(F32)
    inner = jnp.zeros((BLK, 1), F32)
    for p in range(ROWS):
        n_two = h[p] * r_two
        term = dh[p] * n_two
        sums[pl.ds(ROWS + (r ^ SWAP[p]), 1), :] = jnp.sum(term, 0, keepdims=True) * first
        inner = inner + jnp.sum(term * gains[ROWS + p : ROWS + p + 1, :], -1, keepdims=True)
    inner = inner / MODEL_WIDTH
    for p in range(ROWS):
        n_two = h[p] * r_two
        s_two = dh[p] * gains[ROWS + p : ROWS + p + 1, :]
        out = dy[p].astype(F32) + r_two * (s_two - n_two * inner)
        dh[p] = out
        dhb[p] = out.astype(BF16)
    dh_own[...] = dh[c]
    nq, nkv = qn.shape[1] // HEAD_DIMENSION, kn.shape[1] // HEAD_DIMENSION
    d_o = dot_nt(dhb[0], w0[...])
    for p, w in ((1, w1), (2, w2), (3, w3)):
        d_o = d_o + dot_nt(dhb[p], w[...])
    d_o = d_o.astype(BF16)
    cos, sin = cos_r[...], sin_r[...]
    factor = HEAD_DIMENSION ** (-0.5)
    q_sum = jnp.zeros((1, HEAD_DIMENSION), F32)
    k_sum = jnp.zeros((1, HEAD_DIMENSION), F32)

    def norm_back(grad, normed, scale, gain):
        gained = grad * gain
        return scale * (gained - normed * jnp.mean(gained * normed, -1, keepdims=True))

    for g in range(nkv):
        d_k = jnp.zeros((BLK, HEAD_DIMENSION), F32)
        d_v = jnp.zeros((BLK, HEAD_DIMENSION), F32)
        for n in range(g * GROUPS, (g + 1) * GROUPS):
            grad = d_o[:, n * HEAD_DIMENSION : (n + 1) * HEAD_DIMENSION]
            delta = jnp.sum(grad.astype(F32) * head(o, n).astype(F32), -1, keepdims=True)
            probs = pr[n]
            d_v = d_v + dot_tn(probs.astype(BF16), grad)
            d_s = (probs * (dot_nt(grad, head(v, g)) - delta)).astype(BF16)
            d_q = dot(d_s, head(kr, g)) * factor
            d_k = d_k + dot_tn(d_s, head(qr, n))
            e_q = rope_back(d_q, cos, sin)
            normed = head(qn, n)
            q_sum = q_sum + jnp.sum(e_q * normed, 0, keepdims=True)
            d_qkv[:, n * HEAD_DIMENSION : (n + 1) * HEAD_DIMENSION] = norm_back(
                e_q, normed, sc[:, n : n + 1], qg_r[...]
            ).astype(BF16)
        e_k = rope_back(d_k * factor, cos, sin)
        normed = head(kn, g)
        k_sum = k_sum + jnp.sum(e_k * normed, 0, keepdims=True)
        at = (nq + g) * HEAD_DIMENSION
        d_qkv[:, at : at + HEAD_DIMENSION] = norm_back(
            e_k, normed, sc[:, nq + g : nq + g + 1], kg_r[...]
        ).astype(BF16)
        at = (nq + nkv + g) * HEAD_DIMENSION
        d_qkv[:, at : at + HEAD_DIMENSION] = d_v.astype(BF16)
    sums[8:9, 0:HEAD_DIMENSION] = q_sum
    sums[8:9, HEAD_DIMENSION : 2 * HEAD_DIMENSION] = k_sum
    total = jnp.zeros((BLK, 1), F32)
    for p in range(ROWS):
        xf = x[p].astype(F32)
        total = total + jnp.sum(xf * xf, -1, keepdims=True)
    r_one = lax.rsqrt(total / MODEL_WIDTH + epsilon)
    inner = jnp.zeros((BLK, 1), F32)
    for p, q in enumerate((q0, q1, q2, q3)):
        d_a = dot_nt(d_qkv[...], q[0:BLK, :])
        term = d_a * (x[p].astype(F32) * r_one)
        sums[pl.ds(r ^ SWAP[p], 1), :] = jnp.sum(term, 0, keepdims=True)
        inner = inner + jnp.sum(term * gains[p : p + 1, :], -1, keepdims=True)
        part[p] = d_a.astype(BF16)
    row = jnp.transpose(jnp.broadcast_to(inner, (BLK, 128)))[0:16, :]
    high = row.astype(BF16).astype(F32)
    ids16 = lax.broadcasted_iota(jnp.int32, (16, BLK), 0)
    tail = jnp.where(ids16 == 0, high, jnp.where(ids16 == 1, row - high, 0.0)).astype(BF16)
    for k, slot in enumerate((s0, s1, s2, s3)):
        slot[0:BLK, :] = part[c ^ k]
        slot[BLK : BLK + 16, :] = tail


def finish(ids, t0, t1, t2, t3, dh_own, x, gains, out):
    c = ids[1]
    refs = (t0, t1, t2, t3)
    d_a = refs[0][0:BLK, :].astype(F32)
    tail = refs[0][BLK : BLK + 16, :].astype(F32)
    for ref in refs[1:]:
        d_a = d_a + ref[0:BLK, :].astype(F32)
        tail = tail + ref[BLK : BLK + 16, :].astype(F32)
    row = jnp.broadcast_to(tail[0:1] + tail[1:2], (128, BLK))
    inner = jnp.transpose(row)[:, 0:1] / MODEL_WIDTH
    total = jnp.zeros((BLK, 1), F32)
    for p in range(ROWS):
        xf = x[p].astype(F32)
        total = total + jnp.sum(xf * xf, -1, keepdims=True)
    r_one = lax.rsqrt(total / MODEL_WIDTH + epsilon)
    gain = gains[pl.ds(c, 1), :]
    n_one = x[c].astype(F32) * r_one
    out[...] = (dh_own[...] + r_one * (d_a * gain - n_one * inner)).astype(BF16)


def row_swap(values, bit):
    return lax.ppermute(values, "row", [(i, i ^ bit) for i in range(ROWS)])


def col_swap(values, bit):
    return lax.ppermute(values, "col", [(i, i ^ bit) for i in range(ROWS)])


def all_of_row(shard):
    other = row_swap(shard, 2)
    return (shard, other, row_swap(shard, 1), row_swap(other, 1))


def to_sequence(block):
    return [
        lax.ppermute(
            block, ("row", "col"),
            [(r * ROWS + c, c * ROWS + (r ^ k)) for r in range(ROWS) for c in range(ROWS)],
        )
        for k in range(ROWS)
    ]


def to_owner(block):
    return lax.ppermute(
        block, ("row", "col"),
        [(r * ROWS + c, (r ^ SWAP[c]) * ROWS + r) for r in range(ROWS) for c in range(ROWS)],
    )


def scatter_col(slots):
    return [slots[0]] + [col_swap(slots[k], k) for k in range(1, ROWS)]


def gather_col(block):
    return [block] + [col_swap(block, k) for k in range(1, ROWS)]


def add_all(parts):
    total = parts[0].astype(F32)
    for item in parts[1:]:
        total = total + item.astype(F32)
    return total


def per_device(
    n_dp, block_input, query_weight, key_weight, value_weight, projection_weight,
    w_gate, w_up, w_down, attn_gain, ffn_gain, query_gain, key_gain, cotangent,
):
    width_q, width_kv, width_ff = query_weight.shape[1], key_weight.shape[1], w_gate.shape[1]
    width_qkv = width_q + 2 * width_kv
    nq = width_q // HEAD_DIMENSION
    r, c = lax.axis_index("row"), lax.axis_index("col")
    rc = r ^ c
    ids = jnp.stack([r, c, ((rc & 1) << 1) | (rc >> 1)]).astype(jnp.int32)
    cos_np, sin_np = rope_tables()
    cos, sin = jnp.asarray(cos_np), jnp.asarray(sin_np)
    qg, kg = query_gain.reshape(1, -1), key_gain.reshape(1, -1)
    blocks = (ROWS, BLK, BLK)
    slot = sds((BLK, BLK), BF16)

    xs = to_sequence(block_input)
    (msg_q,) = call(
        pack_qkv, [sds((BLK + 16, width_qkv), BF16)],
        (query_weight, key_weight, value_weight, attn_gain.reshape(1, -1), ffn_gain.reshape(1, -1)),
    )
    q_all = all_of_row(msg_q)
    p_all = all_of_row(projection_weight)
    (msg_f,) = call(pack_ffn, [sds((BLK, 3 * width_ff), BF16)], (w_gate, w_up, w_down))
    f_all = all_of_row(msg_f)
    ys = to_sequence(cotangent.astype(BF16))

    x_full, a_full, gains, o, qn, kn, sc, qr, kr, v, pr = call(
        attn_forward,
        [
            sds(blocks, BF16), sds(blocks, BF16), sds((8, BLK), F32), sds((BLK, width_q), BF16),
            sds((BLK, width_q), F32), sds((BLK, width_kv), F32), sds((BLK, HEAD_DIMENSION), F32),
            sds((BLK, width_q), BF16), sds((BLK, width_kv), BF16), sds((BLK, width_kv), BF16),
            sds((nq, BLK, BLK), F32),
        ],
        (*xs, *q_all, cos, sin, qg, kg), [pltpu.VMEM((BLK, width_qkv), F32)],
        2 * BLK * MODEL_WIDTH * width_qkv, ids,
    )
    slots = call(
        project, [slot] * ROWS, (o, *p_all), [pltpu.VMEM(blocks, BF16)],
        2 * BLK * MODEL_WIDTH * width_q, ids,
    )
    h_sum = add_all(scatter_col(slots)).astype(BF16)
    h_parts = gather_col(h_sum)
    *slots, b_full, dy_full, m, d_gu, h_full = call(
        ffn,
        [slot] * ROWS
        + [
            sds(blocks, BF16), sds(blocks, BF16), sds((BLK, width_ff), BF16),
            sds((BLK, 2 * width_ff), BF16), sds(blocks, F32),
        ],
        (*h_parts, x_full, *ys, *f_all, gains),
        [
            pltpu.VMEM((BLK, 2 * width_ff), F32), pltpu.VMEM((BLK, width_ff), F32),
            pltpu.VMEM(blocks, BF16),
        ],
        10 * BLK * MODEL_WIDTH * width_ff, ids,
    )
    b_sum = add_all(scatter_col(slots)).astype(BF16)
    b_parts = gather_col(b_sum)

    f_send, f_keep = call(
        ffn_grads, [sds((2 * BLK, 3 * width_ff), BF16)] * 2, (b_full, d_gu, m, dy_full),
        (), 6 * BLK * MODEL_WIDTH * width_ff,
    )
    *slots, h_own = call(
        down, [slot] * ROWS + [sds((BLK, BLK), F32)], (m, *f_all, h_full),
        [pltpu.VMEM(blocks, BF16)], 2 * BLK * MODEL_WIDTH * width_ff, ids,
    )
    y_own = (h_own + add_all(scatter_col(slots))).astype(BF16)
    block_output = to_owner(y_own).astype(F32)

    *slots, dh_full, d_qkv, dh_own, sums = call(
        attn_backward,
        [sds((BLK + 16, BLK), BF16)] * ROWS
        + [
            sds(blocks, BF16), sds((BLK, width_qkv), BF16), sds((BLK, BLK), F32),
            sds((16, BLK), F32),
        ],
        (*b_parts, h_full, dy_full, gains, *p_all, x_full, *q_all,
         o, qn, kn, sc, qr, kr, v, pr, cos, sin, qg, kg),
        [pltpu.VMEM(blocks, F32), pltpu.VMEM(blocks, BF16)],
        2 * BLK * MODEL_WIDTH * (width_qkv + width_q) + 10 * BLK * BLK * width_q, ids,
    )
    a_parts = scatter_col(slots)
    a_send, a_keep = call(
        attn_grads, [sds((2 * BLK, width_qkv + width_q), BF16)] * 2, (a_full, d_qkv, o, dh_full),
        (), 2 * BLK * MODEL_WIDTH * (width_qkv + width_q),
    )
    (in_own,) = call(finish, [slot], (*a_parts, dh_own, x_full, gains), (), 0, ids)
    input_grad = to_owner(in_own).astype(F32)

    def reduce_grad(send, keep):
        got = row_swap(send, 1)
        mine = keep[0:BLK].astype(F32) + got[0:BLK].astype(F32)
        theirs = (keep[BLK:].astype(F32) + got[BLK:].astype(F32)).astype(BF16)
        total = (mine + row_swap(theirs, 2).astype(F32)).astype(BF16)
        if n_dp == 2:
            return total.astype(F32) + lax.ppermute(total, "dp", [(0, 1), (1, 0)]).astype(F32)
        return lax.psum(total, "dp").astype(F32)

    g_f = reduce_grad(f_send, f_keep)
    g_a = reduce_grad(a_send, a_keep)

    for bit in (1, 2):
        sums = sums + col_swap(sums, bit)
    for bit in (1, 2):
        sums = sums + row_swap(sums, bit)
    if n_dp == 2:
        sums = sums + lax.ppermute(sums, "dp", [(0, 1), (1, 0)])
    else:
        sums = lax.psum(sums, "dp")
    attn_dgain = lax.dynamic_slice_in_dim(sums, r, 1, 0)[0]
    ffn_dgain = lax.dynamic_slice_in_dim(sums, ROWS + r, 1, 0)[0]
    slabs = lambda values: jnp.concatenate(
        [values[:, i * BLK : (i + 1) * BLK] for i in range(values.shape[1] // BLK)], 0
    )
    return (
        block_output,
        input_grad,
        g_a[:, :width_q],
        g_a[:, width_q : width_q + width_kv],
        g_a[:, width_q + width_kv : width_qkv],
        slabs(g_a[:, width_qkv:]),
        g_f[:, :width_ff],
        g_f[:, width_ff : 2 * width_ff],
        slabs(g_f[:, 2 * width_ff :]),
        attn_dgain,
        ffn_dgain,
        sums[8, :HEAD_DIMENSION],
        sums[8, HEAD_DIMENSION:],
    )


def solution(mesh):
    tokens = P(("dp", "col"), "row")
    return jax.shard_map(
        functools.partial(per_device, mesh.shape["dp"]),
        mesh=mesh,
        in_specs=(
            tokens, P("row", "col"), P("row", "col"), P("row", "col"), P("col", "row"),
            P("row", "col"), P("row", "col"), P("col", "row"), P("row"), P("row"), P(), P(), tokens,
        ),
        out_specs=(
            tokens, tokens, P("row", "col"), P("row", "col"), P("row", "col"), P("col", "row"),
            P("row", "col"), P("row", "col"), P("col", "row"), P("row"), P("row"), P(), P(),
        ),
        check_vma=False,
    )
```

time: 508 us -> 285 us (0.56)
  blocking collectives: 201 us -> 0 us
  starting transfers between devices: 30.6 us -> 91.9 us
  waiting for transfers between devices: 174 us -> 139 us
  matrix products: 31.6 us -> 0 us
  Pallas kernels: 0 us -> 22.8 us
  other arithmetic: 30.8 us -> 13 us
  between operations: 14.7 us -> 1.04 us
  local copies, waits for them, and re-layouts: 23.9 us -> 15 us
    ppermute x0 -> x48, waiting for transfers between devices: none -> 139 us  [the longest x15 50.8 us: row_swap(): return lax.ppermute(values, 'row', [(i, i ^ bit) for i in range(ROWS)])]
    reduce_scatter x8 -> x0, waiting for transfers between devices: 114 us -> none  [the longest x2 32.3 us: back_onto_col(): return lax.psum_scatter(values, 'col', scatter_dimension=0, tiled=True)]
    ppermute x0 -> x48, starting transfers between devices: none -> 91.9 us  [the longest x20 35.1 us: col_swap(): return lax.ppermute(values, 'col', [(i, i ^ bit) for i in range(ROWS)])]
    all_to_all x4 -> x0, blocking collectives: 74.9 us -> none  [to_tokens(): lax.all_to_all(values, 'row', split_axis=1, concat_axis=0, tiled=True)]
    psum x5 -> x0, blocking collectives: 64.7 us -> none  [the longest x1 38.9 us: per_device(): lax.psum((attn_full, ffn_full, qg_part, kg_part), ('dp', 'row', 'col'))]
    all_gather x4 -> x0, blocking collectives: 60.9 us -> none  [the longest x2 32.5 us: back_from_col(): return lax.all_gather(values, 'col', axis=0, tiled=True)]
    all_to_all x4 -> x0, waiting for transfers between devices: 32.2 us -> none  [to_sequence(): lax.all_to_all(values, 'row', split_axis=0, concat_axis=1, tiled=True)]
    dot_general x18 -> x0, matrix products: 31.6 us -> none  [the longest x12 27.9 us: matrix_product(): return jnp.dot(left, right, preferred_element_type=jnp.float32)]
  transfers between devices with their start and end apart: 17 -> 48, of which waited for: 13 -> 21; matrix products, arithmetic and copies ran while one was open for 11% -> 5% of each run, Pallas kernels for 0% -> 6%
where the time goes in v1:
time: 285 us; the launch traced here: 282 us
  waiting for transfers between devices  139 us (49%)
  starting transfers between devices  91.9 us (32%)
  Pallas kernels  22.8 us (8%)
  local copies, waits for them, and re-layouts  15 us (5%)
  other arithmetic  13 us (5%)
    ppermute x15, waiting for transfers between devices, row_swap(): return lax.ppermute(values, 'row', [(i, i ^ bit) for i in range(ROWS)])  50.8 us
    ppermute x20, waiting for transfers between devices, col_swap(): return lax.ppermute(values, 'col', [(i, i ^ bit) for i in range(ROWS)])  42.7 us
    ppermute x20, starting transfers between devices, col_swap(): return lax.ppermute(values, 'col', [(i, i ^ bit) for i in range(ROWS)])  35.1 us
    ppermute x2, waiting for transfers between devices, reduce_grad(): lax.ppermute(total, 'dp', [(0, 1), (1, 0)]).astype(F32)  33.5 us
    ppermute x15, starting transfers between devices, row_swap(): return lax.ppermute(values, 'row', [(i, i ^ bit) for i in range(ROWS)])  23.9 us
    ppermute x8, starting transfers between devices, to_sequence(): lax.ppermute(block, ('row', 'col'), [(r * ROWS + c, c * ROWS + (r ^ k)) f...  22.9 us
    pallas_call x10, Pallas kernels, call(): pl.pallas_call(body, out_shape=[jax.ShapeDtypeStruct(o.shape, o.dtype) fo...  22.8 us
    ppermute x8, waiting for transfers between devices, to_sequence(): lax.ppermute(block, ('row', 'col'), [(r * ROWS + c, c * ROWS + (r ^ k)) f...  11.5 us
  transfers between devices with their start and end apart: 48, of which 21 were waited for; matrix products, arithmetic and copies ran while one was open for 5% of the time, Pallas kernels for 6%

profile of v1, /device:TPU:1, one launch (start us, length us, event | category | flops | bytes accessed | tf_op | source)
XLA Modules:
  0.0 282.3 jit_solution(17559478686029355226)
XLA Ops:
  7.0 4.0 %collective-permute-start = (bf16[256,256]{1,0:T(8,128)(2,1)S(1)}, bf16[256,256]{1,0:T(8,128)(2,1)S(1)}, u32[]{:S(2)}, u32[]{:S(2)}) collective-permute-start(bf16[256,256]{1,0:T(8,128)(2,1)S(1)} %copy-done.33), channel_id=1, source_target_pairs={{0,0},{1,4},{2,8},{3,12},{4,1},{5,5},{6,9},{7,13},{8,2},{9,6},{10,... | collective-permute-start | bytes 393224 | tf_op jit(solution)/shard_map/ppermute | solution.py:392
  14.7 7.5 %collective-permute-start.2 = (bf16[256,256]{1,0:T(8,128)(2,1)S(1)}, bf16[256,256]{1,0:T(8,128)(2,1)S(1)}, u32[]{:S(2)}, u32[]{:S(2)}) collective-permute-start(bf16[256,256]{1,0:T(8,128)(2,1)S(1)} %copy-done.33), channel_id=1, source_target_pairs={{0,2},{1,6},{2,10},{3,14},{4,3},{5,7},{6,11},{7,15},{8,0},{9,4},{1... | collective-permute-start | bytes 393224 | tf_op jit(solution)/shard_map/ppermute | solution.py:392
  22.2 25.9 %collective-permute-done.4.q1 = bf16[272,1024]{1,0:T(8,128)(2,1)S(1)} collective-permute-done((bf16[272,1024]{1,0:T(8,128)(2,1)S(1)}, bf16[272,1024]{1,0:T(8,128)(2,1)S(1)}, u32[]{:S(2)}, u32[]{:S(2)}) %collective-permute-start.4) | collective-permute-done | bytes 557088 | tf_op jit(solution)/shard_map/ppermute | solution.py:378
  59.7 4.7 %collective-permute-done.7.w1 = bf16[512,256]{1,0:T(8,128)(2,1)} collective-permute-done((bf16[512,256]{1,0:T(8,128)(2,1)}, bf16[512,256]{1,0:T(8,128)(2,1)}, u32[]{:S(2)}, u32[]{:S(2)}) %collective-permute-start.7) | collective-permute-done | bytes 262176 | tf_op jit(solution)/shard_map/ppermute | solution.py:378
  69.0 3.7 %collective-permute-start.16 = (bf16[256,256]{1,0:T(8,128)(2,1)}, bf16[256,256]{1,0:T(8,128)(2,1)S(1)}, u32[]{:S(2)}, u32[]{:S(2)}) collective-permute-start(bf16[256,256]{1,0:T(8,128)(2,1)} %convert_element_type.113), channel_id=1, source_target_pairs={{0,0},{1,4},{2,8},{3,12},{4,1},{5,5},{6,9},{7,13},{8,2},{9,6},{10,... | collective-permute-start | bytes 393224 | tf_op jit(solution)/shard_map/ppermute | solution.py:392
  78.0 3.7 %shard_map.247 = (bf16[4,256,256]{2,1,0:T(8,128)(2,1)S(1)}, bf16[4,256,256]{2,1,0:T(8,128)(2,1)S(1)}, f32[8,256]{1,0:T(8,128)S(1)}, bf16[256,512]{1,0:T(8,128)(2...) custom-call(s32[3]{0:T(128)S(1)} %pad_add_fusion.ids, ...), custom_call_target="tpu_custom_call" | custom-call | flops 536870912 | bytes 6824972 | tf_op jit(solution)/shard_map/pallas_call | solution.py:60
  87.2 3.6 %collective-permute-done.12 = bf16[256,256]{1,0:T(8,128)(2,1)S(1)} collective-permute-done((bf16[256,256]{1,0:T(8,128)(2,1)S(1)}, bf16[256,256]{1,0:T(8,128)(2,1)S(1)}, u32[]{:S(2)}, u32[]{:S(2)}) %collective-permute-start.12) | collective-permute-done | bytes 131104 | tf_op jit(solution)/shard_map/ppermute | solution.py:382
  91.3 5.8 %collective-permute-done.11 = bf16[256,256]{1,0:T(8,128)(2,1)S(1)} collective-permute-done((bf16[256,256]{1,0:T(8,128)(2,1)S(1)}, bf16[256,256]{1,0:T(8,128)(2,1)S(1)}, u32[]{:S(2)}, u32[]{:S(2)}) %collective-permute-start.11) | collective-permute-done | bytes 131104 | tf_op jit(solution)/shard_map/ppermute | solution.py:382
  105.7 3.9 %collective-permute-done.19.y3 = bf16[256,256]{1,0:T(8,128)(2,1)S(1)} collective-permute-done((bf16[256,256]{1,0:T(8,128)(2,1)S(1)}, bf16[256,256]{1,0:T(8,128)(2,1)S(1)}, u32[]{:S(2)}, u32[]{:S(2)}) %collective-permute-start.19) | collective-permute-done | bytes 131104 | tf_op jit(solution)/shard_map/ppermute | solution.py:392
  109.6 8.2 %collective-permute-start.15 = (bf16[256,256]{1,0:T(8,128)(2,1)S(1)}, bf16[256,256]{1,0:T(8,128)(2,1)S(1)}, u32[]{:S(2)}, u32[]{:S(2)}) collective-permute-start(bf16[256,256]{1,0:T(8,128)(2,1)S(1)} %add_convert_fusion.6.t0), channel_id=1, source_target_pairs={{0,3},{1,2},{2,1},{3,0},{4,7},{5,6},{6,5},{7,4},{8,11},{9,10},{10,... | collective-permute-start | bytes 393224 | tf_op jit(solution)/shard_map/ppermute | solution.py:382
  120.2 4.6 %shard_map.250 = (bf16[256,256]{1,0:T(8,128)(2,1)S(1)}, bf16[256,256]{1,0:T(8,128)(2,1)S(1)}, bf16[256,256]{1,0:T(8,128)(2,1)S(1)}, bf16[256,256]{1,0:T(8,128)(2...) custom-call(s32[3]{0:T(128)S(1)} %pad_add_fusion.ids, ...), custom_call_target="tpu_custom_call" | custom-call | flops 2013265920 | bytes 10100748 | tf_op jit(solution)/shard_map/pallas_call | solution.py:60
  124.8 3.4 %collective-permute-start.29 = (bf16[256,256]{1,0:T(8,128)(2,1)S(1)}, bf16[256,256]{1,0:T(8,128)(2,1)S(1)}, u32[]{:S(2)}, u32[]{:S(2)}) collective-permute-start(bf16[256,256]{1,0:T(8,128)(2,1)S(1)} %get-tuple-element.71), channel_id=1, source_target_pairs={{0,3},{1,2},{2,1},{3,0},{4,7},{5,6},{6,5},{7,4},{8,11},{9,10},{10,... | collective-permute-start | bytes 393224 | tf_op jit(solution)/shard_map/ppermute | solution.py:382
  131.3 5.3 %collective-permute-done.28 = bf16[256,256]{1,0:T(8,128)(2,1)S(1)} collective-permute-done((bf16[256,256]{1,0:T(8,128)(2,1)S(1)}, bf16[256,256]{1,0:T(8,128)(2,1)S(1)}, u32[]{:S(2)}, u32[]{:S(2)}) %collective-permute-start.28) | collective-permute-done | bytes 131104 | tf_op jit(solution)/shard_map/ppermute | solution.py:382
  144.3 5.0 %collective-permute-done.31.t2 = bf16[256,256]{1,0:T(8,128)(2,1)S(1)} collective-permute-done((bf16[256,256]{1,0:T(8,128)(2,1)S(1)}, bf16[256,256]{1,0:T(8,128)(2,1)S(1)}, u32[]{:S(2)}, u32[]{:S(2)}) %collective-permute-start.31) | collective-permute-done | bytes 131104 | tf_op jit(solution)/shard_map/ppermute | solution.py:382
  149.4 6.5 %shard_map.252 = (bf16[272,256]{1,0:T(8,128)(2,1)S(1)}, bf16[272,256]{1,0:T(8,128)(2,1)}, bf16[272,256]{1,0:T(8,128)(2,1)}, bf16[272,256]{1,0:T(8,128)(2,1)}, bf...) custom-call(s32[3]{0:T(128)S(1)} %pad_add_fusion.ids, ...), custom_call_target="tpu_custom_call" | custom-call | flops 1140850688 | bytes 10806284 | tf_op jit(solution)/shard_map/pallas_call | solution.py:60
  166.1 3.5 %collective-permute-start.38 = (bf16[256,1536]{1,0:T(8,128)(2,1)}, bf16[256,1536]{1,0:T(8,128)(2,1)}, u32[]{:S(2)}, u32[]{:S(2)}) collective-permute-start(bf16[256,1536]{1,0:T(8,128)(2,1)} %add_convert_fusion.3), channel_id=1, source_target_pairs={{0,8},{4,12},{8,0},{12,4},{1,9},{5,13},{9,1},{13,5},{2,10},{6,14},... | collective-permute-start | bytes 2359304 | tf_op jit(solution)/shard_map/ppermute | solution.py:378
  172.3 4.6 %collective-permute-done.24 = bf16[256,256]{1,0:T(8,128)(2,1)S(1)} collective-permute-done((bf16[256,256]{1,0:T(8,128)(2,1)S(1)}, bf16[256,256]{1,0:T(8,128)(2,1)S(1)}, u32[]{:S(2)}, u32[]{:S(2)}) %collective-permute-start.24) | collective-permute-done | bytes 131104 | tf_op jit(solution)/shard_map/ppermute | solution.py:382
  181.9 4.1 %collective-permute-start.44 = (f32[16,256]{1,0:T(8,128)S(1)}, f32[16,256]{1,0:T(8,128)S(1)}, u32[]{:S(2)}, u32[]{:S(2)}) collective-permute-start(f32[16,256]{1,0:T(8,128)S(1)} %add.95), channel_id=1, source_target_pairs={{0,2},{1,3},{2,0},{3,1},{4,6},{5,7},{6,4},{7,5},{8,10},{9,11},{10,... | collective-permute-start | bytes 49160 | tf_op jit(solution)/shard_map/ppermute | solution.py:382
  188.3 5.8 %collective-permute-start.45 = (f32[16,256]{1,0:T(8,128)S(1)}, f32[16,256]{1,0:T(8,128)S(1)}, u32[]{:S(2)}, u32[]{:S(2)}) collective-permute-start(f32[16,256]{1,0:T(8,128)S(1)} %add.96), channel_id=1, source_target_pairs={{0,4},{4,0},{8,12},{12,8},{1,5},{5,1},{9,13},{13,9},{2,6},{6,2},{1... | collective-permute-start | bytes 49160 | tf_op jit(solution)/shard_map/ppermute | solution.py:378
  194.9 19.3 %collective-permute-done.46 = f32[16,256]{1,0:T(8,128)S(1)} collective-permute-done((f32[16,256]{1,0:T(8,128)S(1)}, f32[16,256]{1,0:T(8,128)S(1)}, u32[]{:S(2)}, u32[]{:S(2)}) %collective-permute-start.46) | collective-permute-done | bytes 16416 | tf_op jit(solution)/shard_map/ppermute | solution.py:378
  220.8 9.4 %collective-permute-done.34.t2 = bf16[272,256]{1,0:T(8,128)(2,1)S(1)} collective-permute-done((bf16[272,256]{1,0:T(8,128)(2,1)}, bf16[272,256]{1,0:T(8,128)(2,1)S(1)}, u32[]{:S(2)}, u32[]{:S(2)}) %collective-permute-start.34) | collective-permute-done | bytes 139296 | tf_op jit(solution)/shard_map/ppermute | solution.py:382
  231.2 5.3 %collective-permute-start.36 = (bf16[256,256]{1,0:T(8,128)(2,1)S(1)}, bf16[256,256]{1,0:T(8,128)(2,1)S(1)}, u32[]{:S(2)}, u32[]{:S(2)}) collective-permute-start(bf16[256,256]{1,0:T(8,128)(2,1)S(1)} %shard_map.253), channel_id=1, source_target_pairs={{0,0},{1,8},{2,4},{3,12},{4,5},{5,13},{6,1},{7,9},{8,10},{9,2},{10... | collective-permute-start | bytes 393224 | tf_op jit(solution)/shard_map/ppermute | solution.py:401
  243.5 14.1 %collective-permute-done.39 = bf16[256,1536]{1,0:T(8,128)(2,1)S(1)} collective-permute-done((bf16[256,1536]{1,0:T(8,128)(2,1)S(1)}, bf16[256,1536]{1,0:T(8,128)(2,1)S(1)}, u32[]{:S(2)}, u32[]{:S(2)}) %collective-permute-start.39) | collective-permute-done | bytes 786464 | tf_op jit(solution)/shard_map/ppermute | solution.py:520
  260.4 19.3 %collective-permute-done.42 = bf16[256,2304]{1,0:T(8,128)(2,1)S(1)} collective-permute-done((bf16[256,2304]{1,0:T(8,128)(2,1)S(1)}, bf16[256,2304]{1,0:T(8,128)(2,1)S(1)}, u32[]{:S(2)}, u32[]{:S(2)}) %collective-permute-start.42) | collective-permute-done | bytes 1179680 | tf_op jit(solution)/shard_map/ppermute | solution.py:520
  (176 shorter events, 99.8 us)
Async XLA Ops:
  3.8 51.8 %collective-permute-start.20 = (bf16[256,2304]{1,0:T(8,128)(2,1)S(1)}, bf16[256,2304]{1,0:T(8,128)(2,1)}, u32[]{:S(2)}, u32[]{:S(2)}) collective-permute-start(bf16[256,2304]{1,0:T(8,128)(2,1)S(1)} %shard_map.249.f0), channel_id=1, source_target_pairs={{0,8},{4,12},{8,0},{12,4},{1,9},{5,13},{9,1},{13,5},{2,10},{6,14},... | collective-permute-start | bytes 3538952 | tf_op jit(solution)/shard_map/ppermute | solution.py:378
  6.0 42.1 %collective-permute-start.4 = (bf16[272,1024]{1,0:T(8,128)(2,1)S(1)}, bf16[272,1024]{1,0:T(8,128)(2,1)S(1)}, u32[]{:S(2)}, u32[]{:S(2)}) collective-permute-start(bf16[272,1024]{1,0:T(8,128)(2,1)S(1)} %shard_map.246.q0), channel_id=1, source_target_pairs={{0,8},{4,12},{8,0},{12,4},{1,9},{5,13},{9,1},{13,5},{2,10},{6,14},... | collective-permute-start | bytes 1671176 | tf_op jit(solution)/shard_map/ppermute | solution.py:378
  11.0 56.3 %collective-permute-start.5 = (bf16[272,1024]{1,0:T(8,128)(2,1)S(1)}, bf16[272,1024]{1,0:T(8,128)(2,1)S(1)}, u32[]{:S(2)}, u32[]{:S(2)}) collective-permute-start(bf16[272,1024]{1,0:T(8,128)(2,1)S(1)} %shard_map.246.q0), channel_id=1, source_target_pairs={{0,4},{4,0},{8,12},{12,8},{1,5},{5,1},{9,13},{13,9},{2,6},{6,2},{1... | collective-permute-start | bytes 1671176 | tf_op jit(solution)/shard_map/ppermute | solution.py:378
  11.1 38.6 %collective-permute-start.1 = (bf16[256,256]{1,0:T(8,128)(2,1)S(1)}, bf16[256,256]{1,0:T(8,128)(2,1)S(1)}, u32[]{:S(2)}, u32[]{:S(2)}) collective-permute-start(bf16[256,256]{1,0:T(8,128)(2,1)S(1)} %copy-done.33), channel_id=1, source_target_pairs={{0,1},{1,5},{2,9},{3,13},{4,0},{5,4},{6,8},{7,12},{8,3},{9,7},{10,... | collective-permute-start | bytes 393224 | tf_op jit(solution)/shard_map/ppermute | solution.py:392
  14.7 38.8 %collective-permute-start.2 = (bf16[256,256]{1,0:T(8,128)(2,1)S(1)}, bf16[256,256]{1,0:T(8,128)(2,1)S(1)}, u32[]{:S(2)}, u32[]{:S(2)}) collective-permute-start(bf16[256,256]{1,0:T(8,128)(2,1)S(1)} %copy-done.33), channel_id=1, source_target_pairs={{0,2},{1,6},{2,10},{3,14},{4,3},{5,7},{6,11},{7,15},{8,0},{9,4},{1... | collective-permute-start | bytes 393224 | tf_op jit(solution)/shard_map/ppermute | solution.py:392
  48.1 20.8 %collective-permute-start.6 = (bf16[272,1024]{1,0:T(8,128)(2,1)S(1)}, bf16[272,1024]{1,0:T(8,128)(2,1)S(1)}, u32[]{:S(2)}, u32[]{:S(2)}) collective-permute-start(bf16[272,1024]{1,0:T(8,128)(2,1)S(1)} %collective-permute-done.4.q1), channel_id=1, source_target_pairs={{0,4},{4,0},{8,12},{12,8},{1,5},{5,1},{9,13},{13,9},{2,6},{6,2},{1... | collective-permute-start | bytes 1671176 | tf_op jit(solution)/shard_map/ppermute | solution.py:378
  54.2 63.7 %collective-permute-start.21 = (bf16[256,2304]{1,0:T(8,128)(2,1)S(1)}, bf16[256,2304]{1,0:T(8,128)(2,1)}, u32[]{:S(2)}, u32[]{:S(2)}) collective-permute-start(bf16[256,2304]{1,0:T(8,128)(2,1)S(1)} %shard_map.249.f0), channel_id=1, source_target_pairs={{0,4},{4,0},{8,12},{12,8},{1,5},{5,1},{9,13},{13,9},{2,6},{6,2},{1... | collective-permute-start | bytes 3538952 | tf_op jit(solution)/shard_map/ppermute | solution.py:378
  55.6 64.6 %collective-permute-start.22 = (bf16[256,2304]{1,0:T(8,128)(2,1)}, bf16[256,2304]{1,0:T(8,128)(2,1)}, u32[]{:S(2)}, u32[]{:S(2)}) collective-permute-start(bf16[256,2304]{1,0:T(8,128)(2,1)} %collective-permute-done.20.f1), channel_id=1, source_target_pairs={{0,4},{4,0},{8,12},{12,8},{1,5},{5,1},{9,13},{13,9},{2,6},{6,2},{1... | collective-permute-start | bytes 3538952 | tf_op jit(solution)/shard_map/ppermute | solution.py:378
  64.4 17.3 %collective-permute-start.8 = (bf16[512,256]{1,0:T(8,128)(2,1)}, bf16[512,256]{1,0:T(8,128)(2,1)}, u32[]{:S(2)}, u32[]{:S(2)}) collective-permute-start(bf16[512,256]{1,0:T(8,128)(2,1)} %w0.3), channel_id=1, source_target_pairs={{0,4},{4,0},{8,12},{12,8},{1,5},{5,1},{9,13},{13,9},{2,6},{6,2},{1... | collective-permute-start | bytes 786440 | tf_op jit(solution)/shard_map/ppermute | solution.py:378
  67.3 14.4 %collective-permute-start.9 = (bf16[512,256]{1,0:T(8,128)(2,1)}, bf16[512,256]{1,0:T(8,128)(2,1)}, u32[]{:S(2)}, u32[]{:S(2)}) collective-permute-start(bf16[512,256]{1,0:T(8,128)(2,1)} %collective-permute-done.7.w1), channel_id=1, source_target_pairs={{0,4},{4,0},{8,12},{12,8},{1,5},{5,1},{9,13},{13,9},{2,6},{6,2},{1... | collective-permute-start | bytes 786440 | tf_op jit(solution)/shard_map/ppermute | solution.py:378
  69.0 17.0 %collective-permute-start.16 = (bf16[256,256]{1,0:T(8,128)(2,1)}, bf16[256,256]{1,0:T(8,128)(2,1)S(1)}, u32[]{:S(2)}, u32[]{:S(2)}) collective-permute-start(bf16[256,256]{1,0:T(8,128)(2,1)} %convert_element_type.113), channel_id=1, source_target_pairs={{0,0},{1,4},{2,8},{3,12},{4,1},{5,5},{6,9},{7,13},{8,2},{9,6},{10,... | collective-permute-start | bytes 393224 | tf_op jit(solution)/shard_map/ppermute | solution.py:392
  86.0 14.6 %collective-permute-start.10 = (bf16[256,256]{1,0:T(8,128)(2,1)S(1)}, bf16[256,256]{1,0:T(8,128)(2,1)S(1)}, u32[]{:S(2)}, u32[]{:S(2)}) collective-permute-start(bf16[256,256]{1,0:T(8,128)(2,1)S(1)} %get-tuple-element.56), channel_id=1, source_target_pairs={{0,1},{1,0},{2,3},{3,2},{4,5},{5,4},{6,7},{7,6},{8,9},{9,8},{10,11... | collective-permute-start | bytes 393224 | tf_op jit(solution)/shard_map/ppermute | solution.py:382
  101.8 16.0 %collective-permute-start.13 = (bf16[256,256]{1,0:T(8,128)(2,1)S(1)}, bf16[256,256]{1,0:T(8,128)(2,1)S(1)}, u32[]{:S(2)}, u32[]{:S(2)}) collective-permute-start(bf16[256,256]{1,0:T(8,128)(2,1)S(1)} %add_convert_fusion.6.t0), channel_id=1, source_target_pairs={{0,1},{1,0},{2,3},{3,2},{4,5},{5,4},{6,7},{7,6},{8,9},{9,8},{10,11... | collective-permute-start | bytes 393224 | tf_op jit(solution)/shard_map/ppermute | solution.py:382
  103.7 14.1 %collective-permute-start.14 = (bf16[256,256]{1,0:T(8,128)(2,1)S(1)}, bf16[256,256]{1,0:T(8,128)(2,1)S(1)}, u32[]{:S(2)}, u32[]{:S(2)}) collective-permute-start(bf16[256,256]{1,0:T(8,128)(2,1)S(1)} %add_convert_fusion.6.t0), channel_id=1, source_target_pairs={{0,2},{1,3},{2,0},{3,1},{4,6},{5,7},{6,4},{7,5},{8,10},{9,11},{10,... | collective-permute-start | bytes 393224 | tf_op jit(solution)/shard_map/ppermute | solution.py:382
  141.7 27.9 %collective-permute-start.40 = (bf16[512,2304]{1,0:T(8,128)(2,1)S(1)}, bf16[512,2304]{1,0:T(8,128)(2,1)}, u32[]{:S(2)}, u32[]{:S(2)}) collective-permute-start(bf16[512,2304]{1,0:T(8,128)(2,1)S(1)} %get-tuple-element.93), channel_id=1, source_target_pairs={{0,4},{4,0},{8,12},{12,8},{1,5},{5,1},{9,13},{13,9},{2,6},{6,2},{1... | collective-permute-start | bytes 7077896 | tf_op jit(solution)/shard_map/ppermute | solution.py:378
  163.3 13.5 %collective-permute-start.24 = (bf16[256,256]{1,0:T(8,128)(2,1)S(1)}, bf16[256,256]{1,0:T(8,128)(2,1)S(1)}, u32[]{:S(2)}, u32[]{:S(2)}) collective-permute-start(bf16[256,256]{1,0:T(8,128)(2,1)S(1)} %get-tuple-element.66), channel_id=1, source_target_pairs={{0,2},{1,3},{2,0},{3,1},{4,6},{5,7},{6,4},{7,5},{8,10},{9,11},{10,... | collective-permute-start | bytes 393224 | tf_op jit(solution)/shard_map/ppermute | solution.py:382
  164.9 12.0 %collective-permute-start.23 = (bf16[256,256]{1,0:T(8,128)(2,1)S(1)}, bf16[256,256]{1,0:T(8,128)(2,1)S(1)}, u32[]{:S(2)}, u32[]{:S(2)}) collective-permute-start(bf16[256,256]{1,0:T(8,128)(2,1)S(1)} %get-tuple-element.65), channel_id=1, source_target_pairs={{0,1},{1,0},{2,3},{3,2},{4,5},{5,4},{6,7},{7,6},{8,9},{9,8},{10,11... | collective-permute-start | bytes 393224 | tf_op jit(solution)/shard_map/ppermute | solution.py:382
  166.1 70.4 %collective-permute-start.38 = (bf16[256,1536]{1,0:T(8,128)(2,1)}, bf16[256,1536]{1,0:T(8,128)(2,1)}, u32[]{:S(2)}, u32[]{:S(2)}) collective-permute-start(bf16[256,1536]{1,0:T(8,128)(2,1)} %add_convert_fusion.3), channel_id=1, source_target_pairs={{0,8},{4,12},{8,0},{12,4},{1,9},{5,13},{9,1},{13,5},{2,10},{6,14},... | collective-permute-start | bytes 2359304 | tf_op jit(solution)/shard_map/ppermute | solution.py:378
  172.2 66.1 %collective-permute-start.41 = (bf16[256,2304]{1,0:T(8,128)(2,1)}, bf16[256,2304]{1,0:T(8,128)(2,1)}, u32[]{:S(2)}, u32[]{:S(2)}) collective-permute-start(bf16[256,2304]{1,0:T(8,128)(2,1)} %add_convert_fusion.1), channel_id=1, source_target_pairs={{0,8},{4,12},{8,0},{12,4},{1,9},{5,13},{9,1},{13,5},{2,10},{6,14},... | collective-permute-start | bytes 3538952 | tf_op jit(solution)/shard_map/ppermute | solution.py:378
  176.9 40.9 %collective-permute-start.26 = (bf16[256,256]{1,0:T(8,128)(2,1)S(1)}, bf16[256,256]{1,0:T(8,128)(2,1)S(1)}, u32[]{:S(2)}, u32[]{:S(2)}) collective-permute-start(bf16[256,256]{1,0:T(8,128)(2,1)S(1)} %add_convert_fusion.5), channel_id=1, source_target_pairs={{0,0},{1,8},{2,4},{3,12},{4,5},{5,13},{6,1},{7,9},{8,10},{9,2},{10... | collective-permute-start | bytes 393224 | tf_op jit(solution)/shard_map/ppermute | solution.py:401
  194.9 19.3 %collective-permute-start.46 = (f32[16,256]{1,0:T(8,128)S(1)}, f32[16,256]{1,0:T(8,128)S(1)}, u32[]{:S(2)}, u32[]{:S(2)}) collective-permute-start(f32[16,256]{1,0:T(8,128)S(1)} %add.97), channel_id=1, source_target_pairs={{0,8},{4,12},{8,0},{12,4},{1,9},{5,13},{9,1},{13,5},{2,10},{6,14},... | collective-permute-start | bytes 49160 | tf_op jit(solution)/shard_map/ppermute | solution.py:378
  217.9 12.4 %collective-permute-start.34 = (bf16[272,256]{1,0:T(8,128)(2,1)}, bf16[272,256]{1,0:T(8,128)(2,1)S(1)}, u32[]{:S(2)}, u32[]{:S(2)}) collective-permute-start(bf16[272,256]{1,0:T(8,128)(2,1)} %get-tuple-element.82), channel_id=1, source_target_pairs={{0,2},{1,3},{2,0},{3,1},{4,6},{5,7},{6,4},{7,5},{8,10},{9,11},{10,... | collective-permute-start | bytes 417800 | tf_op jit(solution)/shard_map/ppermute | solution.py:382
  238.0 19.7 %collective-permute-start.39 = (bf16[256,1536]{1,0:T(8,128)(2,1)S(1)}, bf16[256,1536]{1,0:T(8,128)(2,1)S(1)}, u32[]{:S(2)}, u32[]{:S(2)}) collective-permute-start(bf16[256,1536]{1,0:T(8,128)(2,1)S(1)} %add_convert_fusion.2), channel_id=1, source_target_pairs={{0,16},{16,0},{1,17},{17,1},{2,18},{18,2},{3,19},{19,3},{4,20},{20... | collective-permute-start | bytes 2359304 | tf_op jit(solution)/shard_map/ppermute | solution.py:520
  240.5 39.3 %collective-permute-start.42 = (bf16[256,2304]{1,0:T(8,128)(2,1)S(1)}, bf16[256,2304]{1,0:T(8,128)(2,1)S(1)}, u32[]{:S(2)}, u32[]{:S(2)}) collective-permute-start(bf16[256,2304]{1,0:T(8,128)(2,1)S(1)} %add_convert_fusion), channel_id=1, source_target_pairs={{0,16},{16,0},{1,17},{17,1},{2,18},{18,2},{3,19},{19,3},{4,20},{20... | collective-permute-start | bytes 3538952 | tf_op jit(solution)/shard_map/ppermute | solution.py:520
  (58 other events, 701.0 us)

commit v2 on v1

--- a/solution.py
+++ b/solution.py
@@ -50,9 +50,11 @@
     return lax.dot_general(left, right, (((0,), (0,)), ((), ())), preferred_element_type=F32)
 
 
-def call(body, outs, args, scratch=(), flops=0, smem=None):
+def call(body, outs, args, scratch=(), flops=0, smem=None, anywhere=()):
     vm = pl.BlockSpec(memory_space=pltpu.VMEM)
-    in_specs = [vm] * len(args)
+    in_specs = [
+        pl.BlockSpec(memory_space=pltpu.HBM) if n in anywhere else vm for n in range(len(args))
+    ]
     if smem is not None:
         in_specs = [pl.BlockSpec(memory_space=pltpu.SMEM)] + in_specs
         args = (smem,) + tuple(args)
@@ -63,7 +65,7 @@
         in_specs=in_specs,
         out_specs=[vm] * len(outs),
         scratch_shapes=list(scratch),
-        compiler_params=pltpu.CompilerParams(vmem_limit_bytes=40 << 20),
+        compiler_params=pltpu.CompilerParams(vmem_limit_bytes=16 << 20),
         cost_estimate=pl.CostEstimate(flops=flops, bytes_accessed=moved, transcendentals=0),
     )(*args)
 
@@ -79,11 +81,26 @@
     return high, mid, rest - mid
 
 
-def pack_qkv(wq, wk, wv, ga, gf, out):
+def copy_all(pairs, sems):
+    copies = [pltpu.make_async_copy(src, dst, sems.at[n]) for n, (src, dst) in enumerate(pairs)]
+    for item in copies:
+        item.start()
+    return copies
+
+
+def pack_attn(wq, wk, wv, wp, x, dy, ga, gf, out, both, wide, sems):
     nq, nk = wq.shape[1], wk.shape[1]
-    out[0:BLK, 0:nq] = wq[...]
-    out[0:BLK, nq : nq + nk] = wk[...]
-    out[0:BLK, nq + nk :] = wv[...]
+    pairs = [
+        (wq, out.at[0:BLK, 0:nq]),
+        (wk, out.at[0:BLK, nq : nq + nk]),
+        (wv, out.at[0:BLK, nq + nk : nq + 2 * nk]),
+        (x, both.at[0:BLK, :]),
+        (dy, wide),
+    ]
+    for i in range(nq // BLK):
+        at = nq + 2 * nk + i * BLK
+        pairs.append((wp.at[i * BLK : (i + 1) * BLK, :], out.at[0:BLK, at : at + BLK]))
+    copies = copy_all(pairs, sems)
     rows = split3(ga[...]) + split3(gf[...])
     ids = lax.broadcasted_iota(jnp.int32, (16, BLK), 0)
     extra = jnp.zeros((16, BLK), F32)
@@ -91,14 +108,19 @@
         extra = jnp.where(ids == n, jnp.broadcast_to(row, (16, BLK)), extra)
     out[BLK : BLK + 16, :] = jnp.zeros((16, out.shape[1]), BF16)
     out[BLK : BLK + 16, 0:BLK] = extra.astype(BF16)
-
-
-def pack_ffn(wg, wu, wd, out):
+    for item in copies:
+        item.wait()
+    both[BLK:, :] = wide[...].astype(BF16)
+
+
+def pack_ffn(wg, wu, wd, out, sems):
     nf = wg.shape[1]
-    out[:, 0:nf] = wg[...]
-    out[:, nf : 2 * nf] = wu[...]
+    pairs = [(wg, out.at[:, 0:nf]), (wu, out.at[:, nf : 2 * nf])]
     for i in range(nf // BLK):
-        out[:, 2 * nf + i * BLK : 2 * nf + (i + 1) * BLK] = wd[i * BLK : (i + 1) * BLK, :]
+        at = 2 * nf + i * BLK
+        pairs.append((wd.at[i * BLK : (i + 1) * BLK, :], out.at[:, at : at + BLK]))
+    for item in copy_all(pairs, sems):
+        item.wait()
 
 
 def rope(values, cos, sin):
@@ -115,12 +137,16 @@
 
 def attn_forward(
     ids, x0, x1, x2, x3, q0, q1, q2, q3, cos_r, sin_r, qg_r, kg_r,
-    x_out, a_out, gains, o_out, qn_out, kn_out, sc_out, qr_out, kr_out, v_out, pr_out, qkv,
+    x_out, dy_out, a_out, gains, o_out, qn_out, kn_out, sc_out, qr_out, kr_out, v_out, pr_out,
+    t0, t1, t2, t3, qkv, place, sems,
 ):
     s1 = ids[2]
     qs = (q0, q1, q2, q3)
-    for k, ref in enumerate((x0, x1, x2, x3)):
-        x_out[s1 ^ SWAP[k]] = ref[...]
+    nd = qkv.shape[1]
+    pairs = [(ref.at[0:BLK, :], x_out.at[s1 ^ SWAP[k]]) for k, ref in enumerate((x0, x1, x2, x3))]
+    pairs += [(ref.at[BLK:, :], dy_out.at[s1 ^ SWAP[k]]) for k, ref in enumerate((x0, x1, x2, x3))]
+    for item in copy_all(pairs, sems):
+        item.wait()
     total = jnp.zeros((BLK, 1), F32)
     for p in range(ROWS):
         x = x_out[p].astype(F32)
@@ -132,7 +158,7 @@
     for p in range(ROWS):
         a_out[p] = ((x_out[p].astype(F32) * r_one) * gains[p : p + 1, :]).astype(BF16)
     for p in range(ROWS):
-        part = dot(a_out[p], qs[p][0:BLK, :])
+        part = dot(a_out[p], qs[p][0:BLK, 0:nd])
         if p == 0:
             qkv[...] = part
         else:
@@ -172,26 +198,25 @@
         o_out[:, n * HEAD_DIMENSION : (n + 1) * HEAD_DIMENSION] = dot(
             probs.astype(BF16), head(v_out, g)
         ).astype(BF16)
-
-
-def project(ids, o, w0, w1, w2, w3, s0, s1, s2, s3, place):
-    for p, w in enumerate((w0, w1, w2, w3)):
-        place[p] = dot(o[...], w[...]).astype(BF16)
-    for k, slot in enumerate((s0, s1, s2, s3)):
+    for p in range(ROWS):
+        acc = dot(o_out[:, 0:BLK], qs[p][0:BLK, nd : nd + BLK])
+        for i in range(1, o_out.shape[1] // BLK):
+            at = nd + i * BLK
+            acc = acc + dot(o_out[:, i * BLK : (i + 1) * BLK], qs[p][0:BLK, at : at + BLK])
+        place[p] = acc.astype(BF16)
+    for k, slot in enumerate((t0, t1, t2, t3)):
         slot[...] = place[ids[1] ^ k]
 
 
 def ffn(
-    ids, t0, t1, t2, t3, x, y0, y1, y2, y3, f0, f1, f2, f3, gains,
-    s0, s1, s2, s3, b_out, dy_out, m_out, d_out, h_out, gu, da, place,
+    ids, t0, t1, t2, t3, x, dy, f0, f1, f2, f3, gains,
+    s0, s1, s2, s3, b_out, m_out, d_out, h_out, gu, da, place,
 ):
-    c, swapped = ids[1], ids[2]
+    c = ids[1]
     fs = (f0, f1, f2, f3)
     nf = m_out.shape[1]
     for k, ref in enumerate((t0, t1, t2, t3)):
         h_out[c ^ k] = ref[...].astype(F32)
-    for k, ref in enumerate((y0, y1, y2, y3)):
-        dy_out[swapped ^ SWAP[k]] = ref[...]
     total = jnp.zeros((BLK, 1), F32)
     for p in range(ROWS):
         h = h_out[p] + x[p].astype(F32)
@@ -209,9 +234,9 @@
     for i in range(nf // BLK):
         at = slice(2 * nf + i * BLK, 2 * nf + (i + 1) * BLK)
         cols = slice(i * BLK, (i + 1) * BLK)
-        acc = dot_nt(dy_out[0], fs[0][:, at])
+        acc = dot_nt(dy[0], fs[0][:, at])
         for p in range(1, ROWS):
-            acc = acc + dot_nt(dy_out[p], fs[p][:, at])
+            acc = acc + dot_nt(dy[p], fs[p][:, at])
         da[:, cols] = acc
     for i in range(nf // BLK):
         cols = slice(i * BLK, (i + 1) * BLK)
@@ -228,7 +253,7 @@
         slot[...] = place[c ^ k]
 
 
-def down(ids, m, f0, f1, f2, f3, h, s0, s1, s2, s3, h_own, place):
+def down(ids, m, f0, f1, f2, f3, h, place, h_own):
     nf = m.shape[1]
     for p, f in enumerate((f0, f1, f2, f3)):
         acc = jnp.zeros((BLK, BLK), F32)
@@ -236,38 +261,35 @@
             at = slice(2 * nf + i * BLK, 2 * nf + (i + 1) * BLK)
             acc = acc + dot(m[:, i * BLK : (i + 1) * BLK], f[:, at])
         place[p] = acc.astype(BF16)
-    for k, slot in enumerate((s0, s1, s2, s3)):
-        slot[...] = place[ids[1] ^ k]
     h_own[...] = h[ids[1]]
 
 
-def ffn_grads(b, d, m, dy, send, keep):
+def ffn_grads(b, d, m, dy, down_s, gu_s, down_k, gu_k):
     nf = m.shape[1]
     for p in range(ROWS):
+        out = down_k if p < 2 else down_s
+        at = (p % 2) * nf
+        out[at : at + nf, :] = dot_tn(m[...], dy[p]).astype(BF16)
+    for p in range(ROWS):
+        out = gu_k if p < 2 else gu_s
+        out[(p % 2) * BLK : (p % 2 + 1) * BLK, :] = dot_tn(b[p], d[...]).astype(BF16)
+
+
+def proj_grads(o, dh, send, keep):
+    width = o.shape[1]
+    for p in range(ROWS):
         out = keep if p < 2 else send
-        rows = slice((p % 2) * BLK, (p % 2 + 1) * BLK)
-        out[rows, 0 : 2 * nf] = dot_tn(b[p], d[...]).astype(BF16)
-        for i in range(nf // BLK):
-            at = slice(2 * nf + i * BLK, 2 * nf + (i + 1) * BLK)
-            out[rows, at] = dot_tn(m[:, i * BLK : (i + 1) * BLK], dy[p]).astype(BF16)
-
-
-def attn_grads(a, d, o, dh, send, keep):
-    nd = d.shape[1]
+        at = (p % 2) * width
+        out[at : at + width, :] = dot_tn(o[...], dh[p]).astype(BF16)
+
+
+def qkv_grads(a, d, send, keep):
     for p in range(ROWS):
         out = keep if p < 2 else send
-        rows = slice((p % 2) * BLK, (p % 2 + 1) * BLK)
-        out[rows, 0:nd] = dot_tn(a[p], d[...]).astype(BF16)
-        for i in range(o.shape[1] // BLK):
-            at = slice(nd + i * BLK, nd + (i + 1) * BLK)
-            out[rows, at] = dot_tn(o[:, i * BLK : (i + 1) * BLK], dh[p]).astype(BF16)
-
-
-def attn_backward(
-    ids, t0, t1, t2, t3, h, dy, gains, w0, w1, w2, w3, x, q0, q1, q2, q3,
-    o, qn, kn, sc, qr, kr, v, pr, cos_r, sin_r, qg_r, kg_r,
-    s0, s1, s2, s3, dhb, d_qkv, dh_own, sums, dh, part,
-):
+        out[(p % 2) * BLK : (p % 2 + 1) * BLK, :] = dot_tn(a[p], d[...]).astype(BF16)
+
+
+def norm_backward(ids, t0, t1, t2, t3, h, dy, gains, w0, w1, w2, w3, dhb, dh_own, d_o, sums, dh):
     r, c = ids[0], ids[1]
     for k, ref in enumerate((t0, t1, t2, t3)):
         dh[c ^ k] = ref[...].astype(F32)
@@ -291,11 +313,22 @@
         dh[p] = out
         dhb[p] = out.astype(BF16)
     dh_own[...] = dh[c]
+    width = d_o.shape[1]
+    for i in range(width // BLK):
+        at = slice(w0.shape[1] - width + i * BLK, w0.shape[1] - width + (i + 1) * BLK)
+        grad = dot_nt(dhb[0], w0[0:BLK, at])
+        for p, w in ((1, w1), (2, w2), (3, w3)):
+            grad = grad + dot_nt(dhb[p], w[0:BLK, at])
+        d_o[:, i * BLK : (i + 1) * BLK] = grad.astype(BF16)
+
+
+def attn_backward(
+    ids, d_o, sums_in, y_place, gains, x, q0, q1, q2, q3, o, qn, kn, sc, qr, kr, v, pr, cos_r, sin_r, qg_r, kg_r,
+    s0, s1, s2, s3, d_qkv, part, sums,
+):
+    r, c = ids[0], ids[1]
     nq, nkv = qn.shape[1] // HEAD_DIMENSION, kn.shape[1] // HEAD_DIMENSION
-    d_o = dot_nt(dhb[0], w0[...])
-    for p, w in ((1, w1), (2, w2), (3, w3)):
-        d_o = d_o + dot_nt(dhb[p], w[...])
-    d_o = d_o.astype(BF16)
+    sums[...] = sums_in[...]
     cos, sin = cos_r[...], sin_r[...]
     factor = HEAD_DIMENSION ** (-0.5)
     q_sum = jnp.zeros((1, HEAD_DIMENSION), F32)
@@ -309,7 +342,7 @@
         d_k = jnp.zeros((BLK, HEAD_DIMENSION), F32)
         d_v = jnp.zeros((BLK, HEAD_DIMENSION), F32)
         for n in range(g * GROUPS, (g + 1) * GROUPS):
-            grad = d_o[:, n * HEAD_DIMENSION : (n + 1) * HEAD_DIMENSION]
+            grad = head(d_o, n)
             delta = jnp.sum(grad.astype(F32) * head(o, n).astype(F32), -1, keepdims=True)
             probs = pr[n]
             d_v = d_v + dot_tn(probs.astype(BF16), grad)
@@ -340,7 +373,7 @@
     r_one = lax.rsqrt(total / MODEL_WIDTH + epsilon)
     inner = jnp.zeros((BLK, 1), F32)
     for p, q in enumerate((q0, q1, q2, q3)):
-        d_a = dot_nt(d_qkv[...], q[0:BLK, :])
+        d_a = dot_nt(d_qkv[...], q[0:BLK, 0 : d_qkv.shape[1]])
         term = d_a * (x[p].astype(F32) * r_one)
         sums[pl.ds(r ^ SWAP[p], 1), :] = jnp.sum(term, 0, keepdims=True)
         inner = inner + jnp.sum(term * gains[p : p + 1, :], -1, keepdims=True)
@@ -349,19 +382,30 @@
     high = row.astype(BF16).astype(F32)
     ids16 = lax.broadcasted_iota(jnp.int32, (16, BLK), 0)
     tail = jnp.where(ids16 == 0, high, jnp.where(ids16 == 1, row - high, 0.0)).astype(BF16)
+    parts = split3(sums[...])
     for k, slot in enumerate((s0, s1, s2, s3)):
         slot[0:BLK, :] = part[c ^ k]
-        slot[BLK : BLK + 16, :] = tail
-
-
-def finish(ids, t0, t1, t2, t3, dh_own, x, gains, out):
+        slot[BLK : 2 * BLK, :] = y_place[c ^ k]
+        slot[2 * BLK : 2 * BLK + 16, :] = tail
+        for i, item in enumerate(parts):
+            slot[2 * BLK + 16 * (i + 1) : 2 * BLK + 16 * (i + 2), :] = item.astype(BF16)
+
+
+def finish(ids, t0, t1, t2, t3, dh_own, h_own, x, gains, out, sums, each):
     c = ids[1]
     refs = (t0, t1, t2, t3)
-    d_a = refs[0][0:BLK, :].astype(F32)
-    tail = refs[0][BLK : BLK + 16, :].astype(F32)
+    rows = lambda ref, at, n: ref[at : at + n, :].astype(F32)
+    d_a = rows(t0, 0, BLK)
+    y = h_own[...] + rows(t0, BLK, BLK)
+    tail = rows(t0, 2 * BLK, 16)
     for ref in refs[1:]:
-        d_a = d_a + ref[0:BLK, :].astype(F32)
-        tail = tail + ref[BLK : BLK + 16, :].astype(F32)
+        d_a = d_a + rows(ref, 0, BLK)
+        y = y + rows(ref, BLK, BLK)
+        tail = tail + rows(ref, 2 * BLK, 16)
+    for k, ref in enumerate(refs):
+        at = 2 * BLK + 16
+        each[c ^ k] = rows(ref, at, 16) + rows(ref, at + 16, 16) + rows(ref, at + 32, 16)
+    sums[...] = (each[0] + each[1]) + (each[2] + each[3])
     row = jnp.broadcast_to(tail[0:1] + tail[1:2], (128, BLK))
     inner = jnp.transpose(row)[:, 0:1] / MODEL_WIDTH
     total = jnp.zeros((BLK, 1), F32)
@@ -371,7 +415,8 @@
     r_one = lax.rsqrt(total / MODEL_WIDTH + epsilon)
     gain = gains[pl.ds(c, 1), :]
     n_one = x[c].astype(F32) * r_one
-    out[...] = (dh_own[...] + r_one * (d_a * gain - n_one * inner)).astype(BF16)
+    out[0:BLK, :] = (dh_own[...] + r_one * (d_a * gain - n_one * inner)).astype(BF16)
+    out[BLK:, :] = y.astype(BF16)
 
 
 def row_swap(values, bit):
@@ -380,11 +425,6 @@
 
 def col_swap(values, bit):
     return lax.ppermute(values, "col", [(i, i ^ bit) for i in range(ROWS)])
-
-
-def all_of_row(shard):
-    other = row_swap(shard, 2)
-    return (shard, other, row_swap(shard, 1), row_swap(other, 1))
 
 
 def to_sequence(block):
@@ -402,6 +442,44 @@
         block, ("row", "col"),
         [(r * ROWS + c, (r ^ SWAP[c]) * ROWS + r) for r in range(ROWS) for c in range(ROWS)],
     )
+
+
+def after(values, gate):
+    return lax.optimization_barrier((values, gate))[0]
+
+
+def core_stage(send, keep):
+    got = row_swap(send, 1)
+    half = keep.shape[0] // 2
+    mine = keep[:half].astype(F32) + got[:half].astype(F32)
+    theirs = keep[half:].astype(F32) + got[half:].astype(F32)
+    return mine, theirs.astype(BF16)
+
+
+def y_stage(parts):
+    mine, theirs = parts
+    return (mine + row_swap(theirs, 2).astype(F32)).astype(BF16)
+
+
+def last_sum(own, other, *outs):
+    at = 0
+    for out in outs:
+        cols = slice(at, at + out.shape[1])
+        out[...] = own[:, cols].astype(F32) + other[:, cols].astype(F32)
+        at = at + out.shape[1]
+
+
+def last_split(own, total, *outs):
+    at = 0
+    for out in outs:
+        out[...] = total[:, at : at + out.shape[1]]
+        at = at + out.shape[1]
+
+
+def dp_send(n_dp, total):
+    if n_dp == 2:
+        return lax.ppermute(total, "dp", [(0, 1), (1, 0)])
+    return lax.psum(total, "dp").astype(F32)
 
 
 def scatter_col(slots):
@@ -435,117 +513,131 @@
     blocks = (ROWS, BLK, BLK)
     slot = sds((BLK, BLK), BF16)
 
-    xs = to_sequence(block_input)
-    (msg_q,) = call(
-        pack_qkv, [sds((BLK + 16, width_qkv), BF16)],
-        (query_weight, key_weight, value_weight, attn_gain.reshape(1, -1), ffn_gain.reshape(1, -1)),
-    )
-    q_all = all_of_row(msg_q)
-    p_all = all_of_row(projection_weight)
-    (msg_f,) = call(pack_ffn, [sds((BLK, 3 * width_ff), BF16)], (w_gate, w_up, w_down))
-    f_all = all_of_row(msg_f)
-    ys = to_sequence(cotangent.astype(BF16))
-
-    x_full, a_full, gains, o, qn, kn, sc, qr, kr, v, pr = call(
+    sem = lambda n: pltpu.SemaphoreType.DMA((n,))
+    msg_q, msg_x = call(
+        pack_attn, [sds((BLK + 16, width_qkv + width_q), BF16), sds((2 * BLK, BLK), BF16)],
+        (query_weight, key_weight, value_weight, projection_weight, block_input, cotangent,
+         attn_gain.reshape(1, -1), ffn_gain.reshape(1, -1)),
+        [pltpu.VMEM((BLK, BLK), F32), sem(5 + width_q // BLK)], 0, None, (0, 1, 2, 3, 4, 5),
+    )
+    xs = to_sequence(msg_x)
+    q_far = row_swap(msg_q, 2)
+    q_all = (msg_q, q_far, row_swap(msg_q, 1), row_swap(q_far, 1))
+    (msg_f,) = call(
+        pack_ffn, [sds((BLK, 3 * width_ff), BF16)],
+        after((w_gate, w_up, w_down), (q_far, xs)), [sem(2 + width_ff // BLK)], 0, None, (0, 1, 2),
+    )
+    f_far = row_swap(msg_f, 2)
+
+    x_full, dy_full, a_full, gains, o, qn, kn, sc, qr, kr, v, pr, *slots = call(
         attn_forward,
         [
-            sds(blocks, BF16), sds(blocks, BF16), sds((8, BLK), F32), sds((BLK, width_q), BF16),
+            sds(blocks, BF16), sds(blocks, BF16), sds(blocks, BF16), sds((8, BLK), F32),
+            sds((BLK, width_q), BF16),
             sds((BLK, width_q), F32), sds((BLK, width_kv), F32), sds((BLK, HEAD_DIMENSION), F32),
             sds((BLK, width_q), BF16), sds((BLK, width_kv), BF16), sds((BLK, width_kv), BF16),
             sds((nq, BLK, BLK), F32),
-        ],
-        (*xs, *q_all, cos, sin, qg, kg), [pltpu.VMEM((BLK, width_qkv), F32)],
-        2 * BLK * MODEL_WIDTH * width_qkv, ids,
-    )
-    slots = call(
-        project, [slot] * ROWS, (o, *p_all), [pltpu.VMEM(blocks, BF16)],
-        2 * BLK * MODEL_WIDTH * width_q, ids,
-    )
-    h_sum = add_all(scatter_col(slots)).astype(BF16)
+        ] + [slot] * ROWS,
+        (*xs, *q_all, cos, sin, qg, kg),
+        [pltpu.VMEM((BLK, width_qkv), F32), pltpu.VMEM(blocks, BF16), sem(2 * ROWS)],
+        2 * BLK * MODEL_WIDTH * (width_qkv + width_q), ids, (0, 1, 2, 3),
+    )
+    h_slots = scatter_col(slots)
+    h_sum = add_all(h_slots).astype(BF16)
     h_parts = gather_col(h_sum)
-    *slots, b_full, dy_full, m, d_gu, h_full = call(
+    f_all = (msg_f, f_far, row_swap(after(msg_f, h_slots), 1), row_swap(after(f_far, h_parts), 1))
+    *slots, b_full, m, d_gu, h_full = call(
         ffn,
         [slot] * ROWS
         + [
-            sds(blocks, BF16), sds(blocks, BF16), sds((BLK, width_ff), BF16),
+            sds(blocks, BF16), sds((BLK, width_ff), BF16),
             sds((BLK, 2 * width_ff), BF16), sds(blocks, F32),
         ],
-        (*h_parts, x_full, *ys, *f_all, gains),
+        (*h_parts, x_full, dy_full, *f_all, gains),
         [
             pltpu.VMEM((BLK, 2 * width_ff), F32), pltpu.VMEM((BLK, width_ff), F32),
             pltpu.VMEM(blocks, BF16),
         ],
         10 * BLK * MODEL_WIDTH * width_ff, ids,
     )
-    b_sum = add_all(scatter_col(slots)).astype(BF16)
+    b_slots = scatter_col(slots)
+    down_s, gu_s, down_k, gu_k = call(
+        ffn_grads, [sds((2 * width_ff, BLK), BF16), sds((2 * BLK, 2 * width_ff), BF16)] * 2,
+        (b_full, d_gu, m, dy_full), (), 6 * BLK * MODEL_WIDTH * width_ff,
+    )
+    mid_down, mid_gu = core_stage(down_s, down_k), core_stage(gu_s, gu_k)
+    b_sum = add_all(after(b_slots, (mid_down, mid_gu))).astype(BF16)
     b_parts = gather_col(b_sum)
-
-    f_send, f_keep = call(
-        ffn_grads, [sds((2 * BLK, 3 * width_ff), BF16)] * 2, (b_full, d_gu, m, dy_full),
-        (), 6 * BLK * MODEL_WIDTH * width_ff,
-    )
-    *slots, h_own = call(
-        down, [slot] * ROWS + [sds((BLK, BLK), F32)], (m, *f_all, h_full),
-        [pltpu.VMEM(blocks, BF16)], 2 * BLK * MODEL_WIDTH * width_ff, ids,
-    )
-    y_own = (h_own + add_all(scatter_col(slots))).astype(BF16)
-    block_output = to_owner(y_own).astype(F32)
-
-    *slots, dh_full, d_qkv, dh_own, sums = call(
+    y_down, y_gu = y_stage(mid_down), y_stage(mid_gu)
+    x_down, x_gu = dp_send(n_dp, y_down), dp_send(n_dp, y_gu)
+    y_place, h_own = call(
+        down, [sds(blocks, BF16), sds((BLK, BLK), F32)], (m, *f_all, h_full),
+        (), 2 * BLK * MODEL_WIDTH * width_ff, ids,
+    )
+
+    dh_full, dh_own, d_o, sums = call(
+        norm_backward,
+        [sds(blocks, BF16), sds((BLK, BLK), F32), sds((BLK, width_q), BF16), sds((16, BLK), F32)],
+        (*after(b_parts, (y_down, y_place)), h_full, dy_full, gains, *q_all),
+        [pltpu.VMEM(blocks, F32)], 2 * BLK * MODEL_WIDTH * width_q, ids,
+    )
+    proj_s, proj_k = call(
+        proj_grads, [sds((2 * width_q, BLK), BF16)] * 2, (o, dh_full), (),
+        2 * BLK * MODEL_WIDTH * width_q,
+    )
+    *slots, d_qkv = call(
         attn_backward,
-        [sds((BLK + 16, BLK), BF16)] * ROWS
-        + [
-            sds(blocks, BF16), sds((BLK, width_qkv), BF16), sds((BLK, BLK), F32),
-            sds((16, BLK), F32),
-        ],
-        (*b_parts, h_full, dy_full, gains, *p_all, x_full, *q_all,
+        [sds((2 * BLK + 64, BLK), BF16)] * ROWS + [sds((BLK, width_qkv), BF16)],
+        (after(d_o, proj_s), sums, y_place, gains, x_full, *q_all,
          o, qn, kn, sc, qr, kr, v, pr, cos, sin, qg, kg),
-        [pltpu.VMEM(blocks, F32), pltpu.VMEM(blocks, BF16)],
-        2 * BLK * MODEL_WIDTH * (width_qkv + width_q) + 10 * BLK * BLK * width_q, ids,
+        [pltpu.VMEM(blocks, BF16), pltpu.VMEM((16, BLK), F32)],
+        2 * BLK * MODEL_WIDTH * width_qkv + 10 * BLK * BLK * width_q, ids,
     )
     a_parts = scatter_col(slots)
-    a_send, a_keep = call(
-        attn_grads, [sds((2 * BLK, width_qkv + width_q), BF16)] * 2, (a_full, d_qkv, o, dh_full),
-        (), 2 * BLK * MODEL_WIDTH * (width_qkv + width_q),
-    )
-    (in_own,) = call(finish, [slot], (*a_parts, dh_own, x_full, gains), (), 0, ids)
-    input_grad = to_owner(in_own).astype(F32)
-
-    def reduce_grad(send, keep):
-        got = row_swap(send, 1)
-        mine = keep[0:BLK].astype(F32) + got[0:BLK].astype(F32)
-        theirs = (keep[BLK:].astype(F32) + got[BLK:].astype(F32)).astype(BF16)
-        total = (mine + row_swap(theirs, 2).astype(F32)).astype(BF16)
-        if n_dp == 2:
-            return total.astype(F32) + lax.ppermute(total, "dp", [(0, 1), (1, 0)]).astype(F32)
-        return lax.psum(total, "dp").astype(F32)
-
-    g_f = reduce_grad(f_send, f_keep)
-    g_a = reduce_grad(a_send, a_keep)
-
-    for bit in (1, 2):
-        sums = sums + col_swap(sums, bit)
-    for bit in (1, 2):
+    qkv_s, qkv_k = call(
+        qkv_grads, [sds((2 * BLK, width_qkv), BF16)] * 2,
+        (a_full, after(d_qkv, y_gu)), (), 2 * BLK * MODEL_WIDTH * width_qkv,
+    )
+    mid_proj = core_stage(proj_s, proj_k)
+    mid_qkv = core_stage(qkv_s, qkv_k)
+    y_proj, y_qkv = y_stage(mid_proj), y_stage(mid_qkv)
+    msg_o, sums = call(
+        finish, [sds((2 * BLK, BLK), BF16), sds((16, BLK), F32)],
+        (*after(a_parts, (y_proj, y_qkv)), dh_own, h_own, x_full, gains),
+        [pltpu.VMEM((ROWS, 16, BLK), F32)], 0, ids,
+    )
+    msg_o = to_owner(msg_o)
+    input_grad = msg_o[0:BLK].astype(F32)
+    block_output = msg_o[BLK:].astype(F32)
+    for bit in (2, 1):
         sums = sums + row_swap(sums, bit)
-    if n_dp == 2:
-        sums = sums + lax.ppermute(sums, "dp", [(0, 1), (1, 0)])
-    else:
-        sums = lax.psum(sums, "dp")
+    other = dp_send(n_dp, sums)
+    sums = sums + other if n_dp == 2 else other
+
+    def both(own, other):
+        return other if other.dtype == F32 else own.astype(F32) + other.astype(F32)
+
+    y_down, y_gu = after((y_down, y_gu), y_qkv)
+    g_down = both(y_down, x_down)
+    final = last_sum if n_dp == 2 else last_split
+    g_gate, g_up = call(final, [sds((BLK, width_ff), F32)] * 2, (y_gu, x_gu))
+    g_proj = both(y_proj, dp_send(n_dp, y_proj))
+    g_query, g_key, g_value = call(
+        final, [sds((BLK, width_q), F32), sds((BLK, width_kv), F32), sds((BLK, width_kv), F32)],
+        (y_qkv, dp_send(n_dp, y_qkv)),
+    )
     attn_dgain = lax.dynamic_slice_in_dim(sums, r, 1, 0)[0]
     ffn_dgain = lax.dynamic_slice_in_dim(sums, ROWS + r, 1, 0)[0]
-    slabs = lambda values: jnp.concatenate(
-        [values[:, i * BLK : (i + 1) * BLK] for i in range(values.shape[1] // BLK)], 0
-    )
     return (
         block_output,
         input_grad,
-        g_a[:, :width_q],
-        g_a[:, width_q : width_q + width_kv],
-        g_a[:, width_q + width_kv : width_qkv],
-        slabs(g_a[:, width_qkv:]),
-        g_f[:, :width_ff],
-        g_f[:, width_ff : 2 * width_ff],
-        slabs(g_f[:, 2 * width_ff :]),
+        g_query,
+        g_key,
+        g_value,
+        g_proj,
+        g_gate,
+        g_up,
+        g_down,
         attn_dgain,
         ffn_dgain,
         sums[8, :HEAD_DIMENSION],

time: 285 us -> 206 us (0.72)
  waiting for transfers between devices: 139 us -> 84.6 us
  starting transfers between devices: 91.9 us -> 68.8 us
  other arithmetic: 13 us -> 6 us
  local copies, waits for them, and re-layouts: 15 us -> 18.5 us
  Pallas kernels: 22.8 us -> 26.2 us
    ppermute x15 -> x16, waiting for transfers between devices: 50.8 us -> 25.8 us  [row_swap(): return lax.ppermute(values, 'row', [(i, i ^ bit) for i in range(ROWS)])]
    ppermute x3 -> x5, waiting for transfers between devices: 33.5 us -> 13.7 us  [dp_send(): return lax.ppermute(total, 'dp', [(0, 1), (1, 0)])]
    ppermute x8 -> x4, starting transfers between devices: 22.9 us -> 6.97 us  [to_sequence(): lax.ppermute(block, ('row', 'col'), [(r * ROWS + c, c * ROWS + (r ^ k)) f...]
    ppermute x20 -> x15, starting transfers between devices: 35.1 us -> 20.5 us  [col_swap(): return lax.ppermute(values, 'col', [(i, i ^ bit) for i in range(ROWS)])]
    ppermute x15 -> x16, starting transfers between devices: 23.9 us -> 35.1 us  [row_swap(): return lax.ppermute(values, 'row', [(i, i ^ bit) for i in range(ROWS)])]
    convert_element_type x10 -> x11, other arithmetic: 10.6 us -> 3.1 us  [the longest x4 1.57 us: y_stage(): return (mine + row_swap(theirs, 2).astype(F32)).astype(BF16)]
    ppermute x8 -> x4, waiting for transfers between devices: 11.5 us -> 4.31 us  [to_sequence(): lax.ppermute(block, ('row', 'col'), [(r * ROWS + c, c * ROWS + (r ^ k)) f...]
    unnamed x68 -> x48, local copies, waits for them, and re-layouts: 10.9 us -> 17.4 us
  transfers between devices with their start and end apart: 48 -> 41, of which waited for: 21 -> 19; matrix products, arithmetic and copies ran while one was open for 5% -> 3% of each run, Pallas kernels for 6% -> 9%
where the time goes in v2:
time: 206 us; the launch traced here: 205 us
  waiting for transfers between devices  84.6 us (41%)
  starting transfers between devices  68.8 us (33%)
  Pallas kernels  26.2 us (13%)
  local copies, waits for them, and re-layouts  18.5 us (9%)
  other arithmetic  6 us (3%)
    ppermute x15, waiting for transfers between devices, col_swap(): return lax.ppermute(values, 'col', [(i, i ^ bit) for i in range(ROWS)])  36.2 us
    ppermute x16, starting transfers between devices, row_swap(): return lax.ppermute(values, 'row', [(i, i ^ bit) for i in range(ROWS)])  35.1 us
    pallas_call x13, Pallas kernels, call(): pl.pallas_call(body, out_shape=[jax.ShapeDtypeStruct(o.shape, o.dtype) fo...  26.2 us
    ppermute x16, waiting for transfers between devices, row_swap(): return lax.ppermute(values, 'row', [(i, i ^ bit) for i in range(ROWS)])  25.8 us
    ppermute x15, starting transfers between devices, col_swap(): return lax.ppermute(values, 'col', [(i, i ^ bit) for i in range(ROWS)])  20.5 us
    unnamed x48, local copies, waits for them, and re-layouts  17.4 us
    ppermute x5, waiting for transfers between devices, dp_send(): return lax.ppermute(total, 'dp', [(0, 1), (1, 0)])  13.7 us
    ppermute x4, starting transfers between devices, to_sequence(): lax.ppermute(block, ('row', 'col'), [(r * ROWS + c, c * ROWS + (r ^ k)) f...  6.97 us
  transfers between devices with their start and end apart: 41, of which 19 were waited for; matrix products, arithmetic and copies ran while one was open for 3% of the time, Pallas kernels for 9%

profile of v2, /device:TPU:1, one launch (start us, length us, event | category | flops | bytes accessed | tf_op | source)
XLA Modules:
  0.0 205.0 jit_solution(12791868073294872360)
XLA Ops:
  10.1 3.1 %collective-permute-start.3 = (bf16[512,256]{1,0:T(8,128)(2,1)S(1)}, bf16[512,256]{1,0:T(8,128)(2,1)S(1)}, u32[]{:S(2)}, u32[]{:S(2)}) collective-permute-start(bf16[512,256]{1,0:T(8,128)(2,1)S(1)} %get-tuple-element.86), channel_id=1, source_target_pairs={{0,3},{1,7},{2,11},{3,15},{4,2},{5,6},{6,10},{7,14},{8,1},{9,5},{1... | collective-permute-start | bytes 786440 | tf_op jit(solution)/shard_map/ppermute | solution.py:432
  17.1 4.3 %collective-permute-done.3.x3 = bf16[512,256]{1,0:T(8,128)(2,1)S(1)} collective-permute-done((bf16[512,256]{1,0:T(8,128)(2,1)S(1)}, bf16[512,256]{1,0:T(8,128)(2,1)S(1)}, u32[]{:S(2)}, u32[]{:S(2)}) %collective-permute-start.3) | collective-permute-done | bytes 262176 | tf_op jit(solution)/shard_map/ppermute | solution.py:432
  22.1 18.7 %collective-permute-start.5 = (bf16[272,1536]{1,0:T(8,128)(2,1)S(1)}, bf16[272,1536]{1,0:T(8,128)(2,1)S(1)}, u32[]{:S(2)}, u32[]{:S(2)}) collective-permute-start(bf16[272,1536]{1,0:T(8,128)(2,1)S(1)} %get-tuple-element.87.q0.w0), channel_id=1, source_target_pairs={{0,4},{4,0},{8,12},{12,8},{1,5},{5,1},{9,13},{13,9},{2,6},{6,2},{1... | collective-permute-start | bytes 2506760 | tf_op jit(solution)/shard_map/ppermute | solution.py:423
  53.5 6.0 %shard_map.247 = (bf16[4,256,256]{2,1,0:T(8,128)(2,1)S(1)}, bf16[4,256,256]{2,1,0:T(8,128)(2,1)S(1)}, bf16[4,256,256]{2,1,0:T(8,128)(2,1)S(1)}, f32[8,256]{1,0:T...) custom-call(s32[3]{0:T(128)S(1)} %pad_add_fusion.ids, ...), custom_call_target="tpu_custom_call" | custom-call | flops 805306368 | bytes 9511948 | tf_op jit(solution)/shard_map/pallas_call | solution.py:62
  60.9 2.8 %collective-permute-start.8 = (bf16[256,256]{1,0:T(8,128)(2,1)S(1)}, bf16[256,256]{1,0:T(8,128)(2,1)S(1)}, u32[]{:S(2)}, u32[]{:S(2)}) collective-permute-start(bf16[256,256]{1,0:T(8,128)(2,1)S(1)} %get-tuple-element.90), channel_id=1, source_target_pairs={{0,2},{1,3},{2,0},{3,1},{4,6},{5,7},{6,4},{7,5},{8,10},{9,11},{10,... | collective-permute-start | bytes 393224 | tf_op jit(solution)/shard_map/ppermute | solution.py:427
  64.5 2.6 %collective-permute-done.8 = bf16[256,256]{1,0:T(8,128)(2,1)S(1)} collective-permute-done((bf16[256,256]{1,0:T(8,128)(2,1)S(1)}, bf16[256,256]{1,0:T(8,128)(2,1)S(1)}, u32[]{:S(2)}, u32[]{:S(2)}) %collective-permute-start.8) | collective-permute-done | bytes 131104 | tf_op jit(solution)/shard_map/ppermute | solution.py:427
  67.1 5.7 %collective-permute-done.9 = bf16[256,256]{1,0:T(8,128)(2,1)S(1)} collective-permute-done((bf16[256,256]{1,0:T(8,128)(2,1)S(1)}, bf16[256,256]{1,0:T(8,128)(2,1)S(1)}, u32[]{:S(2)}, u32[]{:S(2)}) %collective-permute-start.9) | collective-permute-done | bytes 131104 | tf_op jit(solution)/shard_map/ppermute | solution.py:427
  79.1 8.6 %collective-permute-done.11.t2 = bf16[256,256]{1,0:T(8,128)(2,1)S(1)} collective-permute-done((bf16[256,256]{1,0:T(8,128)(2,1)S(1)}, bf16[256,256]{1,0:T(8,128)(2,1)S(1)}, u32[]{:S(2)}, u32[]{:S(2)}) %collective-permute-start.11) | collective-permute-done | bytes 131104 | tf_op jit(solution)/shard_map/ppermute | solution.py:427
  89.1 2.7 %collective-permute-done.15.f3 = bf16[256,2304]{1,0:T(8,128)(2,1)S(1)} collective-permute-done((bf16[256,2304]{1,0:T(8,128)(2,1)}, bf16[256,2304]{1,0:T(8,128)(2,1)S(1)}, u32[]{:S(2)}, u32[]{:S(2)}) %collective-permute-start.15) | collective-permute-done | bytes 1179680 | tf_op jit(solution)/shard_map/ppermute | solution.py:423
  91.7 4.3 %shard_map.249 = (bf16[256,256]{1,0:T(8,128)(2,1)S(1)}, bf16[256,256]{1,0:T(8,128)(2,1)S(1)}, bf16[256,256]{1,0:T(8,128)(2,1)S(1)}, bf16[256,256]{1,0:T(8,128)(2...) custom-call(s32[3]{0:T(128)S(1)} %pad_add_fusion.ids, ...), custom_call_target="tpu_custom_call" | custom-call | flops 2013265920 | bytes 9576460 | tf_op jit(solution)/shard_map/pallas_call | solution.py:62
  98.1 4.0 %collective-permute-done.19 = bf16[1536,256]{1,0:T(8,128)(2,1)S(1)} collective-permute-done((bf16[1536,256]{1,0:T(8,128)(2,1)S(1)}, bf16[1536,256]{1,0:T(8,128)(2,1)S(1)}, u32[]{:S(2)}, u32[]{:S(2)}) %collective-permute-start.19) | collective-permute-done | bytes 786464 | tf_op jit(solution)/shard_map/ppermute | solution.py:423
  104.0 2.4 %collective-permute-start.17 = (bf16[256,256]{1,0:T(8,128)(2,1)S(1)}, bf16[256,256]{1,0:T(8,128)(2,1)S(1)}, u32[]{:S(2)}, u32[]{:S(2)}) collective-permute-start(bf16[256,256]{1,0:T(8,128)(2,1)S(1)} %get-tuple-element.102), channel_id=1, source_target_pairs={{0,2},{1,3},{2,0},{3,1},{4,6},{5,7},{6,4},{7,5},{8,10},{9,11},{10,... | collective-permute-start | bytes 393224 | tf_op jit(solution)/shard_map/ppermute | solution.py:427
  110.0 4.7 %collective-permute-done.18 = bf16[256,256]{1,0:T(8,128)(2,1)S(1)} collective-permute-done((bf16[256,256]{1,0:T(8,128)(2,1)S(1)}, bf16[256,256]{1,0:T(8,128)(2,1)S(1)}, u32[]{:S(2)}, u32[]{:S(2)}) %collective-permute-start.18) | collective-permute-done | bytes 131104 | tf_op jit(solution)/shard_map/ppermute | solution.py:427
  115.8 3.4 %collective-permute-start.22 = (bf16[256,256]{1,0:T(8,128)(2,1)S(1)}, bf16[256,256]{1,0:T(8,128)(2,1)S(1)}, u32[]{:S(2)}, u32[]{:S(2)}) collective-permute-start(bf16[256,256]{1,0:T(8,128)(2,1)S(1)} %add_convert_fusion.8.t0), channel_id=1, source_target_pairs={{0,2},{1,3},{2,0},{3,1},{4,6},{5,7},{6,4},{7,5},{8,10},{9,11},{10,... | collective-permute-start | bytes 393224 | tf_op jit(solution)/shard_map/ppermute | solution.py:427
  120.5 7.8 %collective-permute-done.22.t2 = bf16[256,256]{1,0:T(8,128)(2,1)S(1)} collective-permute-done((bf16[256,256]{1,0:T(8,128)(2,1)S(1)}, bf16[256,256]{1,0:T(8,128)(2,1)S(1)}, u32[]{:S(2)}, u32[]{:S(2)}) %collective-permute-start.22) | collective-permute-done | bytes 131104 | tf_op jit(solution)/shard_map/ppermute | solution.py:427
  130.5 4.5 %shard_map.254 = (bf16[576,256]{1,0:T(8,128)(2,1)S(1)}, bf16[576,256]{1,0:T(8,128)(2,1)S(1)}, bf16[576,256]{1,0:T(8,128)(2,1)S(1)}, bf16[576,256]{1,0:T(8,128)(2,1)S(1)}, bf16[256,1024]{1,0:T(8,128)(2,1)S(1)}) custom-call(s32[3]{0:T(128)S(1)} %pad_add_fusion.ids, bf16[256,512]{1,0:T(8,128)(2,1)S(1)} %get-tuple-element.125.d_o, ...), custom_call_target="tpu_custom_call" | custom-call | flops 872415232 | bytes 9397260 | tf_op jit(solution)/shard_map/pallas_call | solution.py:62
  136.1 2.7 %collective-permute-start.31 = (bf16[512,1024]{1,0:T(8,128)(2,1)S(1)}, bf16[512,1024]{1,0:T(8,128)(2,1)S(1)}, u32[]{:S(2)}, u32[]{:S(2)}) collective-permute-start(bf16[512,1024]{1,0:T(8,128)(2,1)S(1)} %get-tuple-element.143), channel_id=1, source_target_pairs={{0,4},{4,0},{8,12},{12,8},{1,5},{5,1},{9,13},{13,9},{2,6},{6,2},{1... | collective-permute-start | bytes 3145736 | tf_op jit(solution)/shard_map/ppermute | solution.py:423
  146.2 13.9 %collective-permute-done.29 = bf16[512,256]{1,0:T(8,128)(2,1)S(1)} collective-permute-done((bf16[512,256]{1,0:T(8,128)(2,1)S(1)}, bf16[512,256]{1,0:T(8,128)(2,1)S(1)}, u32[]{:S(2)}, u32[]{:S(2)}) %collective-permute-start.29) | collective-permute-done | bytes 262176 | tf_op jit(solution)/shard_map/ppermute | solution.py:423
  163.8 5.5 %collective-permute-done.27.t3 = bf16[576,256]{1,0:T(8,128)(2,1)S(1)} collective-permute-done((bf16[576,256]{1,0:T(8,128)(2,1)S(1)}, bf16[576,256]{1,0:T(8,128)(2,1)S(1)}, u32[]{:S(2)}, u32[]{:S(2)}) %collective-permute-start.27) | collective-permute-done | bytes 294944 | tf_op jit(solution)/shard_map/ppermute | solution.py:427
  170.6 2.7 %collective-permute-done.38 = f32[16,256]{1,0:T(8,128)S(1)} collective-permute-done((f32[16,256]{1,0:T(8,128)S(1)}, f32[16,256]{1,0:T(8,128)S(1)}, u32[]{:S(2)}, u32[]{:S(2)}) %collective-permute-start.38) | collective-permute-done | bytes 16416 | tf_op jit(solution)/shard_map/ppermute | solution.py:423
  173.3 3.0 %collective-permute-start.39 = (f32[16,256]{1,0:T(8,128)S(1)}, f32[16,256]{1,0:T(8,128)S(1)}, u32[]{:S(2)}, u32[]{:S(2)}) collective-permute-start(f32[16,256]{1,0:T(8,128)S(1)} %add.97), channel_id=1, source_target_pairs={{0,4},{4,0},{8,12},{12,8},{1,5},{5,1},{9,13},{13,9},{2,6},{6,2},{1... | collective-permute-start | bytes 49160 | tf_op jit(solution)/shard_map/ppermute | solution.py:423
  176.3 8.9 %collective-permute-done.35 = bf16[512,256]{1,0:T(8,128)(2,1)S(1)} collective-permute-done((bf16[512,256]{1,0:T(8,128)(2,1)S(1)}, bf16[512,256]{1,0:T(8,128)(2,1)S(1)}, u32[]{:S(2)}, u32[]{:S(2)}) %collective-permute-start.35) | collective-permute-done | bytes 262176 | tf_op jit(solution)/shard_map/ppermute | solution.py:481
  192.8 4.7 %collective-permute-done.40 = f32[16,256]{1,0:T(8,128)S(1)} collective-permute-done((f32[16,256]{1,0:T(8,128)S(1)}, f32[16,256]{1,0:T(8,128)S(1)}, u32[]{:S(2)}, u32[]{:S(2)}) %collective-permute-start.40) | collective-permute-done | bytes 16416 | tf_op jit(solution)/shard_map/ppermute | solution.py:481
  198.5 4.6 %collective-permute-done.33 = bf16[512,256]{1,0:T(8,128)(2,1)S(1)} collective-permute-done((bf16[512,256]{1,0:T(8,128)(2,1)S(1)}, bf16[512,256]{1,0:T(8,128)(2,1)S(1)}, u32[]{:S(2)}, u32[]{:S(2)}) %collective-permute-start.33) | collective-permute-done | bytes 262176 | tf_op jit(solution)/shard_map/ppermute | solution.py:441
  (138 shorter events, 72.4 us)
Async XLA Ops:
  7.9 32.8 %collective-permute-start.4 = (bf16[272,1536]{1,0:T(8,128)(2,1)S(1)}, bf16[272,1536]{1,0:T(8,128)(2,1)S(1)}, u32[]{:S(2)}, u32[]{:S(2)}) collective-permute-start(bf16[272,1536]{1,0:T(8,128)(2,1)S(1)} %get-tuple-element.87.q0.w0), channel_id=1, source_target_pairs={{0,8},{4,12},{8,0},{12,4},{1,9},{5,13},{9,1},{13,5},{2,10},{6,14},... | collective-permute-start | bytes 2506760 | tf_op jit(solution)/shard_map/ppermute | solution.py:423
  10.1 11.3 %collective-permute-start.3 = (bf16[512,256]{1,0:T(8,128)(2,1)S(1)}, bf16[512,256]{1,0:T(8,128)(2,1)S(1)}, u32[]{:S(2)}, u32[]{:S(2)}) collective-permute-start(bf16[512,256]{1,0:T(8,128)(2,1)S(1)} %get-tuple-element.86), channel_id=1, source_target_pairs={{0,3},{1,7},{2,11},{3,15},{4,2},{5,6},{6,10},{7,14},{8,1},{9,5},{1... | collective-permute-start | bytes 786440 | tf_op jit(solution)/shard_map/ppermute | solution.py:432
  13.2 27.5 %collective-permute-start.2 = (bf16[512,256]{1,0:T(8,128)(2,1)S(1)}, bf16[512,256]{1,0:T(8,128)(2,1)S(1)}, u32[]{:S(2)}, u32[]{:S(2)}) collective-permute-start(bf16[512,256]{1,0:T(8,128)(2,1)S(1)} %get-tuple-element.86), channel_id=1, source_target_pairs={{0,2},{1,6},{2,10},{3,14},{4,3},{5,7},{6,11},{7,15},{8,0},{9,4},{1... | collective-permute-start | bytes 786440 | tf_op jit(solution)/shard_map/ppermute | solution.py:432
  14.3 27.2 %collective-permute-start.1 = (bf16[512,256]{1,0:T(8,128)(2,1)S(1)}, bf16[512,256]{1,0:T(8,128)(2,1)S(1)}, u32[]{:S(2)}, u32[]{:S(2)}) collective-permute-start(bf16[512,256]{1,0:T(8,128)(2,1)S(1)} %get-tuple-element.86), channel_id=1, source_target_pairs={{0,1},{1,5},{2,9},{3,13},{4,0},{5,4},{6,8},{7,12},{8,3},{9,7},{10,... | collective-permute-start | bytes 786440 | tf_op jit(solution)/shard_map/ppermute | solution.py:432
  15.1 27.0 %collective-permute-start = (bf16[512,256]{1,0:T(8,128)(2,1)S(1)}, bf16[512,256]{1,0:T(8,128)(2,1)S(1)}, u32[]{:S(2)}, u32[]{:S(2)}) collective-permute-start(bf16[512,256]{1,0:T(8,128)(2,1)S(1)} %get-tuple-element.86), channel_id=1, source_target_pairs={{0,0},{1,4},{2,8},{3,12},{4,1},{5,5},{6,9},{7,13},{8,2},{9,6},{10,... | collective-permute-start | bytes 786440 | tf_op jit(solution)/shard_map/ppermute | solution.py:432
  22.1 26.7 %collective-permute-start.5 = (bf16[272,1536]{1,0:T(8,128)(2,1)S(1)}, bf16[272,1536]{1,0:T(8,128)(2,1)S(1)}, u32[]{:S(2)}, u32[]{:S(2)}) collective-permute-start(bf16[272,1536]{1,0:T(8,128)(2,1)S(1)} %get-tuple-element.87.q0.w0), channel_id=1, source_target_pairs={{0,4},{4,0},{8,12},{12,8},{1,5},{5,1},{9,13},{13,9},{2,6},{6,2},{1... | collective-permute-start | bytes 2506760 | tf_op jit(solution)/shard_map/ppermute | solution.py:423
  47.0 40.6 %collective-permute-start.13 = (bf16[256,2304]{1,0:T(8,128)(2,1)}, bf16[256,2304]{1,0:T(8,128)(2,1)}, u32[]{:S(2)}, u32[]{:S(2)}) collective-permute-start(bf16[256,2304]{1,0:T(8,128)(2,1)} %shard_map.248.f0), channel_id=1, source_target_pairs={{0,8},{4,12},{8,0},{12,4},{1,9},{5,13},{9,1},{13,5},{2,10},{6,14},... | collective-permute-start | bytes 3538952 | tf_op jit(solution)/shard_map/ppermute | solution.py:423
  75.0 12.6 %collective-permute-start.11 = (bf16[256,256]{1,0:T(8,128)(2,1)S(1)}, bf16[256,256]{1,0:T(8,128)(2,1)S(1)}, u32[]{:S(2)}, u32[]{:S(2)}) collective-permute-start(bf16[256,256]{1,0:T(8,128)(2,1)S(1)} %add_convert_fusion.9.t0), channel_id=1, source_target_pairs={{0,2},{1,3},{2,0},{3,1},{4,6},{5,7},{6,4},{7,5},{8,10},{9,11},{10,... | collective-permute-start | bytes 393224 | tf_op jit(solution)/shard_map/ppermute | solution.py:427
  77.2 10.4 %collective-permute-start.10 = (bf16[256,256]{1,0:T(8,128)(2,1)S(1)}, bf16[256,256]{1,0:T(8,128)(2,1)S(1)}, u32[]{:S(2)}, u32[]{:S(2)}) collective-permute-start(bf16[256,256]{1,0:T(8,128)(2,1)S(1)} %add_convert_fusion.9.t0), channel_id=1, source_target_pairs={{0,1},{1,0},{2,3},{3,2},{4,5},{5,4},{6,7},{7,6},{8,9},{9,8},{10,11... | collective-permute-start | bytes 393224 | tf_op jit(solution)/shard_map/ppermute | solution.py:427
  77.3 11.7 %collective-permute-start.14 = (bf16[256,2304]{1,0:T(8,128)(2,1)}, bf16[256,2304]{1,0:T(8,128)(2,1)S(1)}, u32[]{:S(2)}, u32[]{:S(2)}) collective-permute-start(bf16[256,2304]{1,0:T(8,128)(2,1)} %shard_map.248.f0), channel_id=1, source_target_pairs={{0,4},{4,0},{8,12},{12,8},{1,5},{5,1},{9,13},{13,9},{2,6},{6,2},{1... | collective-permute-start | bytes 3538952 | tf_op jit(solution)/shard_map/ppermute | solution.py:423
  102.2 17.0 %collective-permute-start.24 = (bf16[768,256]{1,0:T(8,128)(2,1)S(1)}, bf16[768,256]{1,0:T(8,128)(2,1)S(1)}, u32[]{:S(2)}, u32[]{:S(2)}) collective-permute-start(bf16[768,256]{1,0:T(8,128)(2,1)S(1)} %add_convert_fusion.5), channel_id=1, source_target_pairs={{0,8},{4,12},{8,0},{12,4},{1,9},{5,13},{9,1},{13,5},{2,10},{6,14},... | collective-permute-start | bytes 1179656 | tf_op jit(solution)/shard_map/ppermute | solution.py:423
  102.5 32.5 %collective-permute-start.30 = (bf16[256,1536]{1,0:T(8,128)(2,1)S(1)}, bf16[256,1536]{1,0:T(8,128)(2,1)S(1)}, u32[]{:S(2)}, u32[]{:S(2)}) collective-permute-start(bf16[256,1536]{1,0:T(8,128)(2,1)S(1)} %add_convert_fusion.1), channel_id=1, source_target_pairs={{0,8},{4,12},{8,0},{12,4},{1,9},{5,13},{9,1},{13,5},{2,10},{6,14},... | collective-permute-start | bytes 2359304 | tf_op jit(solution)/shard_map/ppermute | solution.py:423
  115.8 12.6 %collective-permute-start.22 = (bf16[256,256]{1,0:T(8,128)(2,1)S(1)}, bf16[256,256]{1,0:T(8,128)(2,1)S(1)}, u32[]{:S(2)}, u32[]{:S(2)}) collective-permute-start(bf16[256,256]{1,0:T(8,128)(2,1)S(1)} %add_convert_fusion.8.t0), channel_id=1, source_target_pairs={{0,2},{1,3},{2,0},{3,1},{4,6},{5,7},{6,4},{7,5},{8,10},{9,11},{10,... | collective-permute-start | bytes 393224 | tf_op jit(solution)/shard_map/ppermute | solution.py:427
  119.2 9.2 %collective-permute-start.21 = (bf16[256,256]{1,0:T(8,128)(2,1)S(1)}, bf16[256,256]{1,0:T(8,128)(2,1)S(1)}, u32[]{:S(2)}, u32[]{:S(2)}) collective-permute-start(bf16[256,256]{1,0:T(8,128)(2,1)S(1)} %add_convert_fusion.8.t0), channel_id=1, source_target_pairs={{0,1},{1,0},{2,3},{3,2},{4,5},{5,4},{6,7},{7,6},{8,9},{9,8},{10,11... | collective-permute-start | bytes 393224 | tf_op jit(solution)/shard_map/ppermute | solution.py:427
  141.3 22.0 %collective-permute-start.32 = (bf16[256,1024]{1,0:T(8,128)(2,1)S(1)}, bf16[256,1024]{1,0:T(8,128)(2,1)S(1)}, u32[]{:S(2)}, u32[]{:S(2)}) collective-permute-start(bf16[256,1024]{1,0:T(8,128)(2,1)S(1)} %add_convert_fusion.3), channel_id=1, source_target_pairs={{0,8},{4,12},{8,0},{12,4},{1,9},{5,13},{9,1},{13,5},{2,10},{6,14},... | collective-permute-start | bytes 1572872 | tf_op jit(solution)/shard_map/ppermute | solution.py:423
  141.9 18.2 %collective-permute-start.29 = (bf16[512,256]{1,0:T(8,128)(2,1)S(1)}, bf16[512,256]{1,0:T(8,128)(2,1)S(1)}, u32[]{:S(2)}, u32[]{:S(2)}) collective-permute-start(bf16[512,256]{1,0:T(8,128)(2,1)S(1)} %add_convert_fusion.7), channel_id=1, source_target_pairs={{0,8},{4,12},{8,0},{12,4},{1,9},{5,13},{9,1},{13,5},{2,10},{6,14},... | collective-permute-start | bytes 786440 | tf_op jit(solution)/shard_map/ppermute | solution.py:423
  143.0 19.0 %collective-permute-start.25 = (bf16[576,256]{1,0:T(8,128)(2,1)S(1)}, bf16[576,256]{1,0:T(8,128)(2,1)S(1)}, u32[]{:S(2)}, u32[]{:S(2)}) collective-permute-start(bf16[576,256]{1,0:T(8,128)(2,1)S(1)} %get-tuple-element.135), channel_id=1, source_target_pairs={{0,1},{1,0},{2,3},{3,2},{4,5},{5,4},{6,7},{7,6},{8,9},{9,8},{10,11... | collective-permute-start | bytes 884744 | tf_op jit(solution)/shard_map/ppermute | solution.py:427
  143.0 46.6 %collective-permute-start.37 = (bf16[768,256]{1,0:T(8,128)(2,1)}, bf16[768,256]{1,0:T(8,128)(2,1)S(1)}, u32[]{:S(2)}, u32[]{:S(2)}) collective-permute-start(bf16[768,256]{1,0:T(8,128)(2,1)} %add_convert_fusion.4), channel_id=1, source_target_pairs={{0,16},{16,0},{1,17},{17,1},{2,18},{18,2},{3,19},{19,3},{4,20},{20... | collective-permute-start | bytes 1179656 | tf_op jit(solution)/shard_map/ppermute | solution.py:481
  144.2 19.7 %collective-permute-start.26 = (bf16[576,256]{1,0:T(8,128)(2,1)S(1)}, bf16[576,256]{1,0:T(8,128)(2,1)S(1)}, u32[]{:S(2)}, u32[]{:S(2)}) collective-permute-start(bf16[576,256]{1,0:T(8,128)(2,1)S(1)} %get-tuple-element.136), channel_id=1, source_target_pairs={{0,2},{1,3},{2,0},{3,1},{4,6},{5,7},{6,4},{7,5},{8,10},{9,11},{10,... | collective-permute-start | bytes 884744 | tf_op jit(solution)/shard_map/ppermute | solution.py:427
  162.0 29.5 %collective-permute-start.36 = (bf16[256,1536]{1,0:T(8,128)(2,1)S(1)}, bf16[256,1536]{1,0:T(8,128)(2,1)S(1)}, u32[]{:S(2)}, u32[]{:S(2)}) collective-permute-start(bf16[256,1536]{1,0:T(8,128)(2,1)S(1)} %add_convert_fusion.own), channel_id=1, source_target_pairs={{0,16},{16,0},{1,17},{17,1},{2,18},{18,2},{3,19},{19,3},{4,20},{20... | collective-permute-start | bytes 2359304 | tf_op jit(solution)/shard_map/ppermute | solution.py:481
  163.3 22.0 %collective-permute-start.35 = (bf16[512,256]{1,0:T(8,128)(2,1)S(1)}, bf16[512,256]{1,0:T(8,128)(2,1)S(1)}, u32[]{:S(2)}, u32[]{:S(2)}) collective-permute-start(bf16[512,256]{1,0:T(8,128)(2,1)S(1)} %add_convert_fusion.6), channel_id=1, source_target_pairs={{0,16},{16,0},{1,17},{17,1},{2,18},{18,2},{3,19},{19,3},{4,20},{20... | collective-permute-start | bytes 786440 | tf_op jit(solution)/shard_map/ppermute | solution.py:481
  173.3 15.9 %collective-permute-start.39 = (f32[16,256]{1,0:T(8,128)S(1)}, f32[16,256]{1,0:T(8,128)S(1)}, u32[]{:S(2)}, u32[]{:S(2)}) collective-permute-start(f32[16,256]{1,0:T(8,128)S(1)} %add.97), channel_id=1, source_target_pairs={{0,4},{4,0},{8,12},{12,8},{1,5},{5,1},{9,13},{13,9},{2,6},{6,2},{1... | collective-permute-start | bytes 49160 | tf_op jit(solution)/shard_map/ppermute | solution.py:423
  186.1 17.9 %collective-permute-start.34 = (bf16[256,1024]{1,0:T(8,128)(2,1)S(1)}, bf16[256,1024]{1,0:T(8,128)(2,1)S(1)}, u32[]{:S(2)}, u32[]{:S(2)}) collective-permute-start(bf16[256,1024]{1,0:T(8,128)(2,1)S(1)} %add_convert_fusion.2.own), channel_id=1, source_target_pairs={{0,16},{16,0},{1,17},{17,1},{2,18},{18,2},{3,19},{19,3},{4,20},{20... | collective-permute-start | bytes 1572872 | tf_op jit(solution)/shard_map/ppermute | solution.py:481
  187.3 15.8 %collective-permute-start.33 = (bf16[512,256]{1,0:T(8,128)(2,1)S(1)}, bf16[512,256]{1,0:T(8,128)(2,1)S(1)}, u32[]{:S(2)}, u32[]{:S(2)}) collective-permute-start(bf16[512,256]{1,0:T(8,128)(2,1)S(1)} %get-tuple-element.150), channel_id=1, source_target_pairs={{0,0},{1,8},{2,4},{3,12},{4,5},{5,13},{6,1},{7,9},{8,10},{9,2},{10... | collective-permute-start | bytes 786440 | tf_op jit(solution)/shard_map/ppermute | solution.py:441
  (41 other events, 245.1 us)

commit v3 on v2

--- a/solution.py
+++ b/solution.py
@@ -32,10 +32,7 @@
     )
     angles = places[:, None] * freqs[None, :].astype(np.float32)
     cos, sin = np.cos(angles), np.sin(angles)
-    return (
-        np.concatenate([cos, cos], 1).astype(np.float32),
-        np.concatenate([-sin, sin], 1).astype(np.float32),
-    )
+    return np.concatenate([cos, cos, -sin, sin], 1).astype(np.float32)
 
 
 def dot(left, right):
@@ -55,9 +52,13 @@
     in_specs = [
         pl.BlockSpec(memory_space=pltpu.HBM) if n in anywhere else vm for n in range(len(args))
     ]
+    args = [
+        pltpu.with_memory_space_constraint(a, pltpu.HBM) if n in anywhere else a
+        for n, a in enumerate(args)
+    ]
     if smem is not None:
         in_specs = [pl.BlockSpec(memory_space=pltpu.SMEM)] + in_specs
-        args = (smem,) + tuple(args)
+        args = [smem] + args
     moved = sum(int(np.prod(a.shape)) * a.dtype.itemsize for a in list(args) + list(outs))
     return pl.pallas_call(
         body,
@@ -88,7 +89,7 @@
     return copies
 
 
-def pack_attn(wq, wk, wv, wp, x, dy, ga, gf, out, both, wide, sems):
+def pack_attn(wq, wk, wv, wp, x, dy, ga, gf, out, both, wide, gain, sems):
     nq, nk = wq.shape[1], wk.shape[1]
     pairs = [
         (wq, out.at[0:BLK, 0:nq]),
@@ -96,20 +97,22 @@
         (wv, out.at[0:BLK, nq + nk : nq + 2 * nk]),
         (x, both.at[0:BLK, :]),
         (dy, wide),
+        (ga, gain.at[0:1, :]),
+        (gf, gain.at[8:9, :]),
     ]
     for i in range(nq // BLK):
         at = nq + 2 * nk + i * BLK
         pairs.append((wp.at[i * BLK : (i + 1) * BLK, :], out.at[0:BLK, at : at + BLK]))
     copies = copy_all(pairs, sems)
-    rows = split3(ga[...]) + split3(gf[...])
+    for item in copies:
+        item.wait()
+    rows = split3(gain[0:1, :]) + split3(gain[8:9, :])
     ids = lax.broadcasted_iota(jnp.int32, (16, BLK), 0)
     extra = jnp.zeros((16, BLK), F32)
     for n, row in enumerate(rows):
         extra = jnp.where(ids == n, jnp.broadcast_to(row, (16, BLK)), extra)
     out[BLK : BLK + 16, :] = jnp.zeros((16, out.shape[1]), BF16)
     out[BLK : BLK + 16, 0:BLK] = extra.astype(BF16)
-    for item in copies:
-        item.wait()
     both[BLK:, :] = wide[...].astype(BF16)
 
 
@@ -136,15 +139,16 @@
 
 
 def attn_forward(
-    ids, x0, x1, x2, x3, q0, q1, q2, q3, cos_r, sin_r, qg_r, kg_r,
+    ids, x0, x1, x2, x3, q0, q1, q2, q3, tables, qg_r, kg_r,
     x_out, dy_out, a_out, gains, o_out, qn_out, kn_out, sc_out, qr_out, kr_out, v_out, pr_out,
-    t0, t1, t2, t3, qkv, place, sems,
+    t0, t1, t2, t3, qkv, place, rot, sems,
 ):
     s1 = ids[2]
     qs = (q0, q1, q2, q3)
     nd = qkv.shape[1]
     pairs = [(ref.at[0:BLK, :], x_out.at[s1 ^ SWAP[k]]) for k, ref in enumerate((x0, x1, x2, x3))]
     pairs += [(ref.at[BLK:, :], dy_out.at[s1 ^ SWAP[k]]) for k, ref in enumerate((x0, x1, x2, x3))]
+    pairs.append((tables, rot))
     for item in copy_all(pairs, sems):
         item.wait()
     total = jnp.zeros((BLK, 1), F32)
@@ -163,7 +167,7 @@
             qkv[...] = part
         else:
             qkv[...] += part
-    cos, sin = cos_r[...], sin_r[...]
+    cos, sin = rot[:, :HEAD_DIMENSION], rot[:, HEAD_DIMENSION:]
     nkv = kn_out.shape[1] // HEAD_DIMENSION
     nq = qn_out.shape[1] // HEAD_DIMENSION
     lanes = lax.broadcasted_iota(jnp.int32, (BLK, HEAD_DIMENSION), 1)
@@ -253,7 +257,8 @@
         slot[...] = place[c ^ k]
 
 
-def down(ids, m, f0, f1, f2, f3, h, place, h_own):
+def down(ids, m, f0, f1, f2, f3, h, send, keep, h_own, place):
+    c = ids[1]
     nf = m.shape[1]
     for p, f in enumerate((f0, f1, f2, f3)):
         acc = jnp.zeros((BLK, BLK), F32)
@@ -261,7 +266,10 @@
             at = slice(2 * nf + i * BLK, 2 * nf + (i + 1) * BLK)
             acc = acc + dot(m[:, i * BLK : (i + 1) * BLK], f[:, at])
         place[p] = acc.astype(BF16)
-    h_own[...] = h[ids[1]]
+    for k, out in enumerate((keep, send)):
+        out[0:BLK, :] = place[c ^ k]
+        out[BLK:, :] = place[c ^ 2 ^ k]
+    h_own[...] = h[c]
 
 
 def ffn_grads(b, d, m, dy, down_s, gu_s, down_k, gu_k):
@@ -323,13 +331,15 @@
 
 
 def attn_backward(
-    ids, d_o, sums_in, y_place, gains, x, q0, q1, q2, q3, o, qn, kn, sc, qr, kr, v, pr, cos_r, sin_r, qg_r, kg_r,
-    s0, s1, s2, s3, d_qkv, part, sums,
+    ids, d_o, sums_in, gains, x, q0, q1, q2, q3, o, qn, kn, sc, qr, kr, v, pr, tables, qg_r, kg_r,
+    msg, sums, d_qkv, rot, sems,
 ):
-    r, c = ids[0], ids[1]
+    r = ids[0]
     nq, nkv = qn.shape[1] // HEAD_DIMENSION, kn.shape[1] // HEAD_DIMENSION
+    (table_copy,) = copy_all([(tables, rot)], sems)
     sums[...] = sums_in[...]
-    cos, sin = cos_r[...], sin_r[...]
+    table_copy.wait()
+    cos, sin = rot[:, :HEAD_DIMENSION], rot[:, HEAD_DIMENSION:]
     factor = HEAD_DIMENSION ** (-0.5)
     q_sum = jnp.zeros((1, HEAD_DIMENSION), F32)
     k_sum = jnp.zeros((1, HEAD_DIMENSION), F32)
@@ -377,35 +387,21 @@
         term = d_a * (x[p].astype(F32) * r_one)
         sums[pl.ds(r ^ SWAP[p], 1), :] = jnp.sum(term, 0, keepdims=True)
         inner = inner + jnp.sum(term * gains[p : p + 1, :], -1, keepdims=True)
-        part[p] = d_a.astype(BF16)
+        msg[p, 0:BLK, :] = d_a.astype(BF16)
     row = jnp.transpose(jnp.broadcast_to(inner, (BLK, 128)))[0:16, :]
     high = row.astype(BF16).astype(F32)
     ids16 = lax.broadcasted_iota(jnp.int32, (16, BLK), 0)
     tail = jnp.where(ids16 == 0, high, jnp.where(ids16 == 1, row - high, 0.0)).astype(BF16)
-    parts = split3(sums[...])
-    for k, slot in enumerate((s0, s1, s2, s3)):
-        slot[0:BLK, :] = part[c ^ k]
-        slot[BLK : 2 * BLK, :] = y_place[c ^ k]
-        slot[2 * BLK : 2 * BLK + 16, :] = tail
-        for i, item in enumerate(parts):
-            slot[2 * BLK + 16 * (i + 1) : 2 * BLK + 16 * (i + 2), :] = item.astype(BF16)
-
-
-def finish(ids, t0, t1, t2, t3, dh_own, h_own, x, gains, out, sums, each):
+    for p in range(ROWS):
+        msg[p, BLK : BLK + 16, :] = tail
+
+
+def finish(ids, got, dh_own, x, gains, h_own, y_mine, y_got, out):
     c = ids[1]
-    refs = (t0, t1, t2, t3)
-    rows = lambda ref, at, n: ref[at : at + n, :].astype(F32)
-    d_a = rows(t0, 0, BLK)
-    y = h_own[...] + rows(t0, BLK, BLK)
-    tail = rows(t0, 2 * BLK, 16)
-    for ref in refs[1:]:
-        d_a = d_a + rows(ref, 0, BLK)
-        y = y + rows(ref, BLK, BLK)
-        tail = tail + rows(ref, 2 * BLK, 16)
-    for k, ref in enumerate(refs):
-        at = 2 * BLK + 16
-        each[c ^ k] = rows(ref, at, 16) + rows(ref, at + 16, 16) + rows(ref, at + 32, 16)
-    sums[...] = (each[0] + each[1]) + (each[2] + each[3])
+    rows = lambda at, n: sum(
+        (got[p, at : at + n, :].astype(F32) for p in range(1, ROWS)), got[0, at : at + n, :].astype(F32)
+    )
+    d_a, tail = rows(0, BLK), rows(BLK, 16)
     row = jnp.broadcast_to(tail[0:1] + tail[1:2], (128, BLK))
     inner = jnp.transpose(row)[:, 0:1] / MODEL_WIDTH
     total = jnp.zeros((BLK, 1), F32)
@@ -416,7 +412,7 @@
     gain = gains[pl.ds(c, 1), :]
     n_one = x[c].astype(F32) * r_one
     out[0:BLK, :] = (dh_own[...] + r_one * (d_a * gain - n_one * inner)).astype(BF16)
-    out[BLK:, :] = y.astype(BF16)
+    out[BLK:, :] = (h_own[...] + y_mine[...] + y_got[...].astype(F32)).astype(BF16)
 
 
 def row_swap(values, bit):
@@ -448,17 +444,24 @@
     return lax.optimization_barrier((values, gate))[0]
 
 
-def core_stage(send, keep):
-    got = row_swap(send, 1)
+def half_stage(send, keep, swap):
+    got = swap(send, 1)
     half = keep.shape[0] // 2
     mine = keep[:half].astype(F32) + got[:half].astype(F32)
     theirs = keep[half:].astype(F32) + got[half:].astype(F32)
     return mine, theirs.astype(BF16)
 
 
-def y_stage(parts):
+def core_stage(send, keep):
+    return half_stage(send, keep, row_swap)
+
+
+def y_stage(parts, gate=None):
     mine, theirs = parts
-    return (mine + row_swap(theirs, 2).astype(F32)).astype(BF16)
+    got = row_swap(theirs, 2)
+    if gate is not None:
+        got = after(got, gate)
+    return (mine + got.astype(F32)).astype(BF16)
 
 
 def last_sum(own, other, *outs):
@@ -482,8 +485,24 @@
     return lax.psum(total, "dp").astype(F32)
 
 
+def both(own, other):
+    return other if other.dtype == F32 else own.astype(F32) + other.astype(F32)
+
+
+def total_sums(n_dp, sums):
+    for swap in (row_swap, col_swap):
+        for bit in (2, 1):
+            sums = sums + swap(sums, bit)
+    other = dp_send(n_dp, sums)
+    return sums + other if n_dp == 2 else other
+
+
 def scatter_col(slots):
     return [slots[0]] + [col_swap(slots[k], k) for k in range(1, ROWS)]
+
+
+def trade_col(blocks):
+    return lax.all_to_all(blocks, "col", split_axis=0, concat_axis=0, tiled=True)
 
 
 def gather_col(block):
@@ -507,8 +526,7 @@
     r, c = lax.axis_index("row"), lax.axis_index("col")
     rc = r ^ c
     ids = jnp.stack([r, c, ((rc & 1) << 1) | (rc >> 1)]).astype(jnp.int32)
-    cos_np, sin_np = rope_tables()
-    cos, sin = jnp.asarray(cos_np), jnp.asarray(sin_np)
+    tables = jnp.asarray(rope_tables())
     qg, kg = query_gain.reshape(1, -1), key_gain.reshape(1, -1)
     blocks = (ROWS, BLK, BLK)
     slot = sds((BLK, BLK), BF16)
@@ -518,7 +536,8 @@
         pack_attn, [sds((BLK + 16, width_qkv + width_q), BF16), sds((2 * BLK, BLK), BF16)],
         (query_weight, key_weight, value_weight, projection_weight, block_input, cotangent,
          attn_gain.reshape(1, -1), ffn_gain.reshape(1, -1)),
-        [pltpu.VMEM((BLK, BLK), F32), sem(5 + width_q // BLK)], 0, None, (0, 1, 2, 3, 4, 5),
+        [pltpu.VMEM((BLK, BLK), F32), pltpu.VMEM((16, BLK), F32), sem(7 + width_q // BLK)],
+        0, None, range(8),
     )
     xs = to_sequence(msg_x)
     q_far = row_swap(msg_q, 2)
@@ -538,9 +557,10 @@
             sds((BLK, width_q), BF16), sds((BLK, width_kv), BF16), sds((BLK, width_kv), BF16),
             sds((nq, BLK, BLK), F32),
         ] + [slot] * ROWS,
-        (*xs, *q_all, cos, sin, qg, kg),
-        [pltpu.VMEM((BLK, width_qkv), F32), pltpu.VMEM(blocks, BF16), sem(2 * ROWS)],
-        2 * BLK * MODEL_WIDTH * (width_qkv + width_q), ids, (0, 1, 2, 3),
+        (*xs, *q_all, tables, qg, kg),
+        [pltpu.VMEM((BLK, width_qkv), F32), pltpu.VMEM(blocks, BF16),
+         pltpu.VMEM((BLK, 2 * HEAD_DIMENSION), F32), sem(2 * ROWS + 1)],
+        2 * BLK * MODEL_WIDTH * (width_qkv + width_q), ids, (0, 1, 2, 3, 8),
     )
     h_slots = scatter_col(slots)
     h_sum = add_all(h_slots).astype(BF16)
@@ -570,55 +590,51 @@
     b_parts = gather_col(b_sum)
     y_down, y_gu = y_stage(mid_down), y_stage(mid_gu)
     x_down, x_gu = dp_send(n_dp, y_down), dp_send(n_dp, y_gu)
-    y_place, h_own = call(
-        down, [sds(blocks, BF16), sds((BLK, BLK), F32)], (m, *f_all, h_full),
-        (), 2 * BLK * MODEL_WIDTH * width_ff, ids,
-    )
+    y_send, y_keep, h_own = call(
+        down, [sds((2 * BLK, BLK), BF16)] * 2 + [sds((BLK, BLK), F32)], (m, *f_all, h_full),
+        [pltpu.VMEM(blocks, BF16)], 2 * BLK * MODEL_WIDTH * width_ff, ids,
+    )
+    y_mine, y_theirs = half_stage(after(y_send, b_parts), y_keep, col_swap)
 
     dh_full, dh_own, d_o, sums = call(
         norm_backward,
         [sds(blocks, BF16), sds((BLK, BLK), F32), sds((BLK, width_q), BF16), sds((16, BLK), F32)],
-        (*after(b_parts, (y_down, y_place)), h_full, dy_full, gains, *q_all),
-        [pltpu.VMEM(blocks, F32)], 2 * BLK * MODEL_WIDTH * width_q, ids,
+        (*after(b_parts, (y_down, y_send)), h_full, dy_full, gains, *q_all),
+        [pltpu.VMEM(blocks, F32)], 20 * BLK * MODEL_WIDTH * width_q, ids,
     )
     proj_s, proj_k = call(
         proj_grads, [sds((2 * width_q, BLK), BF16)] * 2, (o, dh_full), (),
         2 * BLK * MODEL_WIDTH * width_q,
     )
-    *slots, d_qkv = call(
+    msg_a, sums, d_qkv = call(
         attn_backward,
-        [sds((2 * BLK + 64, BLK), BF16)] * ROWS + [sds((BLK, width_qkv), BF16)],
-        (after(d_o, proj_s), sums, y_place, gains, x_full, *q_all,
-         o, qn, kn, sc, qr, kr, v, pr, cos, sin, qg, kg),
-        [pltpu.VMEM(blocks, BF16), pltpu.VMEM((16, BLK), F32)],
-        2 * BLK * MODEL_WIDTH * width_qkv + 10 * BLK * BLK * width_q, ids,
-    )
-    a_parts = scatter_col(slots)
+        [sds((ROWS, BLK + 16, BLK), BF16), sds((16, BLK), F32), sds((BLK, width_qkv), BF16)],
+        (after(d_o, proj_s), sums, gains, x_full, *q_all,
+         o, qn, kn, sc, qr, kr, v, pr, tables, qg, kg),
+        [pltpu.VMEM((BLK, 2 * HEAD_DIMENSION), F32), sem(1)],
+        10 * (2 * BLK * MODEL_WIDTH * width_qkv + 10 * BLK * BLK * width_q), ids, (16,),
+    )
+    mid_proj = core_stage(proj_s, proj_k)
     qkv_s, qkv_k = call(
         qkv_grads, [sds((2 * BLK, width_qkv), BF16)] * 2,
-        (a_full, after(d_qkv, y_gu)), (), 2 * BLK * MODEL_WIDTH * width_qkv,
-    )
-    mid_proj = core_stage(proj_s, proj_k)
+        (a_full, after(d_qkv, (x_down, mid_proj, y_gu))), (),
+        40 * BLK * MODEL_WIDTH * width_qkv,
+    )
     mid_qkv = core_stage(qkv_s, qkv_k)
-    y_proj, y_qkv = y_stage(mid_proj), y_stage(mid_qkv)
-    msg_o, sums = call(
-        finish, [sds((2 * BLK, BLK), BF16), sds((16, BLK), F32)],
-        (*after(a_parts, (y_proj, y_qkv)), dh_own, h_own, x_full, gains),
-        [pltpu.VMEM((ROWS, 16, BLK), F32)], 0, ids,
+    a_parts = trade_col(after(msg_a, mid_qkv))
+    y_got = col_swap(y_theirs, 2)
+    sums = total_sums(n_dp, after(sums, mid_qkv))
+    g_down = both(y_down, x_down)
+    y_proj, y_qkv = y_stage(mid_proj), y_stage(mid_qkv, (x_gu, a_parts, y_got, sums, g_down))
+    (msg_o,) = call(
+        finish, [sds((2 * BLK, BLK), BF16)],
+        (after(a_parts, y_qkv), dh_own, x_full, gains, h_own, y_mine, y_got), (), 0, ids,
     )
     msg_o = to_owner(msg_o)
     input_grad = msg_o[0:BLK].astype(F32)
     block_output = msg_o[BLK:].astype(F32)
-    for bit in (2, 1):
-        sums = sums + row_swap(sums, bit)
-    other = dp_send(n_dp, sums)
-    sums = sums + other if n_dp == 2 else other
-
-    def both(own, other):
-        return other if other.dtype == F32 else own.astype(F32) + other.astype(F32)
-
-    y_down, y_gu = after((y_down, y_gu), y_qkv)
-    g_down = both(y_down, x_down)
+
+    y_gu = after(y_gu, y_qkv)
     final = last_sum if n_dp == 2 else last_split
     g_gate, g_up = call(final, [sds((BLK, width_ff), F32)] * 2, (y_gu, x_gu))
     g_proj = both(y_proj, dp_send(n_dp, y_proj))

time: 206 us -> 176 us (0.85)
  waiting for transfers between devices: 84.6 us -> 58.8 us
  local copies, waits for them, and re-layouts: 18.5 us -> 3.93 us
  starting transfers between devices: 68.8 us -> 72.7 us
  other arithmetic: 6 us -> 9.68 us
  Pallas kernels: 26.2 us -> 29.7 us
    ppermute x16, waiting for transfers between devices: 25.8 us -> 3.88 us  [row_swap(): return lax.ppermute(values, 'row', [(i, i ^ bit) for i in range(ROWS)])]
    unnamed x48 -> x42, local copies, waits for them, and re-layouts: 17.4 us -> 2.84 us
    ppermute x5, waiting for transfers between devices: 13.7 us -> 1.74 us  [dp_send(): return lax.ppermute(total, 'dp', [(0, 1), (1, 0)])]
    ppermute x1, waiting for transfers between devices: 4.57 us -> 12.3 us  [to_owner(): lax.ppermute(block, ('row', 'col'), [(r * ROWS + c, (r ^ SWAP[c]) * ROWS...]
    all_to_all x0 -> x1, starting transfers between devices: none -> 3.6 us  [trade_col(): lax.all_to_all(blocks, 'col', split_axis=0, concat_axis=0, tiled=True)]
    pallas_call x13, Pallas kernels: 26.2 us -> 29.7 us  [call(): pl.pallas_call(body, out_shape=[jax.ShapeDtypeStruct(o.shape, o.dtype) fo...]
    convert_element_type x8, other arithmetic: 2.13 us -> 4.68 us  [the longest x4 3.19 us: y_stage(): return (mine + got.astype(F32)).astype(BF16)]
    ppermute x15 -> x16, starting transfers between devices: 20.5 us -> 20.1 us  [col_swap(): return lax.ppermute(values, 'col', [(i, i ^ bit) for i in range(ROWS)])]
  transfers between devices with their start and end apart: 41 -> 43, of which waited for: 19 -> 16; matrix products, arithmetic and copies ran while one was open for 3% -> 5% of each run, Pallas kernels for 9% -> 12%
where the time goes in v3:
time: 176 us
  starting transfers between devices  72.7 us (41%)
  waiting for transfers between devices  58.8 us (33%)
  Pallas kernels  29.7 us (17%)
  other arithmetic  9.68 us (6%)
  local copies, waits for them, and re-layouts  3.93 us (2%)
    ppermute x16, starting transfers between devices, row_swap(): return lax.ppermute(values, 'row', [(i, i ^ bit) for i in range(ROWS)])  37.2 us
    ppermute x16, waiting for transfers between devices, col_swap(): return lax.ppermute(values, 'col', [(i, i ^ bit) for i in range(ROWS)])  36.6 us
    pallas_call x13, Pallas kernels, call(): pl.pallas_call(body, out_shape=[jax.ShapeDtypeStruct(o.shape, o.dtype) fo...  29.7 us
    ppermute x16, starting transfers between devices, col_swap(): return lax.ppermute(values, 'col', [(i, i ^ bit) for i in range(ROWS)])  20.1 us
    ppermute x1, waiting for transfers between devices, to_owner(): lax.ppermute(block, ('row', 'col'), [(r * ROWS + c, (r ^ SWAP[c]) * ROWS...  12.3 us
    ppermute x4, starting transfers between devices, to_sequence(): lax.ppermute(block, ('row', 'col'), [(r * ROWS + c, c * ROWS + (r ^ k)) f...  6.97 us
    ppermute x4, waiting for transfers between devices, to_sequence(): lax.ppermute(block, ('row', 'col'), [(r * ROWS + c, c * ROWS + (r ^ k)) f...  4.29 us
    ppermute x16, waiting for transfers between devices, row_swap(): return lax.ppermute(values, 'row', [(i, i ^ bit) for i in range(ROWS)])  3.88 us
  transfers between devices with their start and end apart: 43, of which 16 were waited for; matrix products, arithmetic and copies ran while one was open for 5% of the time, Pallas kernels for 12%

profile of v3, /device:TPU:1, one launch (start us, length us, event | category | flops | bytes accessed | tf_op | source)
XLA Modules:
  0.0 175.9 jit_solution(10967126860903911802)
XLA Ops:
  4.2 3.1 %collective-permute-start.3 = (bf16[512,256]{1,0:T(8,128)(2,1)S(1)}, bf16[512,256]{1,0:T(8,128)(2,1)S(1)}, u32[]{:S(2)}, u32[]{:S(2)}) collective-permute-start(bf16[512,256]{1,0:T(8,128)(2,1)S(1)} %get-tuple-element.83), channel_id=1, source_target_pairs={{0,3},{1,7},{2,11},{3,15},{4,2},{5,6},{6,10},{7,14},{8,1},{9,5},{1... | collective-permute-start | bytes 786440 | tf_op jit(solution)/shard_map/ppermute | solution.py:428
  11.2 4.3 %collective-permute-done.3.x3 = bf16[512,256]{1,0:T(8,128)(2,1)S(1)} collective-permute-done((bf16[512,256]{1,0:T(8,128)(2,1)S(1)}, bf16[512,256]{1,0:T(8,128)(2,1)S(1)}, u32[]{:S(2)}, u32[]{:S(2)}) %collective-permute-start.3) | collective-permute-done | bytes 262176 | tf_op jit(solution)/shard_map/ppermute | solution.py:428
  15.5 18.7 %collective-permute-start.5 = (bf16[272,1536]{1,0:T(8,128)(2,1)S(1)}, bf16[272,1536]{1,0:T(8,128)(2,1)}, u32[]{:S(2)}, u32[]{:S(2)}) collective-permute-start(bf16[272,1536]{1,0:T(8,128)(2,1)S(1)} %get-tuple-element.84.q0.w0), channel_id=1, source_target_pairs={{0,4},{4,0},{8,12},{12,8},{1,5},{5,1},{9,13},{13,9},{2,6},{6,2},{1... | collective-permute-start | bytes 2506760 | tf_op jit(solution)/shard_map/ppermute | solution.py:419
  36.9 2.4 %collective-permute-start.13 = (bf16[256,2304]{1,0:T(8,128)(2,1)S(1)}, bf16[256,2304]{1,0:T(8,128)(2,1)S(1)}, u32[]{:S(2)}, u32[]{:S(2)}) collective-permute-start(bf16[256,2304]{1,0:T(8,128)(2,1)S(1)} %shard_map.239.f0), channel_id=1, source_target_pairs={{0,8},{4,12},{8,0},{12,4},{1,9},{5,13},{9,1},{13,5},{2,10},{6,14},... | collective-permute-start | bytes 3538952 | tf_op jit(solution)/shard_map/ppermute | solution.py:419
  39.4 6.9 %shard_map.238 = (bf16[4,256,256]{2,1,0:T(8,128)(2,1)S(1)}, bf16[4,256,256]{2,1,0:T(8,128)(2,1)S(1)}, bf16[4,256,256]{2,1,0:T(8,128)(2,1)S(1)}, f32[8,256]{1,0:T...) custom-call(s32[3]{0:T(128)S(1)} %pad_add_fusion.ids, ...), custom_call_target="tpu_custom_call" | custom-call | flops 805306368 | bytes 9511948 | tf_op jit(solution)/shard_map/pallas_call | solution.py:63
  51.2 2.7 %collective-permute-done.8 = bf16[256,256]{1,0:T(8,128)(2,1)S(1)} collective-permute-done((bf16[256,256]{1,0:T(8,128)(2,1)S(1)}, bf16[256,256]{1,0:T(8,128)(2,1)S(1)}, u32[]{:S(2)}, u32[]{:S(2)}) %collective-permute-start.8) | collective-permute-done | bytes 131104 | tf_op jit(solution)/shard_map/ppermute | solution.py:423
  53.9 4.2 %collective-permute-done.9 = bf16[256,256]{1,0:T(8,128)(2,1)S(1)} collective-permute-done((bf16[256,256]{1,0:T(8,128)(2,1)S(1)}, bf16[256,256]{1,0:T(8,128)(2,1)S(1)}, u32[]{:S(2)}, u32[]{:S(2)}) %collective-permute-start.9) | collective-permute-done | bytes 131104 | tf_op jit(solution)/shard_map/ppermute | solution.py:423
  60.1 3.1 %collective-permute-start.11 = (bf16[256,256]{1,0:T(8,128)(2,1)S(1)}, bf16[256,256]{1,0:T(8,128)(2,1)S(1)}, u32[]{:S(2)}, u32[]{:S(2)}) collective-permute-start(bf16[256,256]{1,0:T(8,128)(2,1)S(1)} %add_convert_fusion.10.t0), channel_id=1, source_target_pairs={{0,2},{1,3},{2,0},{3,1},{4,6},{5,7},{6,4},{7,5},{8,10},{9,11},{10,... | collective-permute-start | bytes 393224 | tf_op jit(solution)/shard_map/ppermute | solution.py:423
  63.2 2.5 %collective-permute-start.14 = (bf16[256,2304]{1,0:T(8,128)(2,1)S(1)}, bf16[256,2304]{1,0:T(8,128)(2,1)S(1)}, u32[]{:S(2)}, u32[]{:S(2)}) collective-permute-start(bf16[256,2304]{1,0:T(8,128)(2,1)S(1)} %shard_map.239.f0), channel_id=1, source_target_pairs={{0,4},{4,0},{8,12},{12,8},{1,5},{5,1},{9,13},{13,9},{2,6},{6,2},{1... | collective-permute-start | bytes 3538952 | tf_op jit(solution)/shard_map/ppermute | solution.py:419
  65.7 6.6 %collective-permute-done.11.t2 = bf16[256,256]{1,0:T(8,128)(2,1)S(1)} collective-permute-done((bf16[256,256]{1,0:T(8,128)(2,1)S(1)}, bf16[256,256]{1,0:T(8,128)(2,1)S(1)}, u32[]{:S(2)}, u32[]{:S(2)}) %collective-permute-start.11) | collective-permute-done | bytes 131104 | tf_op jit(solution)/shard_map/ppermute | solution.py:423
  72.2 2.4 %collective-permute-start.15 = (bf16[256,2304]{1,0:T(8,128)(2,1)S(1)}, bf16[256,2304]{1,0:T(8,128)(2,1)S(1)}, u32[]{:S(2)}, u32[]{:S(2)}) collective-permute-start(bf16[256,2304]{1,0:T(8,128)(2,1)S(1)} %collective-permute-done.13.f1), channel_id=1, source_target_pairs={{0,4},{4,0},{8,12},{12,8},{1,5},{5,1},{9,13},{13,9},{2,6},{6,2},{1... | collective-permute-start | bytes 3538952 | tf_op jit(solution)/shard_map/ppermute | solution.py:419
  74.7 2.5 %collective-permute-done.15.f3 = bf16[256,2304]{1,0:T(8,128)(2,1)S(1)} collective-permute-done((bf16[256,2304]{1,0:T(8,128)(2,1)S(1)}, bf16[256,2304]{1,0:T(8,128)(2,1)S(1)}, u32[]{:S(2)}, u32[]{:S(2)}) %collective-permute-start.15) | collective-permute-done | bytes 1179680 | tf_op jit(solution)/shard_map/ppermute | solution.py:419
  77.1 3.2 %shard_map.240 = (bf16[256,256]{1,0:T(8,128)(2,1)S(1)}, bf16[256,256]{1,0:T(8,128)(2,1)S(1)}, bf16[256,256]{1,0:T(8,128)(2,1)S(1)}, bf16[256,256]{1,0:T(8,128)(2...) custom-call(s32[3]{0:T(128)S(1)} %pad_add_fusion.ids, ...), custom_call_target="tpu_custom_call" | custom-call | flops 2013265920 | bytes 9576460 | tf_op jit(solution)/shard_map/pallas_call | solution.py:63
  89.2 4.1 %collective-permute-done.18 = bf16[256,256]{1,0:T(8,128)(2,1)S(1)} collective-permute-done((bf16[256,256]{1,0:T(8,128)(2,1)S(1)}, bf16[256,256]{1,0:T(8,128)(2,1)S(1)}, u32[]{:S(2)}, u32[]{:S(2)}) %collective-permute-start.18) | collective-permute-done | bytes 131104 | tf_op jit(solution)/shard_map/ppermute | solution.py:423
  95.0 3.1 %collective-permute-start.22 = (bf16[256,256]{1,0:T(8,128)(2,1)S(1)}, bf16[256,256]{1,0:T(8,128)(2,1)S(1)}, u32[]{:S(2)}, u32[]{:S(2)}) collective-permute-start(bf16[256,256]{1,0:T(8,128)(2,1)S(1)} %add_convert_fusion.9.t0), channel_id=1, source_target_pairs={{0,2},{1,3},{2,0},{3,1},{4,6},{5,7},{6,4},{7,5},{8,10},{9,11},{10,... | collective-permute-start | bytes 393224 | tf_op jit(solution)/shard_map/ppermute | solution.py:423
  100.3 7.0 %collective-permute-done.22.t2 = bf16[256,256]{1,0:T(8,128)(2,1)S(1)} collective-permute-done((bf16[256,256]{1,0:T(8,128)(2,1)S(1)}, bf16[256,256]{1,0:T(8,128)(2,1)S(1)}, u32[]{:S(2)}, u32[]{:S(2)}) %collective-permute-start.22) | collective-permute-done | bytes 131104 | tf_op jit(solution)/shard_map/ppermute | solution.py:423
  107.2 2.7 %shard_map.243 = (bf16[4,256,256]{2,1,0:T(8,128)(2,1)S(1)}, f32[256,256]{1,0:T(8,128)S(1)}, bf16[256,512]{1,0:T(8,128)(2,1)S(1)}, f32[16,256]{1,0:T(8,128)S(1)}) custom-call(s32[3]{0:T(128)S(1)} %pad_add_fusion.ids, bf16[256,256]{1,0:T(8,128)(2,1)S(1)} %add_convert_fusion.9.t0, bf16[256,256]{1,0:T(8,128)(2,1)S(1)} %collective-permute-done.21.t1, ...), custom_call_target="tpu_custom_call" | custom-call | flops 2684354560 | bytes 6512652 | tf_op jit(solution)/shard_map/pallas_call | solution.py:63
  110.4 2.4 %collective-permute-start.26 = (bf16[1024,256]{1,0:T(8,128)(2,1)S(1)}, bf16[1024,256]{1,0:T(8,128)(2,1)S(1)}, u32[]{:S(2)}, u32[]{:S(2)}) collective-permute-start(bf16[1024,256]{1,0:T(8,128)(2,1)S(1)} %get-tuple-element.121), channel_id=1, source_target_pairs={{0,4},{4,0},{8,12},{12,8},{1,5},{5,1},{9,13},{13,9},{2,6},{6,2},{1... | collective-permute-start | bytes 1572872 | tf_op jit(solution)/shard_map/ppermute | solution.py:419
  112.8 6.6 %shard_map.245 = (bf16[4,272,256]{2,1,0:T(8,128)(2,1)S(1)}, f32[16,256]{1,0:T(8,128)S(1)}, bf16[256,1024]{1,0:T(8,128)(2,1)S(1)}) custom-call(s32[3]{0:T(128)S(1)} %pad_add_fusion.ids, bf16[256,512]{1,0:T(8,128)(2,1)S(1)} %get-tuple-element.122.d_o, f32[16,256]{1,0:T(8,128)S(1)} %get-tuple-element.123.sums_in, f32[8,256]{1,0:T(8,128)S(1)} %get-tuple-element.96.gains, ...), custom_call_target="tpu_custom_call" | custom-call | flops 8724152320 | bytes 8266764 | tf_op jit(solution)/shard_map/pallas_call | solution.py:63
  127.5 3.6 %all-to-all-start = ((bf16[4,272,256]{2,1,0:T(8,128)(2,1)}), bf16[4,272,256]{2,1,0:T(8,128)(2,1)S(1)}, u32[]{:S(2)}, u32[]{:S(2)}) async-start(bf16[4,272,256]{2,1,0:T(8,128)(2,1)} %copy-done), calls=%async_computation | async-start | bytes 1114112 | tf_op jit(solution)/shard_map/all_to_all | solution.py:505
  134.5 2.6 %collective-permute-start.35 = (f32[16,256]{1,0:T(8,128)S(1)}, f32[16,256]{1,0:T(8,128)S(1)}, u32[]{:S(2)}, u32[]{:S(2)}) collective-permute-start(f32[16,256]{1,0:T(8,128)S(1)} %add.107), channel_id=1, source_target_pairs={{0,2},{1,3},{2,0},{3,1},{4,6},{5,7},{6,4},{7,5},{8,10},{9,11},{10,... | collective-permute-start | bytes 49160 | tf_op jit(solution)/shard_map/ppermute | solution.py:423
  139.3 7.3 %collective-permute-done.35 = f32[16,256]{1,0:T(8,128)S(1)} collective-permute-done((f32[16,256]{1,0:T(8,128)S(1)}, f32[16,256]{1,0:T(8,128)S(1)}, u32[]{:S(2)}, u32[]{:S(2)}) %collective-permute-start.35) | collective-permute-done | bytes 16416 | tf_op jit(solution)/shard_map/ppermute | solution.py:423
  152.0 2.2 %collective-permute-done.32.y_got = bf16[256,256]{1,0:T(8,128)(2,1)S(1)} collective-permute-done((bf16[256,256]{1,0:T(8,128)(2,1)S(1)}, bf16[256,256]{1,0:T(8,128)(2,1)S(1)}, u32[]{:S(2)}, u32[]{:S(2)}) %collective-permute-start.32) | collective-permute-done | bytes 131104 | tf_op jit(solution)/shard_map/ppermute | solution.py:423
  161.8 12.3 %collective-permute-done.38 = bf16[512,256]{1,0:T(8,128)(2,1)S(1)} collective-permute-done((bf16[512,256]{1,0:T(8,128)(2,1)S(1)}, bf16[512,256]{1,0:T(8,128)(2,1)S(1)}, u32[]{:S(2)}, u32[]{:S(2)}) %collective-permute-start.38) | collective-permute-done | bytes 262176 | tf_op jit(solution)/shard_map/ppermute | solution.py:437
  (139 shorter events, 58.7 us)
Async XLA Ops:
  2.1 32.1 %collective-permute-start.4 = (bf16[272,1536]{1,0:T(8,128)(2,1)S(1)}, bf16[272,1536]{1,0:T(8,128)(2,1)}, u32[]{:S(2)}, u32[]{:S(2)}) collective-permute-start(bf16[272,1536]{1,0:T(8,128)(2,1)S(1)} %get-tuple-element.84.q0.w0), channel_id=1, source_target_pairs={{0,8},{4,12},{8,0},{12,4},{1,9},{5,13},{9,1},{13,5},{2,10},{6,14},... | collective-permute-start | bytes 2506760 | tf_op jit(solution)/shard_map/ppermute | solution.py:419
  4.2 11.3 %collective-permute-start.3 = (bf16[512,256]{1,0:T(8,128)(2,1)S(1)}, bf16[512,256]{1,0:T(8,128)(2,1)S(1)}, u32[]{:S(2)}, u32[]{:S(2)}) collective-permute-start(bf16[512,256]{1,0:T(8,128)(2,1)S(1)} %get-tuple-element.83), channel_id=1, source_target_pairs={{0,3},{1,7},{2,11},{3,15},{4,2},{5,6},{6,10},{7,14},{8,1},{9,5},{1... | collective-permute-start | bytes 786440 | tf_op jit(solution)/shard_map/ppermute | solution.py:428
  7.4 26.9 %collective-permute-start.2 = (bf16[512,256]{1,0:T(8,128)(2,1)S(1)}, bf16[512,256]{1,0:T(8,128)(2,1)S(1)}, u32[]{:S(2)}, u32[]{:S(2)}) collective-permute-start(bf16[512,256]{1,0:T(8,128)(2,1)S(1)} %get-tuple-element.83), channel_id=1, source_target_pairs={{0,2},{1,6},{2,10},{3,14},{4,3},{5,7},{6,11},{7,15},{8,0},{9,4},{1... | collective-permute-start | bytes 786440 | tf_op jit(solution)/shard_map/ppermute | solution.py:428
  8.4 25.8 %collective-permute-start.1 = (bf16[512,256]{1,0:T(8,128)(2,1)S(1)}, bf16[512,256]{1,0:T(8,128)(2,1)S(1)}, u32[]{:S(2)}, u32[]{:S(2)}) collective-permute-start(bf16[512,256]{1,0:T(8,128)(2,1)S(1)} %get-tuple-element.83), channel_id=1, source_target_pairs={{0,1},{1,5},{2,9},{3,13},{4,0},{5,4},{6,8},{7,12},{8,3},{9,7},{10,... | collective-permute-start | bytes 786440 | tf_op jit(solution)/shard_map/ppermute | solution.py:428
  9.3 26.4 %collective-permute-start = (bf16[512,256]{1,0:T(8,128)(2,1)S(1)}, bf16[512,256]{1,0:T(8,128)(2,1)}, u32[]{:S(2)}, u32[]{:S(2)}) collective-permute-start(bf16[512,256]{1,0:T(8,128)(2,1)S(1)} %get-tuple-element.83), channel_id=1, source_target_pairs={{0,0},{1,4},{2,8},{3,12},{4,1},{5,5},{6,9},{7,13},{8,2},{9,6},{10,... | collective-permute-start | bytes 786440 | tf_op jit(solution)/shard_map/ppermute | solution.py:428
  15.5 23.9 %collective-permute-start.5 = (bf16[272,1536]{1,0:T(8,128)(2,1)S(1)}, bf16[272,1536]{1,0:T(8,128)(2,1)}, u32[]{:S(2)}, u32[]{:S(2)}) collective-permute-start(bf16[272,1536]{1,0:T(8,128)(2,1)S(1)} %get-tuple-element.84.q0.w0), channel_id=1, source_target_pairs={{0,4},{4,0},{8,12},{12,8},{1,5},{5,1},{9,13},{13,9},{2,6},{6,2},{1... | collective-permute-start | bytes 2506760 | tf_op jit(solution)/shard_map/ppermute | solution.py:419
  36.9 35.3 %collective-permute-start.13 = (bf16[256,2304]{1,0:T(8,128)(2,1)S(1)}, bf16[256,2304]{1,0:T(8,128)(2,1)S(1)}, u32[]{:S(2)}, u32[]{:S(2)}) collective-permute-start(bf16[256,2304]{1,0:T(8,128)(2,1)S(1)} %shard_map.239.f0), channel_id=1, source_target_pairs={{0,8},{4,12},{8,0},{12,4},{1,9},{5,13},{9,1},{13,5},{2,10},{6,14},... | collective-permute-start | bytes 3538952 | tf_op jit(solution)/shard_map/ppermute | solution.py:419
  60.1 12.1 %collective-permute-start.11 = (bf16[256,256]{1,0:T(8,128)(2,1)S(1)}, bf16[256,256]{1,0:T(8,128)(2,1)S(1)}, u32[]{:S(2)}, u32[]{:S(2)}) collective-permute-start(bf16[256,256]{1,0:T(8,128)(2,1)S(1)} %add_convert_fusion.10.t0), channel_id=1, source_target_pairs={{0,2},{1,3},{2,0},{3,1},{4,6},{5,7},{6,4},{7,5},{8,10},{9,11},{10,... | collective-permute-start | bytes 393224 | tf_op jit(solution)/shard_map/ppermute | solution.py:423
  63.2 9.0 %collective-permute-start.10 = (bf16[256,256]{1,0:T(8,128)(2,1)S(1)}, bf16[256,256]{1,0:T(8,128)(2,1)S(1)}, u32[]{:S(2)}, u32[]{:S(2)}) collective-permute-start(bf16[256,256]{1,0:T(8,128)(2,1)S(1)} %add_convert_fusion.10.t0), channel_id=1, source_target_pairs={{0,1},{1,0},{2,3},{3,2},{4,5},{5,4},{6,7},{7,6},{8,9},{9,8},{10,11... | collective-permute-start | bytes 393224 | tf_op jit(solution)/shard_map/ppermute | solution.py:423
  63.2 11.5 %collective-permute-start.14 = (bf16[256,2304]{1,0:T(8,128)(2,1)S(1)}, bf16[256,2304]{1,0:T(8,128)(2,1)S(1)}, u32[]{:S(2)}, u32[]{:S(2)}) collective-permute-start(bf16[256,2304]{1,0:T(8,128)(2,1)S(1)} %shard_map.239.f0), channel_id=1, source_target_pairs={{0,4},{4,0},{8,12},{12,8},{1,5},{5,1},{9,13},{13,9},{2,6},{6,2},{1... | collective-permute-start | bytes 3538952 | tf_op jit(solution)/shard_map/ppermute | solution.py:419
  87.9 10.2 %collective-permute-start.24 = (bf16[768,256]{1,0:T(8,128)(2,1)S(1)}, bf16[768,256]{1,0:T(8,128)(2,1)S(1)}, u32[]{:S(2)}, u32[]{:S(2)}) collective-permute-start(bf16[768,256]{1,0:T(8,128)(2,1)S(1)} %add_convert_fusion.5), channel_id=1, source_target_pairs={{0,8},{4,12},{8,0},{12,4},{1,9},{5,13},{9,1},{13,5},{2,10},{6,14},... | collective-permute-start | bytes 1179656 | tf_op jit(solution)/shard_map/ppermute | solution.py:419
  95.0 12.2 %collective-permute-start.22 = (bf16[256,256]{1,0:T(8,128)(2,1)S(1)}, bf16[256,256]{1,0:T(8,128)(2,1)S(1)}, u32[]{:S(2)}, u32[]{:S(2)}) collective-permute-start(bf16[256,256]{1,0:T(8,128)(2,1)S(1)} %add_convert_fusion.9.t0), channel_id=1, source_target_pairs={{0,2},{1,3},{2,0},{3,1},{4,6},{5,7},{6,4},{7,5},{8,10},{9,11},{10,... | collective-permute-start | bytes 393224 | tf_op jit(solution)/shard_map/ppermute | solution.py:423
  98.1 9.1 %collective-permute-start.21 = (bf16[256,256]{1,0:T(8,128)(2,1)S(1)}, bf16[256,256]{1,0:T(8,128)(2,1)S(1)}, u32[]{:S(2)}, u32[]{:S(2)}) collective-permute-start(bf16[256,256]{1,0:T(8,128)(2,1)S(1)} %add_convert_fusion.9.t0), channel_id=1, source_target_pairs={{0,1},{1,0},{2,3},{3,2},{4,5},{5,4},{6,7},{7,6},{8,9},{9,8},{10,11... | collective-permute-start | bytes 393224 | tf_op jit(solution)/shard_map/ppermute | solution.py:423
  98.3 22.3 %collective-permute-start.25 = (bf16[768,256]{1,0:T(8,128)(2,1)S(1)}, bf16[768,256]{1,0:T(8,128)(2,1)S(1)}, u32[]{:S(2)}, u32[]{:S(2)}) collective-permute-start(bf16[768,256]{1,0:T(8,128)(2,1)S(1)} %add_convert_fusion.4), channel_id=1, source_target_pairs={{0,16},{16,0},{1,17},{17,1},{2,18},{18,2},{3,19},{19,3},{4,20},{20... | collective-permute-start | bytes 1179656 | tf_op jit(solution)/shard_map/ppermute | solution.py:484
  99.5 20.7 %collective-permute-start.27 = (bf16[256,1536]{1,0:T(8,128)(2,1)S(1)}, bf16[256,1536]{1,0:T(8,128)(2,1)S(1)}, u32[]{:S(2)}, u32[]{:S(2)}) collective-permute-start(bf16[256,1536]{1,0:T(8,128)(2,1)S(1)} %add_convert_fusion.1), channel_id=1, source_target_pairs={{0,8},{4,12},{8,0},{12,4},{1,9},{5,13},{9,1},{13,5},{2,10},{6,14},... | collective-permute-start | bytes 2359304 | tf_op jit(solution)/shard_map/ppermute | solution.py:419
  121.5 11.0 %collective-permute-start.40 = (bf16[512,256]{1,0:T(8,128)(2,1)S(1)}, bf16[512,256]{1,0:T(8,128)(2,1)}, u32[]{:S(2)}, u32[]{:S(2)}) collective-permute-start(bf16[512,256]{1,0:T(8,128)(2,1)S(1)} %add_convert_fusion.7), channel_id=1, source_target_pairs={{0,8},{4,12},{8,0},{12,4},{1,9},{5,13},{9,1},{13,5},{2,10},{6,14},... | collective-permute-start | bytes 786440 | tf_op jit(solution)/shard_map/ppermute | solution.py:419
  126.3 20.2 %collective-permute-start.31 = (bf16[512,256]{1,0:T(8,128)(2,1)}, bf16[512,256]{1,0:T(8,128)(2,1)}, u32[]{:S(2)}, u32[]{:S(2)}) collective-permute-start(bf16[512,256]{1,0:T(8,128)(2,1)} %get-tuple-element.140), channel_id=1, source_target_pairs={{0,1},{1,0},{2,3},{3,2},{4,5},{5,4},{6,7},{7,6},{8,9},{9,8},{10,11... | collective-permute-start | bytes 786440 | tf_op jit(solution)/shard_map/ppermute | solution.py:423
  126.3 28.5 %collective-permute-start.30 = (bf16[256,1536]{1,0:T(8,128)(2,1)S(1)}, bf16[256,1536]{1,0:T(8,128)(2,1)S(1)}, u32[]{:S(2)}, u32[]{:S(2)}) collective-permute-start(bf16[256,1536]{1,0:T(8,128)(2,1)S(1)} %add_convert_fusion.own), channel_id=1, source_target_pairs={{0,16},{16,0},{1,17},{17,1},{2,18},{18,2},{3,19},{19,3},{4,20},{20... | collective-permute-start | bytes 2359304 | tf_op jit(solution)/shard_map/ppermute | solution.py:484
  127.5 27.3 %all-to-all-start = ((bf16[4,272,256]{2,1,0:T(8,128)(2,1)}), bf16[4,272,256]{2,1,0:T(8,128)(2,1)S(1)}, u32[]{:S(2)}, u32[]{:S(2)}) async-start(bf16[4,272,256]{2,1,0:T(8,128)(2,1)} %copy-done), calls=%async_computation | async-start | bytes 1114112 | tf_op jit(solution)/shard_map/all_to_all | solution.py:505
  133.7 16.4 %collective-permute-start.41 = (bf16[512,256]{1,0:T(8,128)(2,1)S(1)}, bf16[512,256]{1,0:T(8,128)(2,1)S(1)}, u32[]{:S(2)}, u32[]{:S(2)}) collective-permute-start(bf16[512,256]{1,0:T(8,128)(2,1)S(1)} %add_convert_fusion.6), channel_id=1, source_target_pairs={{0,16},{16,0},{1,17},{17,1},{2,18},{18,2},{3,19},{19,3},{4,20},{20... | collective-permute-start | bytes 786440 | tf_op jit(solution)/shard_map/ppermute | solution.py:484
  134.0 20.8 %collective-permute-start.29 = (bf16[256,1024]{1,0:T(8,128)(2,1)}, bf16[256,1024]{1,0:T(8,128)(2,1)}, u32[]{:S(2)}, u32[]{:S(2)}) collective-permute-start(bf16[256,1024]{1,0:T(8,128)(2,1)} %add_convert_fusion.3), channel_id=1, source_target_pairs={{0,8},{4,12},{8,0},{12,4},{1,9},{5,13},{9,1},{13,5},{2,10},{6,14},... | collective-permute-start | bytes 1572872 | tf_op jit(solution)/shard_map/ppermute | solution.py:419
  134.5 12.0 %collective-permute-start.35 = (f32[16,256]{1,0:T(8,128)S(1)}, f32[16,256]{1,0:T(8,128)S(1)}, u32[]{:S(2)}, u32[]{:S(2)}) collective-permute-start(f32[16,256]{1,0:T(8,128)S(1)} %add.107), channel_id=1, source_target_pairs={{0,2},{1,3},{2,0},{3,1},{4,6},{5,7},{6,4},{7,5},{8,10},{9,11},{10,... | collective-permute-start | bytes 49160 | tf_op jit(solution)/shard_map/ppermute | solution.py:423
  156.5 18.5 %collective-permute-start.39 = (bf16[256,1024]{1,0:T(8,128)(2,1)S(1)}, bf16[256,1024]{1,0:T(8,128)(2,1)S(1)}, u32[]{:S(2)}, u32[]{:S(2)}) collective-permute-start(bf16[256,1024]{1,0:T(8,128)(2,1)S(1)} %add_convert_fusion.2.own), channel_id=1, source_target_pairs={{0,16},{16,0},{1,17},{17,1},{2,18},{18,2},{3,19},{19,3},{4,20},{20... | collective-permute-start | bytes 1572872 | tf_op jit(solution)/shard_map/ppermute | solution.py:484
  157.6 16.5 %collective-permute-start.38 = (bf16[512,256]{1,0:T(8,128)(2,1)S(1)}, bf16[512,256]{1,0:T(8,128)(2,1)S(1)}, u32[]{:S(2)}, u32[]{:S(2)}) collective-permute-start(bf16[512,256]{1,0:T(8,128)(2,1)S(1)} %shard_map.247), channel_id=1, source_target_pairs={{0,0},{1,8},{2,4},{3,12},{4,5},{5,13},{6,1},{7,9},{8,10},{9,2},{10... | collective-permute-start | bytes 786440 | tf_op jit(solution)/shard_map/ppermute | solution.py:437
  (40 other events, 334.2 us)

commit v4 on v3

--- a/solution.py
+++ b/solution.py
@@ -618,10 +618,10 @@
     qkv_s, qkv_k = call(
         qkv_grads, [sds((2 * BLK, width_qkv), BF16)] * 2,
         (a_full, after(d_qkv, (x_down, mid_proj, y_gu))), (),
-        40 * BLK * MODEL_WIDTH * width_qkv,
+        2 * BLK * MODEL_WIDTH * width_qkv,
     )
     mid_qkv = core_stage(qkv_s, qkv_k)
-    a_parts = trade_col(after(msg_a, mid_qkv))
+    a_parts = trade_col(after(msg_a, qkv_s))
     y_got = col_swap(y_theirs, 2)
     sums = total_sums(n_dp, after(sums, mid_qkv))
     g_down = both(y_down, x_down)

time: 176 us -> 176 us (level)
  no operation moved by 1% of the time
where the time goes in v4:
time: 176 us
  starting transfers between devices  72.7 us (41%)
  waiting for transfers between devices  58.8 us (33%)
  Pallas kernels  29.7 us (17%)
  other arithmetic  9.68 us (6%)
  local copies, waits for them, and re-layouts  3.92 us (2%)
    ppermute x16, starting transfers between devices, row_swap(): return lax.ppermute(values, 'row', [(i, i ^ bit) for i in range(ROWS)])  37.2 us
    ppermute x16, waiting for transfers between devices, col_swap(): return lax.ppermute(values, 'col', [(i, i ^ bit) for i in range(ROWS)])  36.6 us
    pallas_call x13, Pallas kernels, call(): pl.pallas_call(body, out_shape=[jax.ShapeDtypeStruct(o.shape, o.dtype) fo...  29.7 us
    ppermute x16, starting transfers between devices, col_swap(): return lax.ppermute(values, 'col', [(i, i ^ bit) for i in range(ROWS)])  20.1 us
    ppermute x1, waiting for transfers between devices, to_owner(): lax.ppermute(block, ('row', 'col'), [(r * ROWS + c, (r ^ SWAP[c]) * ROWS...  12.3 us
    ppermute x4, starting transfers between devices, to_sequence(): lax.ppermute(block, ('row', 'col'), [(r * ROWS + c, c * ROWS + (r ^ k)) f...  6.97 us
    ppermute x4, waiting for transfers between devices, to_sequence(): lax.ppermute(block, ('row', 'col'), [(r * ROWS + c, c * ROWS + (r ^ k)) f...  4.29 us
    ppermute x16, waiting for transfers between devices, row_swap(): return lax.ppermute(values, 'row', [(i, i ^ bit) for i in range(ROWS)])  3.88 us
  transfers between devices with their start and end apart: 43, of which 16 were waited for; matrix products, arithmetic and copies ran while one was open for 5% of the time, Pallas kernels for 12%

profile of v4, /device:TPU:1, one launch (start us, length us, event | category | flops | bytes accessed | tf_op | source)
XLA Modules:
  0.0 175.9 jit_solution(14479493879626204611)
XLA Ops:
  4.2 3.1 %collective-permute-start.3 = (bf16[512,256]{1,0:T(8,128)(2,1)S(1)}, bf16[512,256]{1,0:T(8,128)(2,1)S(1)}, u32[]{:S(2)}, u32[]{:S(2)}) collective-permute-start(bf16[512,256]{1,0:T(8,128)(2,1)S(1)} %get-tuple-element.83), channel_id=1, source_target_pairs={{0,3},{1,7},{2,11},{3,15},{4,2},{5,6},{6,10},{7,14},{8,1},{9,5},{1... | collective-permute-start | bytes 786440 | tf_op jit(solution)/shard_map/ppermute | solution.py:428
  11.2 4.3 %collective-permute-done.3.x3 = bf16[512,256]{1,0:T(8,128)(2,1)S(1)} collective-permute-done((bf16[512,256]{1,0:T(8,128)(2,1)S(1)}, bf16[512,256]{1,0:T(8,128)(2,1)S(1)}, u32[]{:S(2)}, u32[]{:S(2)}) %collective-permute-start.3) | collective-permute-done | bytes 262176 | tf_op jit(solution)/shard_map/ppermute | solution.py:428
  15.5 18.7 %collective-permute-start.5 = (bf16[272,1536]{1,0:T(8,128)(2,1)S(1)}, bf16[272,1536]{1,0:T(8,128)(2,1)}, u32[]{:S(2)}, u32[]{:S(2)}) collective-permute-start(bf16[272,1536]{1,0:T(8,128)(2,1)S(1)} %get-tuple-element.84.q0.w0), channel_id=1, source_target_pairs={{0,4},{4,0},{8,12},{12,8},{1,5},{5,1},{9,13},{13,9},{2,6},{6,2},{1... | collective-permute-start | bytes 2506760 | tf_op jit(solution)/shard_map/ppermute | solution.py:419
  36.9 2.4 %collective-permute-start.13 = (bf16[256,2304]{1,0:T(8,128)(2,1)S(1)}, bf16[256,2304]{1,0:T(8,128)(2,1)S(1)}, u32[]{:S(2)}, u32[]{:S(2)}) collective-permute-start(bf16[256,2304]{1,0:T(8,128)(2,1)S(1)} %shard_map.239.f0), channel_id=1, source_target_pairs={{0,8},{4,12},{8,0},{12,4},{1,9},{5,13},{9,1},{13,5},{2,10},{6,14},... | collective-permute-start | bytes 3538952 | tf_op jit(solution)/shard_map/ppermute | solution.py:419
  39.4 6.9 %shard_map.238 = (bf16[4,256,256]{2,1,0:T(8,128)(2,1)S(1)}, bf16[4,256,256]{2,1,0:T(8,128)(2,1)S(1)}, bf16[4,256,256]{2,1,0:T(8,128)(2,1)S(1)}, f32[8,256]{1,0:T...) custom-call(s32[3]{0:T(128)S(1)} %pad_add_fusion.ids, ...), custom_call_target="tpu_custom_call" | custom-call | flops 805306368 | bytes 9511948 | tf_op jit(solution)/shard_map/pallas_call | solution.py:63
  51.2 2.7 %collective-permute-done.8 = bf16[256,256]{1,0:T(8,128)(2,1)S(1)} collective-permute-done((bf16[256,256]{1,0:T(8,128)(2,1)S(1)}, bf16[256,256]{1,0:T(8,128)(2,1)S(1)}, u32[]{:S(2)}, u32[]{:S(2)}) %collective-permute-start.8) | collective-permute-done | bytes 131104 | tf_op jit(solution)/shard_map/ppermute | solution.py:423
  53.9 4.2 %collective-permute-done.9 = bf16[256,256]{1,0:T(8,128)(2,1)S(1)} collective-permute-done((bf16[256,256]{1,0:T(8,128)(2,1)S(1)}, bf16[256,256]{1,0:T(8,128)(2,1)S(1)}, u32[]{:S(2)}, u32[]{:S(2)}) %collective-permute-start.9) | collective-permute-done | bytes 131104 | tf_op jit(solution)/shard_map/ppermute | solution.py:423
  60.1 3.1 %collective-permute-start.11 = (bf16[256,256]{1,0:T(8,128)(2,1)S(1)}, bf16[256,256]{1,0:T(8,128)(2,1)S(1)}, u32[]{:S(2)}, u32[]{:S(2)}) collective-permute-start(bf16[256,256]{1,0:T(8,128)(2,1)S(1)} %add_convert_fusion.10.t0), channel_id=1, source_target_pairs={{0,2},{1,3},{2,0},{3,1},{4,6},{5,7},{6,4},{7,5},{8,10},{9,11},{10,... | collective-permute-start | bytes 393224 | tf_op jit(solution)/shard_map/ppermute | solution.py:423
  63.2 2.5 %collective-permute-start.14 = (bf16[256,2304]{1,0:T(8,128)(2,1)S(1)}, bf16[256,2304]{1,0:T(8,128)(2,1)S(1)}, u32[]{:S(2)}, u32[]{:S(2)}) collective-permute-start(bf16[256,2304]{1,0:T(8,128)(2,1)S(1)} %shard_map.239.f0), channel_id=1, source_target_pairs={{0,4},{4,0},{8,12},{12,8},{1,5},{5,1},{9,13},{13,9},{2,6},{6,2},{1... | collective-permute-start | bytes 3538952 | tf_op jit(solution)/shard_map/ppermute | solution.py:419
  65.7 6.6 %collective-permute-done.11.t2 = bf16[256,256]{1,0:T(8,128)(2,1)S(1)} collective-permute-done((bf16[256,256]{1,0:T(8,128)(2,1)S(1)}, bf16[256,256]{1,0:T(8,128)(2,1)S(1)}, u32[]{:S(2)}, u32[]{:S(2)}) %collective-permute-start.11) | collective-permute-done | bytes 131104 | tf_op jit(solution)/shard_map/ppermute | solution.py:423
  72.2 2.4 %collective-permute-start.15 = (bf16[256,2304]{1,0:T(8,128)(2,1)S(1)}, bf16[256,2304]{1,0:T(8,128)(2,1)S(1)}, u32[]{:S(2)}, u32[]{:S(2)}) collective-permute-start(bf16[256,2304]{1,0:T(8,128)(2,1)S(1)} %collective-permute-done.13.f1), channel_id=1, source_target_pairs={{0,4},{4,0},{8,12},{12,8},{1,5},{5,1},{9,13},{13,9},{2,6},{6,2},{1... | collective-permute-start | bytes 3538952 | tf_op jit(solution)/shard_map/ppermute | solution.py:419
  74.7 2.5 %collective-permute-done.15.f3 = bf16[256,2304]{1,0:T(8,128)(2,1)S(1)} collective-permute-done((bf16[256,2304]{1,0:T(8,128)(2,1)S(1)}, bf16[256,2304]{1,0:T(8,128)(2,1)S(1)}, u32[]{:S(2)}, u32[]{:S(2)}) %collective-permute-start.15) | collective-permute-done | bytes 1179680 | tf_op jit(solution)/shard_map/ppermute | solution.py:419
  77.1 3.2 %shard_map.240 = (bf16[256,256]{1,0:T(8,128)(2,1)S(1)}, bf16[256,256]{1,0:T(8,128)(2,1)S(1)}, bf16[256,256]{1,0:T(8,128)(2,1)S(1)}, bf16[256,256]{1,0:T(8,128)(2...) custom-call(s32[3]{0:T(128)S(1)} %pad_add_fusion.ids, ...), custom_call_target="tpu_custom_call" | custom-call | flops 2013265920 | bytes 9576460 | tf_op jit(solution)/shard_map/pallas_call | solution.py:63
  89.2 4.1 %collective-permute-done.18 = bf16[256,256]{1,0:T(8,128)(2,1)S(1)} collective-permute-done((bf16[256,256]{1,0:T(8,128)(2,1)S(1)}, bf16[256,256]{1,0:T(8,128)(2,1)S(1)}, u32[]{:S(2)}, u32[]{:S(2)}) %collective-permute-start.18) | collective-permute-done | bytes 131104 | tf_op jit(solution)/shard_map/ppermute | solution.py:423
  95.0 3.1 %collective-permute-start.22 = (bf16[256,256]{1,0:T(8,128)(2,1)S(1)}, bf16[256,256]{1,0:T(8,128)(2,1)S(1)}, u32[]{:S(2)}, u32[]{:S(2)}) collective-permute-start(bf16[256,256]{1,0:T(8,128)(2,1)S(1)} %add_convert_fusion.9.t0), channel_id=1, source_target_pairs={{0,2},{1,3},{2,0},{3,1},{4,6},{5,7},{6,4},{7,5},{8,10},{9,11},{10,... | collective-permute-start | bytes 393224 | tf_op jit(solution)/shard_map/ppermute | solution.py:423
  100.3 7.0 %collective-permute-done.22.t2 = bf16[256,256]{1,0:T(8,128)(2,1)S(1)} collective-permute-done((bf16[256,256]{1,0:T(8,128)(2,1)S(1)}, bf16[256,256]{1,0:T(8,128)(2,1)S(1)}, u32[]{:S(2)}, u32[]{:S(2)}) %collective-permute-start.22) | collective-permute-done | bytes 131104 | tf_op jit(solution)/shard_map/ppermute | solution.py:423
  107.2 2.7 %shard_map.243 = (bf16[4,256,256]{2,1,0:T(8,128)(2,1)S(1)}, f32[256,256]{1,0:T(8,128)S(1)}, bf16[256,512]{1,0:T(8,128)(2,1)S(1)}, f32[16,256]{1,0:T(8,128)S(1)}) custom-call(s32[3]{0:T(128)S(1)} %pad_add_fusion.ids, bf16[256,256]{1,0:T(8,128)(2,1)S(1)} %add_convert_fusion.9.t0, bf16[256,256]{1,0:T(8,128)(2,1)S(1)} %collective-permute-done.21.t1, ...), custom_call_target="tpu_custom_call" | custom-call | flops 2684354560 | bytes 6512652 | tf_op jit(solution)/shard_map/pallas_call | solution.py:63
  110.4 2.4 %collective-permute-start.26 = (bf16[1024,256]{1,0:T(8,128)(2,1)S(1)}, bf16[1024,256]{1,0:T(8,128)(2,1)S(1)}, u32[]{:S(2)}, u32[]{:S(2)}) collective-permute-start(bf16[1024,256]{1,0:T(8,128)(2,1)S(1)} %get-tuple-element.121), channel_id=1, source_target_pairs={{0,4},{4,0},{8,12},{12,8},{1,5},{5,1},{9,13},{13,9},{2,6},{6,2},{1... | collective-permute-start | bytes 1572872 | tf_op jit(solution)/shard_map/ppermute | solution.py:419
  112.8 6.6 %shard_map.245 = (bf16[4,272,256]{2,1,0:T(8,128)(2,1)S(1)}, f32[16,256]{1,0:T(8,128)S(1)}, bf16[256,1024]{1,0:T(8,128)(2,1)S(1)}) custom-call(s32[3]{0:T(128)S(1)} %pad_add_fusion.ids, bf16[256,512]{1,0:T(8,128)(2,1)S(1)} %get-tuple-element.122.d_o, f32[16,256]{1,0:T(8,128)S(1)} %get-tuple-element.123.sums_in, f32[8,256]{1,0:T(8,128)S(1)} %get-tuple-element.96.gains, ...), custom_call_target="tpu_custom_call" | custom-call | flops 8724152320 | bytes 8266764 | tf_op jit(solution)/shard_map/pallas_call | solution.py:63
  127.5 3.6 %all-to-all-start = ((bf16[4,272,256]{2,1,0:T(8,128)(2,1)}), bf16[4,272,256]{2,1,0:T(8,128)(2,1)S(1)}, u32[]{:S(2)}, u32[]{:S(2)}) async-start(bf16[4,272,256]{2,1,0:T(8,128)(2,1)} %copy-done), calls=%async_computation | async-start | bytes 1114112 | tf_op jit(solution)/shard_map/all_to_all | solution.py:505
  134.5 2.6 %collective-permute-start.35 = (f32[16,256]{1,0:T(8,128)S(1)}, f32[16,256]{1,0:T(8,128)S(1)}, u32[]{:S(2)}, u32[]{:S(2)}) collective-permute-start(f32[16,256]{1,0:T(8,128)S(1)} %add.107), channel_id=1, source_target_pairs={{0,2},{1,3},{2,0},{3,1},{4,6},{5,7},{6,4},{7,5},{8,10},{9,11},{10,... | collective-permute-start | bytes 49160 | tf_op jit(solution)/shard_map/ppermute | solution.py:423
  139.3 7.3 %collective-permute-done.35 = f32[16,256]{1,0:T(8,128)S(1)} collective-permute-done((f32[16,256]{1,0:T(8,128)S(1)}, f32[16,256]{1,0:T(8,128)S(1)}, u32[]{:S(2)}, u32[]{:S(2)}) %collective-permute-start.35) | collective-permute-done | bytes 16416 | tf_op jit(solution)/shard_map/ppermute | solution.py:423
  152.0 2.2 %collective-permute-done.32.y_got = bf16[256,256]{1,0:T(8,128)(2,1)S(1)} collective-permute-done((bf16[256,256]{1,0:T(8,128)(2,1)S(1)}, bf16[256,256]{1,0:T(8,128)(2,1)S(1)}, u32[]{:S(2)}, u32[]{:S(2)}) %collective-permute-start.32) | collective-permute-done | bytes 131104 | tf_op jit(solution)/shard_map/ppermute | solution.py:423
  161.8 12.3 %collective-permute-done.38 = bf16[512,256]{1,0:T(8,128)(2,1)S(1)} collective-permute-done((bf16[512,256]{1,0:T(8,128)(2,1)S(1)}, bf16[512,256]{1,0:T(8,128)(2,1)S(1)}, u32[]{:S(2)}, u32[]{:S(2)}) %collective-permute-start.38) | collective-permute-done | bytes 262176 | tf_op jit(solution)/shard_map/ppermute | solution.py:437
  (139 shorter events, 58.7 us)
Async XLA Ops:
  2.1 32.1 %collective-permute-start.4 = (bf16[272,1536]{1,0:T(8,128)(2,1)S(1)}, bf16[272,1536]{1,0:T(8,128)(2,1)}, u32[]{:S(2)}, u32[]{:S(2)}) collective-permute-start(bf16[272,1536]{1,0:T(8,128)(2,1)S(1)} %get-tuple-element.84.q0.w0), channel_id=1, source_target_pairs={{0,8},{4,12},{8,0},{12,4},{1,9},{5,13},{9,1},{13,5},{2,10},{6,14},... | collective-permute-start | bytes 2506760 | tf_op jit(solution)/shard_map/ppermute | solution.py:419
  4.2 11.3 %collective-permute-start.3 = (bf16[512,256]{1,0:T(8,128)(2,1)S(1)}, bf16[512,256]{1,0:T(8,128)(2,1)S(1)}, u32[]{:S(2)}, u32[]{:S(2)}) collective-permute-start(bf16[512,256]{1,0:T(8,128)(2,1)S(1)} %get-tuple-element.83), channel_id=1, source_target_pairs={{0,3},{1,7},{2,11},{3,15},{4,2},{5,6},{6,10},{7,14},{8,1},{9,5},{1... | collective-permute-start | bytes 786440 | tf_op jit(solution)/shard_map/ppermute | solution.py:428
  7.4 26.9 %collective-permute-start.2 = (bf16[512,256]{1,0:T(8,128)(2,1)S(1)}, bf16[512,256]{1,0:T(8,128)(2,1)S(1)}, u32[]{:S(2)}, u32[]{:S(2)}) collective-permute-start(bf16[512,256]{1,0:T(8,128)(2,1)S(1)} %get-tuple-element.83), channel_id=1, source_target_pairs={{0,2},{1,6},{2,10},{3,14},{4,3},{5,7},{6,11},{7,15},{8,0},{9,4},{1... | collective-permute-start | bytes 786440 | tf_op jit(solution)/shard_map/ppermute | solution.py:428
  8.4 25.8 %collective-permute-start.1 = (bf16[512,256]{1,0:T(8,128)(2,1)S(1)}, bf16[512,256]{1,0:T(8,128)(2,1)S(1)}, u32[]{:S(2)}, u32[]{:S(2)}) collective-permute-start(bf16[512,256]{1,0:T(8,128)(2,1)S(1)} %get-tuple-element.83), channel_id=1, source_target_pairs={{0,1},{1,5},{2,9},{3,13},{4,0},{5,4},{6,8},{7,12},{8,3},{9,7},{10,... | collective-permute-start | bytes 786440 | tf_op jit(solution)/shard_map/ppermute | solution.py:428
  9.3 26.4 %collective-permute-start = (bf16[512,256]{1,0:T(8,128)(2,1)S(1)}, bf16[512,256]{1,0:T(8,128)(2,1)}, u32[]{:S(2)}, u32[]{:S(2)}) collective-permute-start(bf16[512,256]{1,0:T(8,128)(2,1)S(1)} %get-tuple-element.83), channel_id=1, source_target_pairs={{0,0},{1,4},{2,8},{3,12},{4,1},{5,5},{6,9},{7,13},{8,2},{9,6},{10,... | collective-permute-start | bytes 786440 | tf_op jit(solution)/shard_map/ppermute | solution.py:428
  15.5 23.9 %collective-permute-start.5 = (bf16[272,1536]{1,0:T(8,128)(2,1)S(1)}, bf16[272,1536]{1,0:T(8,128)(2,1)}, u32[]{:S(2)}, u32[]{:S(2)}) collective-permute-start(bf16[272,1536]{1,0:T(8,128)(2,1)S(1)} %get-tuple-element.84.q0.w0), channel_id=1, source_target_pairs={{0,4},{4,0},{8,12},{12,8},{1,5},{5,1},{9,13},{13,9},{2,6},{6,2},{1... | collective-permute-start | bytes 2506760 | tf_op jit(solution)/shard_map/ppermute | solution.py:419
  36.9 35.3 %collective-permute-start.13 = (bf16[256,2304]{1,0:T(8,128)(2,1)S(1)}, bf16[256,2304]{1,0:T(8,128)(2,1)S(1)}, u32[]{:S(2)}, u32[]{:S(2)}) collective-permute-start(bf16[256,2304]{1,0:T(8,128)(2,1)S(1)} %shard_map.239.f0), channel_id=1, source_target_pairs={{0,8},{4,12},{8,0},{12,4},{1,9},{5,13},{9,1},{13,5},{2,10},{6,14},... | collective-permute-start | bytes 3538952 | tf_op jit(solution)/shard_map/ppermute | solution.py:419
  60.1 12.1 %collective-permute-start.11 = (bf16[256,256]{1,0:T(8,128)(2,1)S(1)}, bf16[256,256]{1,0:T(8,128)(2,1)S(1)}, u32[]{:S(2)}, u32[]{:S(2)}) collective-permute-start(bf16[256,256]{1,0:T(8,128)(2,1)S(1)} %add_convert_fusion.10.t0), channel_id=1, source_target_pairs={{0,2},{1,3},{2,0},{3,1},{4,6},{5,7},{6,4},{7,5},{8,10},{9,11},{10,... | collective-permute-start | bytes 393224 | tf_op jit(solution)/shard_map/ppermute | solution.py:423
  63.2 9.0 %collective-permute-start.10 = (bf16[256,256]{1,0:T(8,128)(2,1)S(1)}, bf16[256,256]{1,0:T(8,128)(2,1)S(1)}, u32[]{:S(2)}, u32[]{:S(2)}) collective-permute-start(bf16[256,256]{1,0:T(8,128)(2,1)S(1)} %add_convert_fusion.10.t0), channel_id=1, source_target_pairs={{0,1},{1,0},{2,3},{3,2},{4,5},{5,4},{6,7},{7,6},{8,9},{9,8},{10,11... | collective-permute-start | bytes 393224 | tf_op jit(solution)/shard_map/ppermute | solution.py:423
  63.2 11.5 %collective-permute-start.14 = (bf16[256,2304]{1,0:T(8,128)(2,1)S(1)}, bf16[256,2304]{1,0:T(8,128)(2,1)S(1)}, u32[]{:S(2)}, u32[]{:S(2)}) collective-permute-start(bf16[256,2304]{1,0:T(8,128)(2,1)S(1)} %shard_map.239.f0), channel_id=1, source_target_pairs={{0,4},{4,0},{8,12},{12,8},{1,5},{5,1},{9,13},{13,9},{2,6},{6,2},{1... | collective-permute-start | bytes 3538952 | tf_op jit(solution)/shard_map/ppermute | solution.py:419
  87.9 10.2 %collective-permute-start.24 = (bf16[768,256]{1,0:T(8,128)(2,1)S(1)}, bf16[768,256]{1,0:T(8,128)(2,1)S(1)}, u32[]{:S(2)}, u32[]{:S(2)}) collective-permute-start(bf16[768,256]{1,0:T(8,128)(2,1)S(1)} %add_convert_fusion.5), channel_id=1, source_target_pairs={{0,8},{4,12},{8,0},{12,4},{1,9},{5,13},{9,1},{13,5},{2,10},{6,14},... | collective-permute-start | bytes 1179656 | tf_op jit(solution)/shard_map/ppermute | solution.py:419
  95.0 12.2 %collective-permute-start.22 = (bf16[256,256]{1,0:T(8,128)(2,1)S(1)}, bf16[256,256]{1,0:T(8,128)(2,1)S(1)}, u32[]{:S(2)}, u32[]{:S(2)}) collective-permute-start(bf16[256,256]{1,0:T(8,128)(2,1)S(1)} %add_convert_fusion.9.t0), channel_id=1, source_target_pairs={{0,2},{1,3},{2,0},{3,1},{4,6},{5,7},{6,4},{7,5},{8,10},{9,11},{10,... | collective-permute-start | bytes 393224 | tf_op jit(solution)/shard_map/ppermute | solution.py:423
  98.1 9.1 %collective-permute-start.21 = (bf16[256,256]{1,0:T(8,128)(2,1)S(1)}, bf16[256,256]{1,0:T(8,128)(2,1)S(1)}, u32[]{:S(2)}, u32[]{:S(2)}) collective-permute-start(bf16[256,256]{1,0:T(8,128)(2,1)S(1)} %add_convert_fusion.9.t0), channel_id=1, source_target_pairs={{0,1},{1,0},{2,3},{3,2},{4,5},{5,4},{6,7},{7,6},{8,9},{9,8},{10,11... | collective-permute-start | bytes 393224 | tf_op jit(solution)/shard_map/ppermute | solution.py:423
  98.3 22.3 %collective-permute-start.25 = (bf16[768,256]{1,0:T(8,128)(2,1)S(1)}, bf16[768,256]{1,0:T(8,128)(2,1)S(1)}, u32[]{:S(2)}, u32[]{:S(2)}) collective-permute-start(bf16[768,256]{1,0:T(8,128)(2,1)S(1)} %add_convert_fusion.4), channel_id=1, source_target_pairs={{0,16},{16,0},{1,17},{17,1},{2,18},{18,2},{3,19},{19,3},{4,20},{20... | collective-permute-start | bytes 1179656 | tf_op jit(solution)/shard_map/ppermute | solution.py:484
  99.5 20.7 %collective-permute-start.27 = (bf16[256,1536]{1,0:T(8,128)(2,1)S(1)}, bf16[256,1536]{1,0:T(8,128)(2,1)S(1)}, u32[]{:S(2)}, u32[]{:S(2)}) collective-permute-start(bf16[256,1536]{1,0:T(8,128)(2,1)S(1)} %add_convert_fusion.1), channel_id=1, source_target_pairs={{0,8},{4,12},{8,0},{12,4},{1,9},{5,13},{9,1},{13,5},{2,10},{6,14},... | collective-permute-start | bytes 2359304 | tf_op jit(solution)/shard_map/ppermute | solution.py:419
  121.4 11.0 %collective-permute-start.40 = (bf16[512,256]{1,0:T(8,128)(2,1)S(1)}, bf16[512,256]{1,0:T(8,128)(2,1)}, u32[]{:S(2)}, u32[]{:S(2)}) collective-permute-start(bf16[512,256]{1,0:T(8,128)(2,1)S(1)} %add_convert_fusion.7), channel_id=1, source_target_pairs={{0,8},{4,12},{8,0},{12,4},{1,9},{5,13},{9,1},{13,5},{2,10},{6,14},... | collective-permute-start | bytes 786440 | tf_op jit(solution)/shard_map/ppermute | solution.py:419
  126.3 20.2 %collective-permute-start.31 = (bf16[512,256]{1,0:T(8,128)(2,1)}, bf16[512,256]{1,0:T(8,128)(2,1)}, u32[]{:S(2)}, u32[]{:S(2)}) collective-permute-start(bf16[512,256]{1,0:T(8,128)(2,1)} %get-tuple-element.140), channel_id=1, source_target_pairs={{0,1},{1,0},{2,3},{3,2},{4,5},{5,4},{6,7},{7,6},{8,9},{9,8},{10,11... | collective-permute-start | bytes 786440 | tf_op jit(solution)/shard_map/ppermute | solution.py:423
  126.3 28.5 %collective-permute-start.30 = (bf16[256,1536]{1,0:T(8,128)(2,1)S(1)}, bf16[256,1536]{1,0:T(8,128)(2,1)S(1)}, u32[]{:S(2)}, u32[]{:S(2)}) collective-permute-start(bf16[256,1536]{1,0:T(8,128)(2,1)S(1)} %add_convert_fusion.own), channel_id=1, source_target_pairs={{0,16},{16,0},{1,17},{17,1},{2,18},{18,2},{3,19},{19,3},{4,20},{20... | collective-permute-start | bytes 2359304 | tf_op jit(solution)/shard_map/ppermute | solution.py:484
  127.5 27.3 %all-to-all-start = ((bf16[4,272,256]{2,1,0:T(8,128)(2,1)}), bf16[4,272,256]{2,1,0:T(8,128)(2,1)S(1)}, u32[]{:S(2)}, u32[]{:S(2)}) async-start(bf16[4,272,256]{2,1,0:T(8,128)(2,1)} %copy-done), calls=%async_computation | async-start | bytes 1114112 | tf_op jit(solution)/shard_map/all_to_all | solution.py:505
  133.7 16.4 %collective-permute-start.41 = (bf16[512,256]{1,0:T(8,128)(2,1)S(1)}, bf16[512,256]{1,0:T(8,128)(2,1)S(1)}, u32[]{:S(2)}, u32[]{:S(2)}) collective-permute-start(bf16[512,256]{1,0:T(8,128)(2,1)S(1)} %add_convert_fusion.6), channel_id=1, source_target_pairs={{0,16},{16,0},{1,17},{17,1},{2,18},{18,2},{3,19},{19,3},{4,20},{20... | collective-permute-start | bytes 786440 | tf_op jit(solution)/shard_map/ppermute | solution.py:484
  134.0 20.9 %collective-permute-start.29 = (bf16[256,1024]{1,0:T(8,128)(2,1)}, bf16[256,1024]{1,0:T(8,128)(2,1)}, u32[]{:S(2)}, u32[]{:S(2)}) collective-permute-start(bf16[256,1024]{1,0:T(8,128)(2,1)} %add_convert_fusion.3), channel_id=1, source_target_pairs={{0,8},{4,12},{8,0},{12,4},{1,9},{5,13},{9,1},{13,5},{2,10},{6,14},... | collective-permute-start | bytes 1572872 | tf_op jit(solution)/shard_map/ppermute | solution.py:419
  134.5 12.0 %collective-permute-start.35 = (f32[16,256]{1,0:T(8,128)S(1)}, f32[16,256]{1,0:T(8,128)S(1)}, u32[]{:S(2)}, u32[]{:S(2)}) collective-permute-start(f32[16,256]{1,0:T(8,128)S(1)} %add.107), channel_id=1, source_target_pairs={{0,2},{1,3},{2,0},{3,1},{4,6},{5,7},{6,4},{7,5},{8,10},{9,11},{10,... | collective-permute-start | bytes 49160 | tf_op jit(solution)/shard_map/ppermute | solution.py:423
  156.4 18.5 %collective-permute-start.39 = (bf16[256,1024]{1,0:T(8,128)(2,1)S(1)}, bf16[256,1024]{1,0:T(8,128)(2,1)S(1)}, u32[]{:S(2)}, u32[]{:S(2)}) collective-permute-start(bf16[256,1024]{1,0:T(8,128)(2,1)S(1)} %add_convert_fusion.2.own), channel_id=1, source_target_pairs={{0,16},{16,0},{1,17},{17,1},{2,18},{18,2},{3,19},{19,3},{4,20},{20... | collective-permute-start | bytes 1572872 | tf_op jit(solution)/shard_map/ppermute | solution.py:484
  157.6 16.5 %collective-permute-start.38 = (bf16[512,256]{1,0:T(8,128)(2,1)S(1)}, bf16[512,256]{1,0:T(8,128)(2,1)S(1)}, u32[]{:S(2)}, u32[]{:S(2)}) collective-permute-start(bf16[512,256]{1,0:T(8,128)(2,1)S(1)} %shard_map.247), channel_id=1, source_target_pairs={{0,0},{1,8},{2,4},{3,12},{4,5},{5,13},{6,1},{7,9},{8,10},{9,2},{10... | collective-permute-start | bytes 786440 | tf_op jit(solution)/shard_map/ppermute | solution.py:437
  (40 other events, 338.0 us)
